TPU v7x, 32 devices: a whole 2x2x4 slice. The times are simulated.
32 devices in a mesh: rep: 16 (over z, y, core), shard: 2 (over x).
Axes of the slice: x: 2, y: 2, z: 4, core: 2. Of those that a mesh axis runs over, the one named last changes fastest.
Arguments:
- tokens: bfloat16 [4096, 1024], P(('rep', 'shard')), may hold values from -6 to 6
- lengths: int32 [32], P(('rep', 'shard')), may hold values from 16 to 128, as said below
- cotangent: bfloat16 [4096, 1024], P(('rep', 'shard')), may hold values from -6 to 6
- qkv_weight: bfloat16 [1024, 3072], P('shard'), may hold values from -0.1875 to 0.1875
- query_bias: bfloat16 [1024], P('shard'), may hold values from -3 to 3
- value_bias: bfloat16 [1024], P('shard'), may hold values from -3 to 3
- out_weight: bfloat16 [1024, 1024], P('shard'), may hold values from -0.75 to 0.75
- out_bias: bfloat16 [1024], P('shard'), may hold values from -3 to 3
- norm1_gain: bfloat16 [1024], P('shard'), may hold values from 0.5 to 1.5
- norm1_bias: bfloat16 [1024], P('shard'), may hold values from -3 to 3
- up_weight: bfloat16 [1024, 4096], P('shard'), may hold values from -0.1875 to 0.1875
- up_bias: bfloat16 [4096], P('shard'), may hold values from -3 to 3
- down_weight: bfloat16 [4096, 1024], P('shard'), may hold values from -0.09375 to 0.09375
- down_bias: bfloat16 [1024], P('shard'), may hold values from -3 to 3
- norm2_gain: bfloat16 [1024], P('shard'), may hold values from 0.5 to 1.5
- norm2_bias: bfloat16 [1024], P('shard'), may hold values from -3 to 3
Outputs:
- layer_out: bfloat16 [4096, 1024], P(('rep', 'shard'))
- input_grad: bfloat16 [4096, 1024], P(('rep', 'shard'))
- qkv_weight_grad: float32 [1024, 3072], P('shard')
- query_bias_grad: float32 [1024], P('shard')
- value_bias_grad: float32 [1024], P('shard')
- out_weight_grad: float32 [1024, 1024], P('shard')
- out_bias_grad: float32 [1024], P('shard')
- norm1_gain_grad: float32 [1024], P('shard')
- norm1_bias_grad: float32 [1024], P('shard')
- up_weight_grad: float32 [1024, 4096], P('shard')
- up_bias_grad: float32 [4096], P('shard')
- down_weight_grad: float32 [4096, 1024], P('shard')
- down_bias_grad: float32 [1024], P('shard')
- norm2_gain_grad: float32 [1024], P('shard')
- norm2_bias_grad: float32 [1024], P('shard')
Inputs may be any that keep to these rules, and one draw needn't show every extreme that they name: The alive slots of a sequence are its first lengths slots; some sequence has all 128 alive and some only 16.
All inputs are finite; a program needn't handle non-finite values.
Results may differ from a plain program's by a relative error of at most 0.018.
Values may be sent and summed in bfloat16 or wider, within the bound.
No kernel may reach another device: no remote copies, remote signals or barrier semaphores. Data moves between devices by JAX's collectives and lax.ppermute only.
A program may use at most 192 MiB of HBM per device.

v0:
```python
import jax
import jax.numpy as jnp
from jax import lax
from jax.experimental import pallas as pl
from jax.experimental.pallas import tpu as pltpu
from jax.sharding import PartitionSpec as P

HEADS = 16
CORES = 2

EPS = 1e-06
ROOT_HALF = 0.7071067811865476
INV_ROOT_TAU = 0.3989422804014327

F32 = jnp.float32
BF16 = jnp.bfloat16


def erf_gelu(inputs):
    return 0.5 * inputs * (1.0 + jax.scipy.special.erf(inputs * ROOT_HALF))


def gelu_slope(inputs):
    cumul = 0.5 * (1.0 + jax.scipy.special.erf(inputs * ROOT_HALF))
    return cumul + inputs * jnp.exp(-0.5 * inputs * inputs) * INV_ROOT_TAU


def norm_rows(rows_in, norm_gain, norm_shift):
    row_mean = jnp.mean(rows_in, axis=-1, keepdims=True)
    centred = rows_in - row_mean
    variance = jnp.mean(centred * centred, axis=-1, keepdims=True)
    inv_std = lax.rsqrt(variance + EPS)
    normed = centred * inv_std
    return (normed * norm_gain + norm_shift, normed, inv_std)


def norm_back(upstream, normed, inv_std, norm_gain):
    scaled = upstream * norm_gain
    mean_scaled = jnp.mean(scaled, axis=-1, keepdims=True)
    mean_proj = jnp.mean(scaled * normed, axis=-1, keepdims=True)
    return inv_std * (scaled - mean_scaled - normed * mean_proj)


def dot(left, right):
    return jnp.dot(left, right, preferred_element_type=F32)


def dot_rows(left, right):
    return lax.dot_general(left, right, (((0,), (0,)), ((), ())), preferred_element_type=F32)


def dot_cols(left, right):
    return lax.dot_general(left, right, (((1,), (1,)), ((), ())), preferred_element_type=F32)


def alive_rows(small_refs, i, s, span, along):
    length = small_refs[i][6:7, s : s + 1].astype(F32)
    return lax.broadcasted_iota(jnp.int32, (span, span), along).astype(F32) < length


def attend_kernel(plan, at_ref, *refs):
    blocks, pieces, seqs, heads, size = plan
    toks, refs = refs[:blocks], refs[blocks:]
    smalls, refs = refs[:blocks], refs[blocks:]
    weights, refs = refs[:pieces], refs[pieces:]
    bias_ref, out_ref, tok_ref, qkv_ref, context_ref = refs[:5]
    partials = refs[5:]
    rows = toks[0].shape[0]
    depth = weights[0].shape[0]
    span = rows // seqs
    block = heads * size
    for i in range(blocks):
        tok_ref[i * rows : (i + 1) * rows, :] = toks[i][...]
    acc = jnp.broadcast_to(bias_ref[...], (blocks * rows, 3 * block))
    for k in range(pieces):
        columns = pl.ds(pl.multiple_of(at_ref[k] * depth, depth), depth)
        acc = acc + dot(tok_ref[:, columns], weights[k][...])
    qkv_ref[...] = acc.astype(BF16)
    for i in range(blocks):
        for s in range(seqs):
            alive = alive_rows(smalls, i, s, span, 1)
            first = i * rows + s * span
            here = qkv_ref[first : first + span, :]
            outs = []
            for h in range(heads):
                queries = here[:, h * size : (h + 1) * size]
                keys = here[:, block + h * size : block + (h + 1) * size]
                values = here[:, 2 * block + h * size : 2 * block + (h + 1) * size]
                weight = jnp.where(alive, jnp.exp(dot_cols(queries, keys) * size ** (-0.5)), 0.0)
                probs = weight * (1.0 / jnp.sum(weight, axis=-1, keepdims=True))
                outs.append(dot(probs.astype(BF16), values))
            context_ref[first : first + span, :] = jnp.concatenate(outs, axis=1).astype(BF16)
    result = dot(context_ref[...], out_ref[...])
    for i in range(blocks):
        partials[i][...] = result[i * rows : (i + 1) * rows]


def attend_back_kernel(plan, *refs):
    blocks, _, seqs, heads, size = plan
    grads, refs = refs[:blocks], refs[blocks:]
    smalls, refs = refs[:blocks], refs[blocks:]
    qkv_ref, out_ref, all_ref, grad_ref, sums_ref, back_ref = refs
    rows = grads[0].shape[0]
    span = rows // seqs
    block = heads * size
    for i in range(blocks):
        all_ref[i * rows : (i + 1) * rows, :] = grads[i][...]
    back_ref[...] = dot_cols(all_ref[...], out_ref[...]).astype(BF16)
    query_sum = jnp.zeros((1, block), F32)
    value_sum = jnp.zeros((1, block), F32)
    for i in range(blocks):
        for s in range(seqs):
            alive = alive_rows(smalls, i, s, span, 0)
            first = i * rows + s * span
            here = qkv_ref[first : first + span, :]
            grad_here = back_ref[first : first + span, :]
            by_query, by_key, by_value = [], [], []
            for h in range(heads):
                queries = here[:, h * size : (h + 1) * size]
                keys = here[:, block + h * size : block + (h + 1) * size]
                values = here[:, 2 * block + h * size : 2 * block + (h + 1) * size]
                grad = grad_here[:, h * size : (h + 1) * size]
                weight = jnp.where(alive, jnp.exp(dot_cols(keys, queries) * size ** (-0.5)), 0.0)
                probs = weight * (1.0 / jnp.sum(weight, axis=0, keepdims=True))
                by_value.append(dot(probs.astype(BF16), grad))
                grad_probs = dot_cols(values, grad)
                mean = jnp.sum(probs * grad_probs, axis=0, keepdims=True)
                grad_half = (probs * (grad_probs - mean) * size ** (-0.5)).astype(BF16)
                by_query.append(dot_rows(grad_half, keys))
                by_key.append(dot(grad_half, queries))
            by_query = jnp.concatenate(by_query, axis=1)
            by_key = jnp.concatenate(by_key, axis=1)
            by_value = jnp.concatenate(by_value, axis=1)
            query_sum = query_sum + jnp.sum(by_query, axis=0, keepdims=True)
            value_sum = value_sum + jnp.sum(by_value, axis=0, keepdims=True)
            grad_ref[first : first + span, :] = jnp.concatenate(
                [by_query, by_key, by_value], axis=1
            ).astype(BF16)
    sums_ref[...] = jnp.concatenate([query_sum, value_sum], axis=0)


def whole(count):
    return [pl.BlockSpec(memory_space=pltpu.VMEM)] * count


SCALARS = pl.BlockSpec(memory_space=pltpu.SMEM)
ROOMY = pltpu.CompilerParams(vmem_limit_bytes=48 * 1024 * 1024)


def take_columns(weight, index, block, repeats):
    depth, width = weight.shape
    each = width // repeats
    if block % 128:
        return jnp.concatenate(
            [
                lax.dynamic_slice(weight, (0, t * each + index * block), (depth, block))
                for t in range(repeats)
            ],
            axis=1,
        )

    def kernel(at_ref, in_ref, out_ref, sems):
        copies = []
        for t in range(repeats):
            start = pl.multiple_of(t * each + at_ref[0] * block, 128)
            copies.append(
                pltpu.make_async_copy(
                    in_ref.at[:, pl.ds(start, block)],
                    out_ref.at[:, t * block : (t + 1) * block],
                    sems.at[t],
                )
            )
        for copy in copies:
            copy.start()
        for copy in copies:
            copy.wait()

    return pl.pallas_call(
        kernel,
        in_specs=[SCALARS, pl.BlockSpec(memory_space=pl.ANY)],
        out_specs=whole(1)[0],
        out_shape=jax.ShapeDtypeStruct((depth, repeats * block), weight.dtype),
        scratch_shapes=[pltpu.SemaphoreType.DMA((repeats,))],
        name="take_columns",
    )(index.reshape(1).astype(jnp.int32), weight)


def merge_rows(mine, other, core_at):
    block, width = mine.shape
    tall = min(block, 256)
    steps = block // tall

    def kernel(at_ref, mine_ref, other_ref, out_ref):
        @pl.when(pl.program_id(0) == at_ref[0])
        def _():
            out_ref[...] = mine_ref[...].astype(F32)

        @pl.when(pl.program_id(0) != at_ref[0])
        def _():
            out_ref[...] = other_ref[...].astype(F32)

    return pl.pallas_call(
        kernel,
        grid_spec=pltpu.PrefetchScalarGridSpec(
            num_scalar_prefetch=1,
            grid=(CORES, steps),
            in_specs=[
                pl.BlockSpec((tall, width), lambda h, i, at: (jnp.where(h == at[0], i, 0), 0)),
                pl.BlockSpec((tall, width), lambda h, i, at: (jnp.where(h == at[0], 0, i), 0)),
            ],
            out_specs=pl.BlockSpec((tall, width), lambda h, i, at: (h * steps + i, 0)),
        ),
        out_shape=jax.ShapeDtypeStruct((CORES * block, width), F32),
        name="merge_rows",
    )(core_at.reshape(1).astype(jnp.int32), mine, other)


def merge_columns(mine, other, core_at, num_shard, repeats):
    rows, width = mine.shape
    each = width // (num_shard * repeats)
    if each % 128:
        pair = [jnp.where(core_at == 0, mine, other), jnp.where(core_at == 0, other, mine)]
        pair = jnp.stack([p.reshape(rows, num_shard, repeats, each) for p in pair], axis=3)
        return pair.transpose(0, 2, 1, 3, 4).reshape(rows, CORES * width).astype(F32)
    tall = min(rows, 64)

    def kernel(at_ref, mine_ref, other_ref, out_ref):
        def write(pair):
            for t in range(repeats):
                for p in range(num_shard):
                    for c in range(CORES):
                        to = ((t * num_shard + p) * CORES + c) * each
                        frm = (p * repeats + t) * each
                        out_ref[:, to : to + each] = pair[c][:, frm : frm + each].astype(F32)

        @pl.when(at_ref[0] == 0)
        def _():
            write((mine_ref, other_ref))

        @pl.when(at_ref[0] != 0)
        def _():
            write((other_ref, mine_ref))

    return pl.pallas_call(
        kernel,
        grid_spec=pltpu.PrefetchScalarGridSpec(
            num_scalar_prefetch=1,
            grid=(rows // tall,),
            in_specs=[pl.BlockSpec((tall, width), lambda i, at: (i, 0))] * 2,
            out_specs=pl.BlockSpec((tall, CORES * width), lambda i, at: (i, 0)),
        ),
        out_shape=jax.ShapeDtypeStruct((rows, CORES * width), F32),
        name="merge_columns",
    )(core_at.reshape(1).astype(jnp.int32), mine, other)


def build(num_rep, num_shard):
    parts = num_shard * CORES
    bits = []
    step = CORES
    while step < num_rep:
        bits.append(step)
        step *= 2

    orders = (bits, bits[1::-1] + bits[2:])

    def flip(value, bit):
        return lax.ppermute(value, "rep", [(i, i ^ bit) for i in range(num_rep)])

    def step_flip(value, stage):
        return lax.ppermute(
            value, "rep", [(i, i ^ orders[i % CORES][stage]) for i in range(num_rep)]
        )

    def sibling(value):
        return flip(value, 1)

    def turn(value, by):
        pairs = [(i, (i + by) % num_shard) for i in range(num_shard)]
        return lax.ppermute(value, "shard", pairs)

    def in_order(relative, shard_at):
        placed = []
        for place in range(num_shard):
            behind = (shard_at - place) % num_shard
            item = relative[0]
            for k in range(1, num_shard):
                item = jnp.where(behind == k, relative[k], item)
            placed.append(item)
        return placed

    def on_device(
        tokens, lengths, cotangent, qkv_weight, query_bias, value_bias, out_weight, out_bias,
        norm1_gain, norm1_bias, up_weight, up_bias, down_weight, down_bias, norm2_gain, norm2_bias,
    ):
        rows, width = tokens.shape
        num_seqs = lengths.shape[0]
        depth = qkv_weight.shape[0]
        hidden_size = up_weight.shape[1]
        heads_here = HEADS // parts
        head_size = width // HEADS
        att_block = heads_here * head_size
        ff_block = hidden_size // parts
        rep_at = lax.axis_index("rep")
        shard_at = lax.axis_index("shard")
        core_at = rep_at % CORES
        offsets = range(1, num_shard)

        def gather_rows(own):
            far = []
            for k in offsets:
                far.append(turn(own, k))
            near = [own, sibling(own)]
            far = [[came, sibling(came)] for came in far]
            return near, far

        def stack(near, far):
            return jnp.concatenate(near + [item for pair in far for item in pair], axis=0)

        def split(partial):
            return [partial[i * rows : (i + 1) * rows] for i in range(parts)]

        def scatter_rows(blocks):
            total = None
            for k in offsets:
                other = sibling(blocks[2 * k + 1])
                came = turn((blocks[2 * k] + other).astype(BF16), -k).astype(F32)
                total = came if total is None else total + came
            near = blocks[0] + sibling(blocks[1])
            return near if total is None else near + total

        def qkv_for(shard):
            return take_columns(qkv_weight, shard * CORES + core_at, att_block, 3)

        def up_for(shard):
            return take_columns(up_weight, shard * CORES + core_at, ff_block, 1)

        qkv_send = [qkv_for((shard_at + k) % num_shard) for k in offsets]
        qkv_rel = [turn(item, k) for item, k in zip(qkv_send, offsets)]
        tok_near, tok_far = gather_rows(tokens)
        small = jnp.concatenate(
            [out_bias, norm1_gain, norm1_bias, down_bias, norm2_gain, norm2_bias]
            + [jnp.pad(lengths.astype(BF16), (0, depth - num_seqs))]
        ).reshape(7, depth)
        small_near, small_far = gather_rows(small)
        small_rel = [small] + [pair[0] for pair in small_far]
        qkv_rel = [qkv_for(shard_at)] + qkv_rel
        up_send = [up_for((shard_at + k) % num_shard) for k in offsets]
        up_own = up_for(shard_at)
        up_send, qkv_rel = lax.optimization_barrier((up_send, qkv_rel))
        up_side = (rep_at // bits[0]) % 2
        up_rel = [up_own]
        for item, k in zip(up_send, offsets):
            half = lax.dynamic_slice_in_dim(item, up_side * (depth // 2), depth // 2, 0)
            half = turn(half, k)
            other = flip(half, bits[0])
            low = up_side == 0
            up_rel.append(
                jnp.concatenate([jnp.where(low, half, other), jnp.where(low, other, half)], axis=0)
            )

        small_full = jnp.concatenate(in_order(small_rel, shard_at), axis=1).astype(F32)
        out_bias_full, gain1, shift1, down_bias_full, gain2, shift2 = (
            small_full[i] for i in range(6)
        )
        came_from = (shard_at - jnp.arange(num_shard, dtype=jnp.int32)) % num_shard
        small_all = small_near + [item for pair in small_far for item in pair]

        qkv_mine = jnp.concatenate(in_order(qkv_rel, shard_at), axis=0)
        query_mine = lax.dynamic_slice(query_bias, (core_at * att_block,), (att_block,))
        value_mine = lax.dynamic_slice(value_bias, (core_at * att_block,), (att_block,))
        qkv_bias = jnp.concatenate([query_mine, jnp.zeros_like(query_mine), value_mine]).astype(F32)
        out_mine = lax.dynamic_slice(out_weight, (core_at * att_block, 0), (att_block, width))
        down_mine = lax.dynamic_slice(down_weight, (core_at * ff_block, 0), (ff_block, width))
        up_bias_mine = lax.dynamic_slice(up_bias, (core_at * ff_block,), (ff_block,)).astype(F32)

        all_rows = parts * rows
        plan = (parts, num_shard, num_seqs, heads_here, head_size)
        tok_all, qkv_rows, context, *partials = pl.pallas_call(
            lambda *refs: attend_kernel(plan, *refs),
            in_specs=[SCALARS] + whole(2 * parts + num_shard + 2),
            out_specs=whole(3 + parts),
            out_shape=[
                jax.ShapeDtypeStruct((all_rows, width), BF16),
                jax.ShapeDtypeStruct((all_rows, 3 * att_block), BF16),
                jax.ShapeDtypeStruct((all_rows, att_block), BF16),
            ]
            + [jax.ShapeDtypeStruct((rows, width), F32)] * parts,
            compiler_params=ROOMY,
            name="attend",
        )(
            came_from, *tok_near, *[item for pair in tok_far for item in pair], *small_all,
            *qkv_rel, qkv_bias.reshape(1, -1), out_mine,
        )
        resid1 = tokens.astype(F32) + scatter_rows(partials) + out_bias_full
        hidden1, normed1, inv_std1 = norm_rows(resid1, gain1, shift1)
        hidden1_half, up_rel = lax.optimization_barrier((hidden1.astype(BF16), up_rel))
        hid_all = stack(*gather_rows(hidden1_half))

        up_mine = jnp.concatenate(in_order(up_rel, shard_at), axis=0)
        pre_act = dot(hid_all, up_mine) + up_bias_mine
        activ = erf_gelu(pre_act).astype(BF16)
        resid2 = hidden1 + scatter_rows(split(dot(activ, down_mine))) + down_bias_full
        layer_f32, normed2, inv_std2 = norm_rows(resid2, gain2, shift2)
        layer_out = layer_f32.astype(BF16)

        upstream = cotangent.astype(F32)
        grad_gain2 = jnp.sum(upstream * normed2, axis=0)
        grad_shift2 = jnp.sum(upstream, axis=0)
        grad_resid2 = norm_back(upstream, normed2, inv_std2, gain2)
        grad_down_bias = jnp.sum(grad_resid2, axis=0)
        mlp_all = stack(*gather_rows(grad_resid2.astype(BF16)))
        sum_down = dot_rows(activ, mlp_all).astype(BF16)
        grad_pre = dot_cols(mlp_all, down_mine) * gelu_slope(pre_act)
        grad_pre_half = grad_pre.astype(BF16)
        grad_up_bias = jnp.sum(grad_pre, axis=0)
        sum_up = dot_rows(hid_all, grad_pre_half).astype(BF16)
        grad_hidden1 = grad_resid2 + scatter_rows(split(dot_cols(grad_pre_half, up_mine)))
        grad_gain1 = jnp.sum(grad_hidden1 * normed1, axis=0)
        grad_shift1 = jnp.sum(grad_hidden1, axis=0)
        grad_resid1 = norm_back(grad_hidden1, normed1, inv_std1, gain1)
        grad_out_bias = jnp.sum(grad_resid1, axis=0)
        attn_near, attn_far = gather_rows(grad_resid1.astype(BF16))
        attn_all, grad_qkv, bias_sums = pl.pallas_call(
            lambda *refs: attend_back_kernel(plan, *refs),
            in_specs=whole(2 * parts + 2),
            out_specs=whole(3),
            out_shape=[
                jax.ShapeDtypeStruct((all_rows, width), BF16),
                jax.ShapeDtypeStruct((all_rows, 3 * att_block), BF16),
                jax.ShapeDtypeStruct((2, att_block), F32),
            ],
            scratch_shapes=[pltpu.VMEM((all_rows, att_block), BF16)],
            compiler_params=ROOMY,
            name="attend_back",
        )(
            *attn_near, *[item for pair in attn_far for item in pair], *small_all,
            qkv_rows, out_mine,
        )
        sum_out = dot_rows(context, attn_all).astype(BF16)
        grad_query_bias, grad_value_bias = bias_sums[0], bias_sums[1]
        sum_qkv = dot_rows(tok_all, grad_qkv).astype(BF16)
        input_grad = (grad_resid1 + scatter_rows(split(dot_cols(grad_qkv, qkv_mine)))).astype(BF16)

        def side_at(stage):
            bit = jnp.where(core_at == 0, orders[0][stage], orders[1][stage])
            return (rep_at // bit) % 2

        def halve(value, axis):
            for stage in range(len(bits)):
                side = side_at(stage)
                half = value.shape[axis] // 2
                keep = lax.dynamic_slice_in_dim(value, side * half, half, axis)
                send = lax.dynamic_slice_in_dim(value, (1 - side) * half, half, axis)
                came = step_flip(send, stage)
                value = (keep.astype(F32) + came.astype(F32)).astype(BF16)
            return value

        def double(value):
            for stage in reversed(range(len(bits))):
                came = step_flip(value, stage)
                low = side_at(stage) == 0
                value = jnp.concatenate(
                    [jnp.where(low, value, came), jnp.where(low, came, value)], axis=0
                )
            return value

        def both_cores(value):
            other = sibling(value)
            first = core_at == 0
            return jnp.where(first, value, other), jnp.where(first, other, value)

        def reduce_by_rows(value):
            value = double(halve(value, 0))
            other = sibling(value)
            return merge_rows(value, other, core_at)

        def reduce_by_columns(value, repeats):
            piece = halve(value.reshape(num_shard, depth, -1), 1)
            relative = [lax.dynamic_index_in_dim(piece, shard_at, 0, keepdims=False)]
            for k in offsets:
                out_to = lax.dynamic_index_in_dim(piece, (shard_at + k) % num_shard, 0, keepdims=False)
                relative.append(turn(out_to, k))
            full = double(jnp.concatenate(in_order(relative, shard_at), axis=1))
            other = sibling(full)
            return merge_columns(full, other, core_at, num_shard, repeats)

        total_down = reduce_by_rows(sum_down)
        total_up = reduce_by_columns(sum_up, 1)
        total_out = reduce_by_rows(sum_out)
        total_qkv = reduce_by_columns(sum_qkv, 3)

        row_sums = jnp.stack(
            [grad_out_bias, grad_gain1, grad_shift1, grad_down_bias, grad_gain2, grad_shift2]
        )
        row_sums = row_sums.reshape(6, num_shard, depth)
        mine = lax.dynamic_index_in_dim(row_sums, shard_at, 1, keepdims=False)
        for k in offsets:
            there = lax.dynamic_index_in_dim(row_sums, (shard_at + k) % num_shard, 1, keepdims=False)
            mine = mine + turn(there, k)
        mine = mine + sibling(mine)
        block_sums = jnp.concatenate([grad_query_bias, grad_value_bias, grad_up_bias])
        packed = jnp.concatenate([mine.reshape(-1), block_sums])
        for bit in bits:
            packed = packed + flip(packed, bit)
        mine = packed[: 6 * depth].reshape(6, depth)
        block_sums = packed[6 * depth :]
        first, second = both_cores(block_sums)
        total_query = jnp.concatenate([first[:att_block], second[:att_block]])
        total_value = jnp.concatenate(
            [first[att_block : 2 * att_block], second[att_block : 2 * att_block]]
        )
        total_up_bias = jnp.concatenate([first[2 * att_block :], second[2 * att_block :]])
        return (
            layer_out, input_grad, total_qkv, total_query, total_value, total_out,
            mine[0], mine[1], mine[2], total_up, total_up_bias, total_down, mine[3], mine[4], mine[5],
        )

    return on_device


def solution(mesh):
    rows, group, flat = P(("rep", "shard"), None), P("shard", None), P("shard")
    in_specs = (
        rows, P(("rep", "shard")), rows, group, flat, flat, group, flat, flat, flat,
        group, flat, group, flat, flat, flat,
    )
    out_specs = (
        rows, rows, group, flat, flat, group, flat, flat, flat, group, flat, group, flat, flat, flat,
    )
    return jax.shard_map(
        build(mesh.shape["rep"], mesh.shape["shard"]),
        mesh=mesh, in_specs=in_specs, out_specs=out_specs, check_vma=False,
    )
```

profile of v0, /device:TPU:0, one launch (start us, length us, event | category | flops | bytes accessed | tf_op | source)
XLA Modules:
  0.0 335.8 jit_solution(119693007895022182)
XLA Ops:
  3.0 3.0 collective-permute-start.6
  10.7 18.8 %collective-permute-done.1.refs_3_ = bf16[128,1024]{1,0:T(8,128)(2,1)S(1)} collective-permute-done((bf16[128,1024]{1,0:T(8,128)(2,1)S(1)}, bf16[128,1024]{1,0:T(8,128)(2,1)S(1)}, u32[]{:S(2)}, u32[]{:S(2)}) %collective-permute-start.1) | collective-permute-done | bytes 262176 | tf_op jit(solution)/shard_map/ppermute | solution.py:280
  39.0 7.1 %attend.1 = (bf16[512,1024]{1,0:T(8,128)(2,1)}, bf16[512,768]{1,0:T(8,128)(2,1)S(1)}, bf16[512,256]{1,0:T(8,128)(2,1)S(1)}, f32[128,1024]{1,0:T(8,128)S(1)}, f32...) custom-call(s32[2]{0:T(128)S(1)} %and_select_fusion.refs_0_, bf16[128,1024]{1,0:T(8,128)(2,1)S(1)} %copy-done.3, ...), custom_call_target="tpu_custom_call" | custom-call | tf_op jit(solution)/shard_map/attend/pallas_call | solution.py:379
  54.9 11.1 %collective-permute-done.10 = bf16[256,1024]{1,0:T(8,128)(2,1)S(1)} collective-permute-done((bf16[256,1024]{1,0:T(8,128)(2,1)S(1)}, bf16[256,1024]{1,0:T(8,128)(2,1)S(1)}, u32[]{:S(2)}, u32[]{:S(2)}) %collective-permute-start.10) | collective-permute-done | bytes 524320 | tf_op jit(solution)/shard_map/ppermute | solution.py:280
  67.8 3.4 %collective-permute-done.9 = bf16[128,1024]{1,0:T(8,128)(2,1)S(1)} collective-permute-done((bf16[128,1024]{1,0:T(8,128)(2,1)S(1)}, bf16[128,1024]{1,0:T(8,128)(2,1)S(1)}, u32[]{:S(2)}, u32[]{:S(2)}) %collective-permute-start.9) | collective-permute-done | bytes 262176 | tf_op jit(solution)/shard_map/ppermute | solution.py:280
  71.8 7.2 %collective-permute-done.11 = bf16[256,1024]{1,0:T(8,128)(2,1)S(1)} collective-permute-done((bf16[256,1024]{1,0:T(8,128)(2,1)S(1)}, bf16[256,1024]{1,0:T(8,128)(2,1)S(1)}, u32[]{:S(2)}, u32[]{:S(2)}) %collective-permute-start.11) | collective-permute-done | bytes 524320 | tf_op jit(solution)/shard_map/ppermute | solution.py:268
  81.1 4.6 %collective-permute-done.13 = bf16[128,1024]{1,0:T(8,128)(2,1)S(1)} collective-permute-done((bf16[128,1024]{1,0:T(8,128)(2,1)S(1)}, bf16[128,1024]{1,0:T(8,128)(2,1)S(1)}, u32[]{:S(2)}, u32[]{:S(2)}) %collective-permute-start.13) | collective-permute-done | bytes 262176 | tf_op jit(solution)/shard_map/ppermute | solution.py:280
  95.1 6.6 %collective-permute-done.17 = bf16[128,1024]{1,0:T(8,128)(2,1)S(1)} collective-permute-done((bf16[128,1024]{1,0:T(8,128)(2,1)S(1)}, bf16[128,1024]{1,0:T(8,128)(2,1)S(1)}, u32[]{:S(2)}, u32[]{:S(2)}) %collective-permute-start.17) | collective-permute-done | bytes 262176 | tf_op jit(solution)/shard_map/ppermute | solution.py:280
  106.1 5.8 %collective-permute-done.19 = bf16[128,1024]{1,0:T(8,128)(2,1)S(1)} collective-permute-done((bf16[128,1024]{1,0:T(8,128)(2,1)S(1)}, bf16[128,1024]{1,0:T(8,128)(2,1)S(1)}, u32[]{:S(2)}, u32[]{:S(2)}) %collective-permute-start.19) | collective-permute-done | bytes 262176 | tf_op jit(solution)/shard_map/ppermute | solution.py:280
  113.5 3.4 %fusion.63 = (f32[1024]{0:T(1024)S(1)}, bf16[512,1024]{1,0:T(8,128)(2,1)S(1)}) fusion(f32[512,1024]{1,0:T(8,128)S(1)} %get-tuple-element.130, f32[1024]{0:T(1024)S(1)} %dynamic-slice_convert_fusion, bf16[2048,1024]{1,0:T(8,128)(2,1)S(1)} %copy-done.38, s32[]{:T(128)S(6)} %select_n.506, bf16[128,1024]{1,0:T(8,128)(2,1)S(1)} %collective-permute-done.20, ...), kind=kOutput, calls=%fused_computation.207 | convolution fusion | flops 1084226560 | bytes 6299652 | tf_op jit(solution)/shard_map/dot_general | solution.py:53
  121.2 2.9 convolution_convert_fusion.1
  132.6 2.7 collective-permute-done.23
  150.8 2.9 collective-permute-done.25.refs_2_
  157.3 5.7 %attend_back.1 = (bf16[512,1024]{1,0:T(8,128)(2,1)S(1)}, bf16[512,768]{1,0:T(8,128)(2,1)S(1)}, f32[2,256]{1,0:T(2,128)S(1)}) custom-call(bf16[128,1024]{1,0:T(8,128)(2,1)S(1)} %convert_element_type.209.refs_0_, bf16[128,1024]{1,0:T(8,128)(2,1)S(1)} %collective-permute-done.24.refs_1_, bf16[128,1024]{1,0:T(8,128)(2,1)S(1)} %collective-permute-done.25.refs_2_, ...), custom_call_target="tpu_custom_call" | custom-call | tf_op jit(solution)/shard_map/attend_back/pallas_call | solution.py:424
  182.1 11.6 %collective-permute-done.45 = bf16[64,1024]{1,0:T(8,128)(2,1)S(1)} collective-permute-done((bf16[64,1024]{1,0:T(8,128)(2,1)S(1)}, bf16[64,1024]{1,0:T(8,128)(2,1)S(1)}, u32[]{:S(2)}, u32[]{:S(2)}) %collective-permute-start.45) | collective-permute-done | bytes 131104 | tf_op jit(solution)/shard_map/ppermute | solution.py:271
  193.9 3.0 collective-permute-start.61
  196.9 9.1 %collective-permute-done.46 = bf16[32,1024]{1,0:T(8,128)(2,1)S(1)} collective-permute-done((bf16[32,1024]{1,0:T(8,128)(2,1)S(1)}, bf16[32,1024]{1,0:T(8,128)(2,1)S(1)}, u32[]{:S(2)}, u32[]{:S(2)}) %collective-permute-start.46) | collective-permute-done | bytes 65568 | tf_op jit(solution)/shard_map/ppermute | solution.py:271
  207.7 4.6 %collective-permute-done.61 = bf16[128,1024]{1,0:T(8,128)(2,1)S(1)} collective-permute-done((bf16[128,1024]{1,0:T(8,128)(2,1)S(1)}, bf16[128,1024]{1,0:T(8,128)(2,1)S(1)}, u32[]{:S(2)}, u32[]{:S(2)}) %collective-permute-start.61) | collective-permute-done | bytes 262176 | tf_op jit(solution)/shard_map/ppermute | solution.py:271
  212.5 4.1 %collective-permute-done.47 = bf16[32,1024]{1,0:T(8,128)(2,1)S(1)} collective-permute-done((bf16[32,1024]{1,0:T(8,128)(2,1)S(1)}, bf16[32,1024]{1,0:T(8,128)(2,1)S(1)}, u32[]{:S(2)}, u32[]{:S(2)}) %collective-permute-start.47) | collective-permute-done | bytes 65568 | tf_op jit(solution)/shard_map/ppermute | solution.py:271
  216.6 7.4 %collective-permute-start.48 = (bf16[64,1024]{1,0:T(8,128)(2,1)S(1)}, bf16[64,1024]{1,0:T(8,128)(2,1)S(1)}, u32[]{:S(2)}, u32[]{:S(2)}) collective-permute-start(bf16[64,1024]{1,0:T(8,128)(2,1)S(1)} %pad_maximum_fusion.20), channel_id=1, source_target_pairs={{0,8},{2,6},{4,12},{6,2},{8,0},{10,14},{12,4},{14,10},{16,24},{18,... | collective-permute-start | bytes 393224 | tf_op jit(solution)/shard_map/ppermute | solution.py:271
  229.6 6.6 %collective-permute-done.31 = bf16[2,128,768]{2,1,0:T(8,128)(2,1)S(1)} collective-permute-done((bf16[2,128,768]{2,1,0:T(8,128)(2,1)S(1)}, bf16[2,128,768]{2,1,0:T(8,128)(2,1)S(1)}, u32[]{:S(2)}, u32[]{:S(2)}) %collective-permute-start.31) | collective-permute-done | bytes 393248 | tf_op jit(solution)/shard_map/ppermute | solution.py:271
  236.3 4.0 %collective-permute-start.32 = (bf16[2,64,768]{2,1,0:T(8,128)(2,1)S(1)}, bf16[2,64,768]{2,1,0:T(8,128)(2,1)S(1)}, u32[]{:S(2)}, u32[]{:S(2)}) collective-permute-start(bf16[2,64,768]{2,1,0:T(8,128)(2,1)S(1)} %constant_dynamic-slice_fusion.11), channel_id=1, source_target_pairs={{0,16},{2,18},{4,20},{6,22},{8,24},{10,26},{12,28},{14,30},{16,0},... | collective-permute-start | bytes 589832 | tf_op jit(solution)/shard_map/ppermute | solution.py:271
  240.4 6.1 %collective-permute-done.32 = bf16[2,64,768]{2,1,0:T(8,128)(2,1)S(1)} collective-permute-done((bf16[2,64,768]{2,1,0:T(8,128)(2,1)S(1)}, bf16[2,64,768]{2,1,0:T(8,128)(2,1)S(1)}, u32[]{:S(2)}, u32[]{:S(2)}) %collective-permute-start.32) | collective-permute-done | bytes 196640 | tf_op jit(solution)/shard_map/ppermute | solution.py:271
  249.1 5.8 %collective-permute-start.56 = (bf16[128,2048]{1,0:T(8,128)(2,1)S(1)}, bf16[128,2048]{1,0:T(8,128)(2,1)S(1)}, u32[]{:S(2)}, u32[]{:S(2)}) collective-permute-start(bf16[128,2048]{1,0:T(8,128)(2,1)S(1)} %pad_maximum_fusion.12), channel_id=1, source_target_pairs={{0,8},{2,6},{4,12},{6,2},{8,0},{10,14},{12,4},{14,10},{16,24},{18,... | collective-permute-start | bytes 1572872 | tf_op jit(solution)/shard_map/ppermute | solution.py:271
  257.9 13.5 %collective-permute-done.34 = bf16[64,1536]{1,0:T(8,128)(2,1)S(1)} collective-permute-done((bf16[64,1536]{1,0:T(8,128)(2,1)S(1)}, bf16[64,1536]{1,0:T(8,128)(2,1)S(1)}, u32[]{:S(2)}, u32[]{:S(2)}) %collective-permute-start.34) | collective-permute-done | bytes 196640 | tf_op jit(solution)/shard_map/ppermute | solution.py:271
  274.5 9.0 %collective-permute-done.35 = bf16[128,1536]{1,0:T(8,128)(2,1)S(1)} collective-permute-done((bf16[128,1536]{1,0:T(8,128)(2,1)S(1)}, bf16[128,1536]{1,0:T(8,128)(2,1)S(1)}, u32[]{:S(2)}, u32[]{:S(2)}) %collective-permute-start.35) | collective-permute-done | bytes 393248 | tf_op jit(solution)/shard_map/ppermute | solution.py:271
  289.9 6.3 %collective-permute-done.36 = bf16[256,1536]{1,0:T(8,128)(2,1)S(1)} collective-permute-done((bf16[256,1536]{1,0:T(8,128)(2,1)S(1)}, bf16[256,1536]{1,0:T(8,128)(2,1)S(1)}, u32[]{:S(2)}, u32[]{:S(2)}) %collective-permute-start.36) | collective-permute-done | bytes 786464 | tf_op jit(solution)/shard_map/ppermute | solution.py:271
  300.7 3.7 %collective-permute-done.49 = bf16[128,1024]{1,0:T(8,128)(2,1)S(1)} collective-permute-done((bf16[128,1024]{1,0:T(8,128)(2,1)S(1)}, bf16[128,1024]{1,0:T(8,128)(2,1)S(1)}, u32[]{:S(2)}, u32[]{:S(2)}) %collective-permute-start.49) | collective-permute-done | bytes 262176 | tf_op jit(solution)/shard_map/ppermute | solution.py:271
  304.5 3.5 %collective-permute-done.29 = bf16[128,1024]{1,0:T(8,128)(2,1)S(1)} collective-permute-done((bf16[128,1024]{1,0:T(8,128)(2,1)S(1)}, bf16[128,1024]{1,0:T(8,128)(2,1)S(1)}, u32[]{:S(2)}, u32[]{:S(2)}) %collective-permute-start.29) | collective-permute-done | bytes 262176 | tf_op jit(solution)/shard_map/ppermute | solution.py:280
  314.1 6.9 %merge_columns.2 = f32[512,3072]{1,0:T(8,128)} custom-call(s32[1]{0:T(128)} %bitcast.8.at_ref, bf16[512,1536]{1,0:T(8,128)(2,1)} %pad_maximum_fusion.3.mine_ref, bf16[512,1536]{1,0:T(8,128)(2,1)} %collective-permute-done.37.other_ref), custom_call_target="tpu_custom_call" | custom-call | tf_op jit(solution)/shard_map/merge_columns/pallas_call | solution.py:244
  320.9 7.5 %merge_rows.3 = f32[2048,1024]{1,0:T(8,128)} custom-call(s32[1]{0:T(128)} %bitcast.8.at_ref, bf16[1024,1024]{1,0:T(8,128)(2,1)} %copy-done.14, bf16[1024,1024]{1,0:T(8,128)(2,1)} %collective-permute-done.65.other_ref), custom_call_target="tpu_custom_call" | custom-call | tf_op jit(solution)/shard_map/merge_rows/pallas_call | solution.py:202
  328.4 7.3 %merge_columns.3 = f32[512,4096]{1,0:T(8,128)} custom-call(s32[1]{0:T(128)} %bitcast.8.at_ref, bf16[512,2048]{1,0:T(8,128)(2,1)} %pad_maximum_fusion.1.mine_ref, bf16[512,2048]{1,0:T(8,128)(2,1)} %collective-permute-done.58.other_ref), custom_call_target="tpu_custom_call" | custom-call | tf_op jit(solution)/shard_map/merge_columns/pallas_call | solution.py:244
  (363 shorter events, 127.8 us)
Async XLA Ops:
  3.0 31.7 %collective-permute-start.6 = (bf16[512,768]{1,0:T(8,128)(2,1)}, bf16[512,768]{1,0:T(8,128)(2,1)}, u32[]{:S(2)}, u32[]{:S(2)}) collective-permute-start(bf16[512,768]{1,0:T(8,128)(2,1)} %take_columns.6), channel_id=1, source_target_pairs={{0,1},{1,0},{2,3},{3,2},{4,5},{5,4},{6,7},{7,6},{8,9},{9,8},{10,11... | collective-permute-start | bytes 2359304 | tf_op jit(solution)/shard_map/ppermute | solution.py:280
  6.0 23.5 %collective-permute-start.1 = (bf16[128,1024]{1,0:T(8,128)(2,1)S(1)}, bf16[128,1024]{1,0:T(8,128)(2,1)S(1)}, u32[]{:S(2)}, u32[]{:S(2)}) collective-permute-start(bf16[128,1024]{1,0:T(8,128)(2,1)S(1)} %copy-done.3), channel_id=1, source_target_pairs={{0,1},{1,0},{2,3},{3,2},{4,5},{5,4},{6,7},{7,6},{8,9},{9,8},{10,11... | collective-permute-start | bytes 786440 | tf_op jit(solution)/shard_map/ppermute | solution.py:280
  8.2 21.6 %collective-permute-start.4 = (bf16[7,512]{1,0:T(8,128)(2,1)S(1)}, bf16[7,512]{1,0:T(8,128)(2,1)S(1)}, u32[]{:S(2)}, u32[]{:S(2)}) collective-permute-start(bf16[7,512]{1,0:T(8,128)(2,1)S(1)} %reshape.160.refs_5_.refs_4_), channel_id=1, source_target_pairs={{0,1},{1,0},{2,3},{3,2},{4,5},{5,4},{6,7},{7,6},{8,9},{9,8},{10,11... | collective-permute-start | bytes 21512 | tf_op jit(solution)/shard_map/ppermute | solution.py:280
  10.2 24.5 %collective-permute-start.3 = (bf16[7,512]{1,0:T(8,128)(2,1)S(1)}, bf16[7,512]{1,0:T(8,128)(2,1)S(1)}, u32[]{:S(2)}, u32[]{:S(2)}) collective-permute-start(bf16[7,512]{1,0:T(8,128)(2,1)S(1)} %reshape.160.refs_5_.refs_4_), channel_id=1, source_target_pairs={{0,2},{2,0},{4,6},{6,4},{8,10},{10,8},{12,14},{14,12},{16,18},{18,... | collective-permute-start | bytes 21512 | tf_op jit(solution)/shard_map/ppermute | solution.py:268
  10.2 24.5 %collective-permute-start = (bf16[128,1024]{1,0:T(8,128)(2,1)S(1)}, bf16[128,1024]{1,0:T(8,128)(2,1)S(1)}, u32[]{:S(2)}, u32[]{:S(2)}) collective-permute-start(bf16[128,1024]{1,0:T(8,128)(2,1)S(1)} %copy-done.3), channel_id=1, source_target_pairs={{0,2},{2,0},{4,6},{6,4},{8,10},{10,8},{12,14},{14,12},{16,18},{18,... | collective-permute-start | bytes 786440 | tf_op jit(solution)/shard_map/ppermute | solution.py:268
  51.1 14.9 %collective-permute-start.10 = (bf16[256,1024]{1,0:T(8,128)(2,1)S(1)}, bf16[256,1024]{1,0:T(8,128)(2,1)S(1)}, u32[]{:S(2)}, u32[]{:S(2)}) collective-permute-start(bf16[256,1024]{1,0:T(8,128)(2,1)S(1)} %constant_dynamic-slice_fusion.14), channel_id=1, source_target_pairs={{0,1},{1,0},{2,3},{3,2},{4,5},{5,4},{6,7},{7,6},{8,9},{9,8},{10,11... | collective-permute-start | bytes 1572872 | tf_op jit(solution)/shard_map/ppermute | solution.py:280
  52.9 14.8 %collective-permute-start.7 = (f32[128,1024]{1,0:T(8,128)}, f32[128,1024]{1,0:T(8,128)S(1)}, u32[]{:S(2)}, u32[]{:S(2)}) collective-permute-start(f32[128,1024]{1,0:T(8,128)} %copy-done.11), channel_id=1, source_target_pairs={{0,2},{2,0},{4,6},{6,4},{8,10},{10,8},{12,14},{14,12},{16,18},{18,... | collective-permute-start | bytes 1572872 | tf_op jit(solution)/shard_map/ppermute | solution.py:268
  54.4 16.7 %collective-permute-start.9 = (bf16[128,1024]{1,0:T(8,128)(2,1)S(1)}, bf16[128,1024]{1,0:T(8,128)(2,1)S(1)}, u32[]{:S(2)}, u32[]{:S(2)}) collective-permute-start(bf16[128,1024]{1,0:T(8,128)(2,1)S(1)} %add_convert_fusion.10), channel_id=1, source_target_pairs={{0,1},{1,0},{2,3},{3,2},{4,5},{5,4},{6,7},{7,6},{8,9},{9,8},{10,11... | collective-permute-start | bytes 786440 | tf_op jit(solution)/shard_map/ppermute | solution.py:280
  66.0 13.0 %collective-permute-start.11 = (bf16[256,1024]{1,0:T(8,128)(2,1)S(1)}, bf16[256,1024]{1,0:T(8,128)(2,1)S(1)}, u32[]{:S(2)}, u32[]{:S(2)}) collective-permute-start(bf16[256,1024]{1,0:T(8,128)(2,1)S(1)} %collective-permute-done.10), channel_id=1, source_target_pairs={{0,4},{2,6},{4,0},{6,2},{8,12},{10,14},{12,8},{14,10},{16,20},{18,... | collective-permute-start | bytes 1572872 | tf_op jit(solution)/shard_map/ppermute | solution.py:268
  125.2 21.8 %collective-permute-start.51 = (bf16[2,256,1024]{2,1,0:T(8,128)(2,1)}, bf16[2,256,1024]{2,1,0:T(8,128)(2,1)}, u32[]{:S(2)}, u32[]{:S(2)}) collective-permute-start(bf16[2,256,1024]{2,1,0:T(8,128)(2,1)} %constant_dynamic-slice_fusion.5), channel_id=1, source_target_pairs={{0,4},{2,10},{4,0},{6,14},{8,12},{10,2},{12,8},{14,6},{16,20},{18,... | collective-permute-start | bytes 3145736 | tf_op jit(solution)/shard_map/ppermute | solution.py:271
  131.1 22.6 %collective-permute-start.59 = (bf16[512,1024]{1,0:T(8,128)(2,1)}, bf16[512,1024]{1,0:T(8,128)(2,1)}, u32[]{:S(2)}, u32[]{:S(2)}) collective-permute-start(bf16[512,1024]{1,0:T(8,128)(2,1)} %constant_dynamic-slice_fusion.2), channel_id=1, source_target_pairs={{0,4},{2,10},{4,0},{6,14},{8,12},{10,2},{12,8},{14,6},{16,20},{18,... | collective-permute-start | bytes 3145736 | tf_op jit(solution)/shard_map/ppermute | solution.py:271
  149.1 29.2 %collective-permute-start.52 = (bf16[2,128,1024]{2,1,0:T(8,128)(2,1)S(1)}, bf16[2,128,1024]{2,1,0:T(8,128)(2,1)S(1)}, u32[]{:S(2)}, u32[]{:S(2)}) collective-permute-start(bf16[2,128,1024]{2,1,0:T(8,128)(2,1)S(1)} %constant_dynamic-slice_fusion.4), channel_id=1, source_target_pairs={{0,8},{2,6},{4,12},{6,2},{8,0},{10,14},{12,4},{14,10},{16,24},{18,... | collective-permute-start | bytes 1572872 | tf_op jit(solution)/shard_map/ppermute | solution.py:271
  155.4 26.4 %collective-permute-start.60 = (bf16[256,1024]{1,0:T(8,128)(2,1)S(1)}, bf16[256,1024]{1,0:T(8,128)(2,1)S(1)}, u32[]{:S(2)}, u32[]{:S(2)}) collective-permute-start(bf16[256,1024]{1,0:T(8,128)(2,1)S(1)} %constant_dynamic-slice_fusion.1), channel_id=1, source_target_pairs={{0,8},{2,6},{4,12},{6,2},{8,0},{10,14},{12,4},{14,10},{16,24},{18,... | collective-permute-start | bytes 1572872 | tf_op jit(solution)/shard_map/ppermute | solution.py:271
  165.1 16.0 %collective-permute-start.44 = (bf16[128,1024]{1,0:T(8,128)(2,1)S(1)}, bf16[128,1024]{1,0:T(8,128)(2,1)S(1)}, u32[]{:S(2)}, u32[]{:S(2)}) collective-permute-start(bf16[128,1024]{1,0:T(8,128)(2,1)S(1)} %constant_dynamic-slice_fusion.8), channel_id=1, source_target_pairs={{0,4},{2,10},{4,0},{6,14},{8,12},{10,2},{12,8},{14,6},{16,20},{18,... | collective-permute-start | bytes 786440 | tf_op jit(solution)/shard_map/ppermute | solution.py:271
  168.5 131.5 %collective-permute-start.28 = (f32[128,1024]{1,0:T(8,128)S(1)}, f32[128,1024]{1,0:T(8,128)S(1)}, u32[]{:S(2)}, u32[]{:S(2)}) collective-permute-start(f32[128,1024]{1,0:T(8,128)S(1)} %slice.156), channel_id=1, source_target_pairs={{0,2},{2,0},{4,6},{6,4},{8,10},{10,8},{12,14},{14,12},{16,18},{18,... | collective-permute-start | bytes 1572872 | tf_op jit(solution)/shard_map/ppermute | solution.py:268
  176.7 47.3 %collective-permute-start.30 = (bf16[2,256,768]{2,1,0:T(8,128)(2,1)S(1)}, bf16[2,256,768]{2,1,0:T(8,128)(2,1)S(1)}, u32[]{:S(2)}, u32[]{:S(2)}) collective-permute-start(bf16[2,256,768]{2,1,0:T(8,128)(2,1)S(1)} %constant_dynamic-slice_fusion.13), channel_id=1, source_target_pairs={{0,4},{2,10},{4,0},{6,14},{8,12},{10,2},{12,8},{14,6},{16,20},{18,... | collective-permute-start | bytes 2359304 | tf_op jit(solution)/shard_map/ppermute | solution.py:271
  178.6 27.5 %collective-permute-start.53 = (bf16[2,64,1024]{2,1,0:T(8,128)(2,1)S(1)}, bf16[2,64,1024]{2,1,0:T(8,128)(2,1)S(1)}, u32[]{:S(2)}, u32[]{:S(2)}) collective-permute-start(bf16[2,64,1024]{2,1,0:T(8,128)(2,1)S(1)} %constant_dynamic-slice_fusion.3), channel_id=1, source_target_pairs={{0,16},{2,18},{4,20},{6,22},{8,24},{10,26},{12,28},{14,30},{16,0},... | collective-permute-start | bytes 786440 | tf_op jit(solution)/shard_map/ppermute | solution.py:271
  181.1 12.6 %collective-permute-start.45 = (bf16[64,1024]{1,0:T(8,128)(2,1)S(1)}, bf16[64,1024]{1,0:T(8,128)(2,1)S(1)}, u32[]{:S(2)}, u32[]{:S(2)}) collective-permute-start(bf16[64,1024]{1,0:T(8,128)(2,1)S(1)} %constant_dynamic-slice_fusion.7), channel_id=1, source_target_pairs={{0,8},{2,6},{4,12},{6,2},{8,0},{10,14},{12,4},{14,10},{16,24},{18,... | collective-permute-start | bytes 393224 | tf_op jit(solution)/shard_map/ppermute | solution.py:271
  193.9 18.4 %collective-permute-start.61 = (bf16[128,1024]{1,0:T(8,128)(2,1)S(1)}, bf16[128,1024]{1,0:T(8,128)(2,1)S(1)}, u32[]{:S(2)}, u32[]{:S(2)}) collective-permute-start(bf16[128,1024]{1,0:T(8,128)(2,1)S(1)} %constant_dynamic-slice_fusion), channel_id=1, source_target_pairs={{0,16},{2,18},{4,20},{6,22},{8,24},{10,26},{12,28},{14,30},{16,0},... | collective-permute-start | bytes 786440 | tf_op jit(solution)/shard_map/ppermute | solution.py:271
  206.2 17.7 %collective-permute-start.54 = (bf16[64,1024]{1,0:T(8,128)(2,1)S(1)}, bf16[64,1024]{1,0:T(8,128)(2,1)S(1)}, u32[]{:S(2)}, u32[]{:S(2)}) collective-permute-start(bf16[64,1024]{1,0:T(8,128)(2,1)S(1)} %dynamic-slice_bitcast_fusion), channel_id=1, source_target_pairs={{0,1},{1,0},{2,3},{3,2},{4,5},{5,4},{6,7},{7,6},{8,9},{9,8},{10,11... | collective-permute-start | bytes 393224 | tf_op jit(solution)/shard_map/ppermute | solution.py:280
  212.4 15.8 %collective-permute-start.62 = (bf16[128,1024]{1,0:T(8,128)(2,1)S(1)}, bf16[128,1024]{1,0:T(8,128)(2,1)S(1)}, u32[]{:S(2)}, u32[]{:S(2)}) collective-permute-start(bf16[128,1024]{1,0:T(8,128)(2,1)S(1)} %add_convert_fusion.6), channel_id=1, source_target_pairs={{0,16},{2,18},{4,20},{6,22},{8,24},{10,26},{12,28},{14,30},{16,0},... | collective-permute-start | bytes 786440 | tf_op jit(solution)/shard_map/ppermute | solution.py:271
  216.6 81.2 %collective-permute-start.48 = (bf16[64,1024]{1,0:T(8,128)(2,1)S(1)}, bf16[64,1024]{1,0:T(8,128)(2,1)S(1)}, u32[]{:S(2)}, u32[]{:S(2)}) collective-permute-start(bf16[64,1024]{1,0:T(8,128)(2,1)S(1)} %pad_maximum_fusion.20), channel_id=1, source_target_pairs={{0,8},{2,6},{4,12},{6,2},{8,0},{10,14},{12,4},{14,10},{16,24},{18,... | collective-permute-start | bytes 393224 | tf_op jit(solution)/shard_map/ppermute | solution.py:271
  224.4 15.9 %collective-permute-start.55 = (bf16[64,2048]{1,0:T(8,128)(2,1)S(1)}, bf16[64,2048]{1,0:T(8,128)(2,1)S(1)}, u32[]{:S(2)}, u32[]{:S(2)}) collective-permute-start(bf16[64,2048]{1,0:T(8,128)(2,1)S(1)} %pad_maximum_fusion.16), channel_id=1, source_target_pairs={{0,16},{2,18},{4,20},{6,22},{8,24},{10,26},{12,28},{14,30},{16,0},... | collective-permute-start | bytes 786440 | tf_op jit(solution)/shard_map/ppermute | solution.py:271
  228.3 26.8 %collective-permute-start.63 = (bf16[256,1024]{1,0:T(8,128)(2,1)S(1)}, bf16[256,1024]{1,0:T(8,128)(2,1)S(1)}, u32[]{:S(2)}, u32[]{:S(2)}) collective-permute-start(bf16[256,1024]{1,0:T(8,128)(2,1)S(1)} %pad_maximum_fusion.13), channel_id=1, source_target_pairs={{0,8},{2,6},{4,12},{6,2},{8,0},{10,14},{12,4},{14,10},{16,24},{18,... | collective-permute-start | bytes 1572872 | tf_op jit(solution)/shard_map/ppermute | solution.py:271
  249.1 22.6 %collective-permute-start.56 = (bf16[128,2048]{1,0:T(8,128)(2,1)S(1)}, bf16[128,2048]{1,0:T(8,128)(2,1)S(1)}, u32[]{:S(2)}, u32[]{:S(2)}) collective-permute-start(bf16[128,2048]{1,0:T(8,128)(2,1)S(1)} %pad_maximum_fusion.12), channel_id=1, source_target_pairs={{0,8},{2,6},{4,12},{6,2},{8,0},{10,14},{12,4},{14,10},{16,24},{18,... | collective-permute-start | bytes 1572872 | tf_op jit(solution)/shard_map/ppermute | solution.py:271
  254.9 16.5 %collective-permute-start.34 = (bf16[64,1536]{1,0:T(8,128)(2,1)S(1)}, bf16[64,1536]{1,0:T(8,128)(2,1)S(1)}, u32[]{:S(2)}, u32[]{:S(2)}) collective-permute-start(bf16[64,1536]{1,0:T(8,128)(2,1)S(1)} %pad_maximum_fusion.17), channel_id=1, source_target_pairs={{0,16},{2,18},{4,20},{6,22},{8,24},{10,26},{12,28},{14,30},{16,0},... | collective-permute-start | bytes 589832 | tf_op jit(solution)/shard_map/ppermute | solution.py:271
  255.4 30.8 %collective-permute-start.64 = (bf16[512,1024]{1,0:T(8,128)(2,1)S(1)}, bf16[512,1024]{1,0:T(8,128)(2,1)S(1)}, u32[]{:S(2)}, u32[]{:S(2)}) collective-permute-start(bf16[512,1024]{1,0:T(8,128)(2,1)S(1)} %pad_maximum_fusion.9), channel_id=1, source_target_pairs={{0,4},{2,10},{4,0},{6,14},{8,12},{10,2},{12,8},{14,6},{16,20},{18,... | collective-permute-start | bytes 3145736 | tf_op jit(solution)/shard_map/ppermute | solution.py:271
  272.1 15.2 %collective-permute-start.57 = (bf16[256,2048]{1,0:T(8,128)(2,1)S(1)}, bf16[256,2048]{1,0:T(8,128)(2,1)S(1)}, u32[]{:S(2)}, u32[]{:S(2)}) collective-permute-start(bf16[256,2048]{1,0:T(8,128)(2,1)S(1)} %pad_maximum_fusion.8), channel_id=1, source_target_pairs={{0,4},{2,10},{4,0},{6,14},{8,12},{10,2},{12,8},{14,6},{16,20},{18,... | collective-permute-start | bytes 3145736 | tf_op jit(solution)/shard_map/ppermute | solution.py:271
  283.7 12.5 %collective-permute-start.36 = (bf16[256,1536]{1,0:T(8,128)(2,1)S(1)}, bf16[256,1536]{1,0:T(8,128)(2,1)S(1)}, u32[]{:S(2)}, u32[]{:S(2)}) collective-permute-start(bf16[256,1536]{1,0:T(8,128)(2,1)S(1)} %pad_maximum_fusion.10), channel_id=1, source_target_pairs={{0,4},{2,10},{4,0},{6,14},{8,12},{10,2},{12,8},{14,6},{16,20},{18,... | collective-permute-start | bytes 2359304 | tf_op jit(solution)/shard_map/ppermute | solution.py:271
  287.0 33.9 %collective-permute-start.65 = (bf16[1024,1024]{1,0:T(8,128)(2,1)S(1)}, bf16[1024,1024]{1,0:T(8,128)(2,1)}, u32[]{:S(2)}, u32[]{:S(2)}) collective-permute-start(bf16[1024,1024]{1,0:T(8,128)(2,1)S(1)} %pad_maximum_fusion.2.mine_ref), channel_id=1, source_target_pairs={{0,2},{2,0},{4,6},{6,4},{8,10},{10,8},{12,14},{14,12},{16,18},{18,... | collective-permute-start | bytes 6291464 | tf_op jit(solution)/shard_map/ppermute | solution.py:268
  289.9 38.5 %collective-permute-start.58 = (bf16[512,2048]{1,0:T(8,128)(2,1)}, bf16[512,2048]{1,0:T(8,128)(2,1)}, u32[]{:S(2)}, u32[]{:S(2)}) collective-permute-start(bf16[512,2048]{1,0:T(8,128)(2,1)} %pad_maximum_fusion.1.mine_ref), channel_id=1, source_target_pairs={{0,2},{2,0},{4,6},{6,4},{8,10},{10,8},{12,14},{14,12},{16,18},{18,... | collective-permute-start | bytes 6291464 | tf_op jit(solution)/shard_map/ppermute | solution.py:268
  297.8 16.3 %collective-permute-start.37 = (bf16[512,1536]{1,0:T(8,128)(2,1)}, bf16[512,1536]{1,0:T(8,128)(2,1)}, u32[]{:S(2)}, u32[]{:S(2)}) collective-permute-start(bf16[512,1536]{1,0:T(8,128)(2,1)} %pad_maximum_fusion.3.mine_ref), channel_id=1, source_target_pairs={{0,2},{2,0},{4,6},{6,4},{8,10},{10,8},{12,14},{14,12},{16,18},{18,... | collective-permute-start | bytes 4718600 | tf_op jit(solution)/shard_map/ppermute | solution.py:268
  (85 other events, 532.1 us)
where the time goes:
time: 337 us; the launch traced here: 336 us
  waiting for transfers between devices  156 us (46%)
  starting transfers between devices  76.6 us (23%)
  Pallas kernels  45.8 us (14%)
  other arithmetic  23.2 us (7%)
  local copies, waits for them, and re-layouts  17.6 us (5%)
  matrix products  14.5 us (4%)
    ppermute x24, waiting for transfers between devices, step_flip(): lax.ppermute(value, 'rep', [(i, i ^ orders[i % CORES][stage]) for i in ra...  77.4 us
    ppermute x14, waiting for transfers between devices, turn(): return lax.ppermute(value, 'shard', pairs)  61.6 us
    ppermute x24, starting transfers between devices, step_flip(): lax.ppermute(value, 'rep', [(i, i ^ orders[i % CORES][stage]) for i in ra...  45 us
    ppermute x14, starting transfers between devices, turn(): return lax.ppermute(value, 'shard', pairs)  22.4 us
    ppermute x28, waiting for transfers between devices, flip(): return lax.ppermute(value, 'rep', [(i, i ^ bit) for i in range(num_rep)])  16.6 us
    pallas_call x2, Pallas kernels, merge_columns(): pl.pallas_call(kernel, grid_spec=pltpu.PrefetchScalarGridSpec(num_scalar_...  14.2 us
    unnamed x117, local copies, waits for them, and re-layouts  11.8 us
    pallas_call x2, Pallas kernels, merge_rows(): pl.pallas_call(kernel, grid_spec=pltpu.PrefetchScalarGridSpec(num_scalar_...  10.1 us
  transfers between devices with their start and end apart: 66, of which 30 were waited for; matrix products, arithmetic and copies ran while one was open for 10% of the time, Pallas kernels for 9%

commit v1 on v0

--- a/solution.py
+++ b/solution.py
@@ -1,3 +1,5 @@
+import math
+
 import jax
 import jax.numpy as jnp
 from jax import lax
@@ -63,19 +65,25 @@
     toks, refs = refs[:blocks], refs[blocks:]
     smalls, refs = refs[:blocks], refs[blocks:]
     weights, refs = refs[:pieces], refs[pieces:]
-    bias_ref, out_ref, tok_ref, qkv_ref, context_ref = refs[:5]
-    partials = refs[5:]
+    bias_ref, out_ref, refs = refs[0], refs[1], refs[2:]
+    late, partials, refs = refs[:4], refs[4 : 4 + blocks], refs[4 + blocks :]
+    tok_ref, weight_ref, qkv_ref, context_ref, sems = refs
+    copies = [
+        pltpu.make_async_copy(frm, to, sems.at[n])
+        for n, (frm, to) in enumerate(zip((tok_ref, weight_ref, qkv_ref, context_ref), late))
+    ]
     rows = toks[0].shape[0]
     depth = weights[0].shape[0]
     span = rows // seqs
     block = heads * size
     for i in range(blocks):
         tok_ref[i * rows : (i + 1) * rows, :] = toks[i][...]
-    acc = jnp.broadcast_to(bias_ref[...], (blocks * rows, 3 * block))
+    copies[0].start()
     for k in range(pieces):
-        columns = pl.ds(pl.multiple_of(at_ref[k] * depth, depth), depth)
-        acc = acc + dot(tok_ref[:, columns], weights[k][...])
-    qkv_ref[...] = acc.astype(BF16)
+        weight_ref[pl.ds(pl.multiple_of(at_ref[k] * depth, depth), depth), :] = weights[k][...]
+    copies[1].start()
+    qkv_ref[...] = (dot(tok_ref[...], weight_ref[...]) + bias_ref[...]).astype(BF16)
+    copies[2].start()
     for i in range(blocks):
         for s in range(seqs):
             alive = alive_rows(smalls, i, s, span, 1)
@@ -90,9 +98,12 @@
                 probs = weight * (1.0 / jnp.sum(weight, axis=-1, keepdims=True))
                 outs.append(dot(probs.astype(BF16), values))
             context_ref[first : first + span, :] = jnp.concatenate(outs, axis=1).astype(BF16)
+    copies[3].start()
     result = dot(context_ref[...], out_ref[...])
     for i in range(blocks):
         partials[i][...] = result[i * rows : (i + 1) * rows]
+    for copy in copies:
+        copy.wait()
 
 
 def attend_back_kernel(plan, *refs):
@@ -144,10 +155,15 @@
 
 
 SCALARS = pl.BlockSpec(memory_space=pltpu.SMEM)
-ROOMY = pltpu.CompilerParams(vmem_limit_bytes=48 * 1024 * 1024)
-
-
-def take_columns(weight, index, block, repeats):
+MEBI = 1024 * 1024
+
+
+def vmem(*shapes, spare=2):
+    used = sum(math.prod(item.shape) * item.dtype.itemsize for item in shapes)
+    return pltpu.CompilerParams(vmem_limit_bytes=min(used + spare * MEBI, 60 * MEBI))
+
+
+def take_columns(weight, index, block, repeats, grant=4):
     depth, width = weight.shape
     each = width // repeats
     if block % 128:
@@ -177,12 +193,13 @@
 
     return pl.pallas_call(
         kernel,
-        in_specs=[SCALARS, pl.BlockSpec(memory_space=pl.ANY)],
+        in_specs=[SCALARS, pl.BlockSpec(memory_space=pltpu.HBM)],
         out_specs=whole(1)[0],
         out_shape=jax.ShapeDtypeStruct((depth, repeats * block), weight.dtype),
         scratch_shapes=[pltpu.SemaphoreType.DMA((repeats,))],
+        compiler_params=pltpu.CompilerParams(vmem_limit_bytes=grant * MEBI),
         name="take_columns",
-    )(index.reshape(1).astype(jnp.int32), weight)
+    )(index.reshape(1).astype(jnp.int32), pltpu.with_memory_space_constraint(weight, pltpu.HBM))
 
 
 def merge_rows(mine, other, core_at):
@@ -211,18 +228,38 @@
             out_specs=pl.BlockSpec((tall, width), lambda h, i, at: (h * steps + i, 0)),
         ),
         out_shape=jax.ShapeDtypeStruct((CORES * block, width), F32),
+        compiler_params=pltpu.CompilerParams(vmem_limit_bytes=6 * MEBI),
         name="merge_rows",
     )(core_at.reshape(1).astype(jnp.int32), mine, other)
 
 
-def merge_columns(mine, other, core_at, num_shard, repeats):
+def swapped(step, steps, swap):
+    per = steps // 4
+    quarter = step // per
+    inner = jnp.logical_and(swap, jnp.logical_and(quarter > 0, quarter < 3))
+    return jnp.where(inner, 3 * per - quarter * per + step % per, step)
+
+
+def merge_columns(mine, other, core_at, num_shard, repeats, swap):
     rows, width = mine.shape
     each = width // (num_shard * repeats)
     if each % 128:
+        if swap:
+            tall = rows // 4
+
+            def straight(item):
+                return jnp.concatenate([item[q * tall : (q + 1) * tall] for q in (0, 2, 1, 3)])
+
+            mine = jnp.where(core_at == 1, straight(mine), mine)
+            other = jnp.where(core_at == 0, straight(other), other)
         pair = [jnp.where(core_at == 0, mine, other), jnp.where(core_at == 0, other, mine)]
         pair = jnp.stack([p.reshape(rows, num_shard, repeats, each) for p in pair], axis=3)
         return pair.transpose(0, 2, 1, 3, 4).reshape(rows, CORES * width).astype(F32)
-    tall = min(rows, 64)
+    tall = min(rows // 4, 64)
+    steps = rows // tall
+
+    def place(i, core):
+        return swapped(i, steps, core == 1) if swap else i
 
     def kernel(at_ref, mine_ref, other_ref, out_ref):
         def write(pair):
@@ -246,10 +283,14 @@
         grid_spec=pltpu.PrefetchScalarGridSpec(
             num_scalar_prefetch=1,
             grid=(rows // tall,),
-            in_specs=[pl.BlockSpec((tall, width), lambda i, at: (i, 0))] * 2,
+            in_specs=[
+                pl.BlockSpec((tall, width), lambda i, at: (place(i, at[0]), 0)),
+                pl.BlockSpec((tall, width), lambda i, at: (place(i, 1 - at[0]), 0)),
+            ],
             out_specs=pl.BlockSpec((tall, CORES * width), lambda i, at: (i, 0)),
         ),
         out_shape=jax.ShapeDtypeStruct((rows, CORES * width), F32),
+        compiler_params=pltpu.CompilerParams(vmem_limit_bytes=6 * MEBI),
         name="merge_columns",
     )(core_at.reshape(1).astype(jnp.int32), mine, other)
 
@@ -262,14 +303,17 @@
         bits.append(step)
         step *= 2
 
-    orders = (bits, bits[1::-1] + bits[2:])
+    mixed = (bits, bits[1::-1] + bits[2:])
+    plain = (bits, bits)
+    routes = {"down": mixed, "up": mixed, "qkv": plain, "out": mixed}
+    backs = {"down": mixed, "up": mixed, "qkv": mixed, "out": mixed}
 
     def flip(value, bit):
         return lax.ppermute(value, "rep", [(i, i ^ bit) for i in range(num_rep)])
 
-    def step_flip(value, stage):
+    def step_flip(value, route, stage):
         return lax.ppermute(
-            value, "rep", [(i, i ^ orders[i % CORES][stage]) for i in range(num_rep)]
+            value, "rep", [(i, i ^ route[i % CORES][stage]) for i in range(num_rep)]
         )
 
     def sibling(value):
@@ -329,13 +373,13 @@
             near = blocks[0] + sibling(blocks[1])
             return near if total is None else near + total
 
-        def qkv_for(shard):
-            return take_columns(qkv_weight, shard * CORES + core_at, att_block, 3)
+        def qkv_for(shard, grant=4):
+            return take_columns(qkv_weight, shard * CORES + core_at, att_block, 3, grant)
 
         def up_for(shard):
             return take_columns(up_weight, shard * CORES + core_at, ff_block, 1)
 
-        qkv_send = [qkv_for((shard_at + k) % num_shard) for k in offsets]
+        qkv_send = [qkv_for((shard_at + k) % num_shard, 60) for k in offsets]
         qkv_rel = [turn(item, k) for item, k in zip(qkv_send, offsets)]
         tok_near, tok_far = gather_rows(tokens)
         small = jnp.concatenate(
@@ -366,7 +410,6 @@
         came_from = (shard_at - jnp.arange(num_shard, dtype=jnp.int32)) % num_shard
         small_all = small_near + [item for pair in small_far for item in pair]
 
-        qkv_mine = jnp.concatenate(in_order(qkv_rel, shard_at), axis=0)
         query_mine = lax.dynamic_slice(query_bias, (core_at * att_block,), (att_block,))
         value_mine = lax.dynamic_slice(value_bias, (core_at * att_block,), (att_block,))
         qkv_bias = jnp.concatenate([query_mine, jnp.zeros_like(query_mine), value_mine]).astype(F32)
@@ -376,30 +419,34 @@
 
         all_rows = parts * rows
         plan = (parts, num_shard, num_seqs, heads_here, head_size)
-        tok_all, qkv_rows, context, *partials = pl.pallas_call(
+        taken = [
+            came_from, *tok_near, *[item for pair in tok_far for item in pair], *small_all,
+            *qkv_rel, qkv_bias.reshape(1, -1), out_mine,
+        ]
+        given = [
+            pltpu.HBM((all_rows, width), BF16),
+            pltpu.HBM((width, 3 * att_block), BF16),
+            pltpu.HBM((all_rows, 3 * att_block), BF16),
+            pltpu.HBM((all_rows, att_block), BF16),
+        ] + [jax.ShapeDtypeStruct((rows, width), F32)] * parts
+        tok_all, qkv_mine, qkv_rows, context, *partials = pl.pallas_call(
             lambda *refs: attend_kernel(plan, *refs),
             in_specs=[SCALARS] + whole(2 * parts + num_shard + 2),
-            out_specs=whole(3 + parts),
-            out_shape=[
-                jax.ShapeDtypeStruct((all_rows, width), BF16),
-                jax.ShapeDtypeStruct((all_rows, 3 * att_block), BF16),
-                jax.ShapeDtypeStruct((all_rows, att_block), BF16),
-            ]
-            + [jax.ShapeDtypeStruct((rows, width), F32)] * parts,
-            compiler_params=ROOMY,
+            out_specs=[pl.BlockSpec(memory_space=pltpu.HBM)] * 4 + whole(parts),
+            out_shape=given,
+            scratch_shapes=[pltpu.VMEM(item.shape, item.dtype) for item in given[:4]]
+            + [pltpu.SemaphoreType.DMA((4,))],
+            compiler_params=vmem(*taken, *given, spare=6),
             name="attend",
-        )(
-            came_from, *tok_near, *[item for pair in tok_far for item in pair], *small_all,
-            *qkv_rel, qkv_bias.reshape(1, -1), out_mine,
-        )
+        )(*taken)
         resid1 = tokens.astype(F32) + scatter_rows(partials) + out_bias_full
         hidden1, normed1, inv_std1 = norm_rows(resid1, gain1, shift1)
-        hidden1_half, up_rel = lax.optimization_barrier((hidden1.astype(BF16), up_rel))
-        hid_all = stack(*gather_rows(hidden1_half))
+        hid_all = stack(*gather_rows(hidden1.astype(BF16)))
 
         up_mine = jnp.concatenate(in_order(up_rel, shard_at), axis=0)
         pre_act = dot(hid_all, up_mine) + up_bias_mine
         activ = erf_gelu(pre_act).astype(BF16)
+        slope = lax.optimization_barrier(gelu_slope(lax.optimization_barrier((pre_act, activ))[0]))
         resid2 = hidden1 + scatter_rows(split(dot(activ, down_mine))) + down_bias_full
         layer_f32, normed2, inv_std2 = norm_rows(resid2, gain2, shift2)
         layer_out = layer_f32.astype(BF16)
@@ -411,7 +458,7 @@
         grad_down_bias = jnp.sum(grad_resid2, axis=0)
         mlp_all = stack(*gather_rows(grad_resid2.astype(BF16)))
         sum_down = dot_rows(activ, mlp_all).astype(BF16)
-        grad_pre = dot_cols(mlp_all, down_mine) * gelu_slope(pre_act)
+        grad_pre = dot_cols(mlp_all, down_mine) * slope
         grad_pre_half = grad_pre.astype(BF16)
         grad_up_bias = jnp.sum(grad_pre, axis=0)
         sum_up = dot_rows(hid_all, grad_pre_half).astype(BF16)
@@ -421,74 +468,74 @@
         grad_resid1 = norm_back(grad_hidden1, normed1, inv_std1, gain1)
         grad_out_bias = jnp.sum(grad_resid1, axis=0)
         attn_near, attn_far = gather_rows(grad_resid1.astype(BF16))
+        taken = [
+            *attn_near, *[item for pair in attn_far for item in pair], *small_all,
+            qkv_rows, out_mine,
+        ]
+        given = [
+            jax.ShapeDtypeStruct((all_rows, width), BF16),
+            jax.ShapeDtypeStruct((all_rows, 3 * att_block), BF16),
+            jax.ShapeDtypeStruct((2, att_block), F32),
+        ]
         attn_all, grad_qkv, bias_sums = pl.pallas_call(
             lambda *refs: attend_back_kernel(plan, *refs),
             in_specs=whole(2 * parts + 2),
             out_specs=whole(3),
-            out_shape=[
-                jax.ShapeDtypeStruct((all_rows, width), BF16),
-                jax.ShapeDtypeStruct((all_rows, 3 * att_block), BF16),
-                jax.ShapeDtypeStruct((2, att_block), F32),
-            ],
+            out_shape=given,
             scratch_shapes=[pltpu.VMEM((all_rows, att_block), BF16)],
-            compiler_params=ROOMY,
+            compiler_params=vmem(*taken, *given, context, spare=6),
             name="attend_back",
-        )(
-            *attn_near, *[item for pair in attn_far for item in pair], *small_all,
-            qkv_rows, out_mine,
-        )
+        )(*taken)
         sum_out = dot_rows(context, attn_all).astype(BF16)
         grad_query_bias, grad_value_bias = bias_sums[0], bias_sums[1]
         sum_qkv = dot_rows(tok_all, grad_qkv).astype(BF16)
-        input_grad = (grad_resid1 + scatter_rows(split(dot_cols(grad_qkv, qkv_mine)))).astype(BF16)
-
-        def side_at(stage):
-            bit = jnp.where(core_at == 0, orders[0][stage], orders[1][stage])
+        input_sum = scatter_rows(split(dot_cols(grad_qkv, qkv_mine)))
+        input_grad = (grad_resid1 + input_sum).astype(BF16)
+
+        def side_at(route, stage):
+            bit = jnp.where(core_at == 0, route[0][stage], route[1][stage])
             return (rep_at // bit) % 2
 
-        def halve(value, axis):
+        def halve(value, axis, name):
+            route = routes[name]
             for stage in range(len(bits)):
-                side = side_at(stage)
+                side = side_at(route, stage)
                 half = value.shape[axis] // 2
+                send = lax.dynamic_slice_in_dim(value, (1 - side) * half, half, axis)
+                came = step_flip(send, route, stage)
                 keep = lax.dynamic_slice_in_dim(value, side * half, half, axis)
-                send = lax.dynamic_slice_in_dim(value, (1 - side) * half, half, axis)
-                came = step_flip(send, stage)
                 value = (keep.astype(F32) + came.astype(F32)).astype(BF16)
             return value
 
-        def double(value):
+        def double(value, name):
+            route = backs[name]
             for stage in reversed(range(len(bits))):
-                came = step_flip(value, stage)
-                low = side_at(stage) == 0
+                came = step_flip(value, route, stage)
+                low = side_at(route, stage) == 0
                 value = jnp.concatenate(
                     [jnp.where(low, value, came), jnp.where(low, came, value)], axis=0
                 )
             return value
 
-        def both_cores(value):
+        def reduce_by_rows(value, name):
+            value = double(halve(value, 0, name), name)
             other = sibling(value)
-            first = core_at == 0
-            return jnp.where(first, value, other), jnp.where(first, other, value)
-
-        def reduce_by_rows(value):
-            value = double(halve(value, 0))
-            other = sibling(value)
-            return merge_rows(value, other, core_at)
-
-        def reduce_by_columns(value, repeats):
-            piece = halve(value.reshape(num_shard, depth, -1), 1)
+            return value, other
+
+        def reduce_by_columns(value, repeats, name):
+            piece = halve(value.reshape(num_shard, depth, -1), 1, name)
             relative = [lax.dynamic_index_in_dim(piece, shard_at, 0, keepdims=False)]
             for k in offsets:
                 out_to = lax.dynamic_index_in_dim(piece, (shard_at + k) % num_shard, 0, keepdims=False)
                 relative.append(turn(out_to, k))
-            full = double(jnp.concatenate(in_order(relative, shard_at), axis=1))
+            full = double(jnp.concatenate(in_order(relative, shard_at), axis=1), name)
             other = sibling(full)
-            return merge_columns(full, other, core_at, num_shard, repeats)
-
-        total_down = reduce_by_rows(sum_down)
-        total_up = reduce_by_columns(sum_up, 1)
-        total_out = reduce_by_rows(sum_out)
-        total_qkv = reduce_by_columns(sum_qkv, 3)
+            swap = routes[name] != backs[name]
+            return merge_columns(full, other, core_at, num_shard, repeats, swap)
+
+        total_down = merge_rows(*reduce_by_rows(sum_down, "down"), core_at)
+        total_up = reduce_by_columns(sum_up, 1, "up")
+        total_qkv = reduce_by_columns(sum_qkv, 3, "qkv")
 
         row_sums = jnp.stack(
             [grad_out_bias, grad_gain1, grad_shift1, grad_down_bias, grad_gain2, grad_shift2]
@@ -499,13 +546,21 @@
             there = lax.dynamic_index_in_dim(row_sums, (shard_at + k) % num_shard, 1, keepdims=False)
             mine = mine + turn(there, k)
         mine = mine + sibling(mine)
-        block_sums = jnp.concatenate([grad_query_bias, grad_value_bias, grad_up_bias])
-        packed = jnp.concatenate([mine.reshape(-1), block_sums])
-        for bit in bits:
-            packed = packed + flip(packed, bit)
+        packed = jnp.concatenate(
+            [mine.reshape(-1), grad_query_bias, grad_value_bias, grad_up_bias]
+        )
+        beside = -(-packed.size // (128 * att_block)) * 128
+        packed_rows = jnp.pad(packed, (0, att_block * beside - packed.size)).astype(BF16)
+        sum_out = jnp.concatenate([sum_out, packed_rows.reshape(att_block, beside)], axis=1)
+        out_here, out_there = reduce_by_rows(sum_out, "out")
+        total_out = merge_rows(out_here[:, :width], out_there[:, :width], core_at)
+        packed = out_here[:, width:].reshape(-1).astype(F32)
+        packed_there = out_there[:, width:].reshape(-1).astype(F32)
         mine = packed[: 6 * depth].reshape(6, depth)
-        block_sums = packed[6 * depth :]
-        first, second = both_cores(block_sums)
+        block_sums = packed[6 * depth : 6 * depth + 2 * att_block + ff_block]
+        other_sums = packed_there[6 * depth : 6 * depth + 2 * att_block + ff_block]
+        first = jnp.where(core_at == 0, block_sums, other_sums)
+        second = jnp.where(core_at == 0, other_sums, block_sums)
         total_query = jnp.concatenate([first[:att_block], second[:att_block]])
         total_value = jnp.concatenate(
             [first[att_block : 2 * att_block], second[att_block : 2 * att_block]]

time: 337 us -> 314 us (0.932)
  Pallas kernels: 45.8 us -> 33 us
  waiting for transfers between devices: 156 us -> 163 us
  starting transfers between devices: 76.6 us -> 70.2 us
  local copies, waits for them, and re-layouts: 17.6 us -> 11.5 us
  other arithmetic: 23.2 us -> 18.1 us
    ppermute x24, waiting for transfers between devices: 77.4 us -> 95.4 us  [step_flip(): lax.ppermute(value, 'rep', [(i, i ^ route[i % CORES][stage]) for i in ran...]
    ppermute x24, starting transfers between devices: 45 us -> 27.9 us  [step_flip(): lax.ppermute(value, 'rep', [(i, i ^ route[i % CORES][stage]) for i in ran...]
    ppermute x28 -> x24, waiting for transfers between devices: 16.6 us -> 3.36 us  [flip(): return lax.ppermute(value, 'rep', [(i, i ^ bit) for i in range(num_rep)])]
    ppermute x28 -> x24, starting transfers between devices: 9.14 us -> 18.7 us  [flip(): return lax.ppermute(value, 'rep', [(i, i ^ bit) for i in range(num_rep)])]
    pallas_call x2, Pallas kernels: 14.2 us -> 8.52 us  [merge_columns(): pl.pallas_call(kernel, grid_spec=pltpu.PrefetchScalarGridSpec(num_scalar_...]
    pallas_call x2, Pallas kernels: 10.1 us -> 5.94 us  [merge_rows(): pl.pallas_call(kernel, grid_spec=pltpu.PrefetchScalarGridSpec(num_scalar_...]
    unnamed x117 -> x94, local copies, waits for them, and re-layouts: 11.8 us -> 7.75 us
  transfers between devices with their start and end apart: 66 -> 62, of which waited for: 30 -> 26; matrix products, arithmetic and copies ran while one was open for 10% -> 9% of each run, Pallas kernels for 9% -> 6%
where the time goes in v1:
time: 314 us; the launch traced here: 313 us
  waiting for transfers between devices  163 us (52%)
  starting transfers between devices  70.2 us (22%)
  Pallas kernels  33 us (11%)
  other arithmetic  18.1 us (6%)
  matrix products  14.3 us (5%)
  local copies, waits for them, and re-layouts  11.5 us (4%)
    ppermute x24, waiting for transfers between devices, step_flip(): lax.ppermute(value, 'rep', [(i, i ^ route[i % CORES][stage]) for i in ran...  95.4 us
    ppermute x14, waiting for transfers between devices, turn(): return lax.ppermute(value, 'shard', pairs)  64.5 us
    ppermute x24, starting transfers between devices, step_flip(): lax.ppermute(value, 'rep', [(i, i ^ route[i % CORES][stage]) for i in ran...  27.9 us
    ppermute x14, starting transfers between devices, turn(): return lax.ppermute(value, 'shard', pairs)  23.6 us
    ppermute x24, starting transfers between devices, flip(): return lax.ppermute(value, 'rep', [(i, i ^ bit) for i in range(num_rep)])  18.7 us
    pallas_call x2, Pallas kernels, merge_columns(): pl.pallas_call(kernel, grid_spec=pltpu.PrefetchScalarGridSpec(num_scalar_...  8.52 us
    unnamed x94, local copies, waits for them, and re-layouts  7.75 us
    pallas_call x1, Pallas kernels, on_device(): pl.pallas_call(lambda *refs: attend_kernel(plan, *refs), in_specs=[SCALAR...  7.07 us
  transfers between devices with their start and end apart: 62, of which 26 were waited for; matrix products, arithmetic and copies ran while one was open for 9% of the time, Pallas kernels for 6%

profile of v1, /device:TPU:0, one launch (start us, length us, event | category | flops | bytes accessed | tf_op | source)
XLA Modules:
  0.0 313.2 jit_solution(12239407274338154978)
XLA Ops:
  3.0 3.0 collective-permute-start.6
  10.7 18.8 %collective-permute-done.1.refs_3_ = bf16[128,1024]{1,0:T(8,128)(2,1)S(1)} collective-permute-done((bf16[128,1024]{1,0:T(8,128)(2,1)S(1)}, bf16[128,1024]{1,0:T(8,128)(2,1)S(1)}, u32[]{:S(2)}, u32[]{:S(2)}) %collective-permute-start.1) | collective-permute-done | bytes 262176 | tf_op jit(solution)/shard_map/ppermute | solution.py:324
  36.1 7.1 %attend.1 = (bf16[512,1024]{1,0:T(8,128)(2,1)}, bf16[1024,768]{1,0:T(8,128)(2,1)}, bf16[512,768]{1,0:T(8,128)(2,1)}, bf16[512,256]{1,0:T(8,128)(2,1)}, f32[128,1...) custom-call(s32[2]{0:T(128)S(1)} %and_select_fusion.refs_0_, ...), custom_call_target="tpu_custom_call" | custom-call | tf_op jit(solution)/shard_map/attend/pallas_call | solution.py:432
  49.8 10.0 %collective-permute-done.13 = bf16[256,1024]{1,0:T(8,128)(2,1)} collective-permute-done((bf16[256,1024]{1,0:T(8,128)(2,1)S(1)}, bf16[256,1024]{1,0:T(8,128)(2,1)}, u32[]{:S(2)}, u32[]{:S(2)}) %collective-permute-start.13) | collective-permute-done | bytes 524320 | tf_op jit(solution)/shard_map/ppermute | solution.py:324
  61.5 3.3 %collective-permute-done.9 = bf16[128,1024]{1,0:T(8,128)(2,1)S(1)} collective-permute-done((bf16[128,1024]{1,0:T(8,128)(2,1)S(1)}, bf16[128,1024]{1,0:T(8,128)(2,1)S(1)}, u32[]{:S(2)}, u32[]{:S(2)}) %collective-permute-start.9) | collective-permute-done | bytes 262176 | tf_op jit(solution)/shard_map/ppermute | solution.py:324
  68.6 4.9 %collective-permute-done.11 = bf16[128,1024]{1,0:T(8,128)(2,1)} collective-permute-done((bf16[128,1024]{1,0:T(8,128)(2,1)S(1)}, bf16[128,1024]{1,0:T(8,128)(2,1)}, u32[]{:S(2)}, u32[]{:S(2)}) %collective-permute-start.11) | collective-permute-done | bytes 262176 | tf_op jit(solution)/shard_map/ppermute | solution.py:324
  75.4 2.6 multiply_convert_fusion
  83.5 6.8 %collective-permute-done.17 = bf16[128,1024]{1,0:T(8,128)(2,1)S(1)} collective-permute-done((bf16[128,1024]{1,0:T(8,128)(2,1)S(1)}, bf16[128,1024]{1,0:T(8,128)(2,1)S(1)}, u32[]{:S(2)}, u32[]{:S(2)}) %collective-permute-start.17) | collective-permute-done | bytes 262176 | tf_op jit(solution)/shard_map/ppermute | solution.py:324
  94.0 6.0 %collective-permute-done.19 = bf16[128,1024]{1,0:T(8,128)(2,1)S(1)} collective-permute-done((bf16[128,1024]{1,0:T(8,128)(2,1)S(1)}, bf16[128,1024]{1,0:T(8,128)(2,1)S(1)}, u32[]{:S(2)}, u32[]{:S(2)}) %collective-permute-start.19) | collective-permute-done | bytes 262176 | tf_op jit(solution)/shard_map/ppermute | solution.py:324
  106.2 2.8 convolution_convert_fusion
  130.8 2.9 collective-permute-done.25.refs_2_
  133.7 6.9 %collective-permute-done.47 = bf16[2,256,1024]{2,1,0:T(8,128)(2,1)} collective-permute-done((bf16[2,256,1024]{2,1,0:T(8,128)(2,1)}, bf16[2,256,1024]{2,1,0:T(8,128)(2,1)}, u32[]{:S(2)}, u32[]{:S(2)}) %collective-permute-start.47) | collective-permute-done | bytes 1048608 | tf_op jit(solution)/shard_map/ppermute | solution.py:315
  144.4 5.7 %attend_back.1 = (bf16[512,1024]{1,0:T(8,128)(2,1)S(1)}, bf16[512,768]{1,0:T(8,128)(2,1)S(1)}, f32[2,256]{1,0:T(2,128)S(1)}) custom-call(bf16[128,1024]{1,0:T(8,128)(2,1)S(1)} %convert_element_type.218.refs_0_, bf16[128,1024]{1,0:T(8,128)(2,1)S(1)} %collective-permute-done.24.refs_1_, bf16[128,1024]{1,0:T(8,128)(2,1)S(1)} %collective-permute-done.25.refs_2_, ...), custom_call_target="tpu_custom_call" | custom-call | tf_op jit(solution)/shard_map/attend_back/pallas_call | solution.py:480
  155.6 2.6 collective-permute-start.57
  159.0 6.7 %collective-permute-done.41 = bf16[64,1152]{1,0:T(8,128)(2,1)S(1)} collective-permute-done((bf16[64,1152]{1,0:T(8,128)(2,1)S(1)}, bf16[64,1152]{1,0:T(8,128)(2,1)S(1)}, u32[]{:S(2)}, u32[]{:S(2)}) %collective-permute-start.41) | collective-permute-done | bytes 147488 | tf_op jit(solution)/shard_map/ppermute | solution.py:315
  172.6 2.6 collective-permute-start.29
  175.3 10.3 %collective-permute-start.27 = (f32[128,1024]{1,0:T(8,128)S(1)}, f32[128,1024]{1,0:T(8,128)S(1)}, u32[]{:S(2)}, u32[]{:S(2)}) collective-permute-start(f32[128,1024]{1,0:T(8,128)S(1)} %get-tuple-element.69), channel_id=1, source_target_pairs={{0,2},{2,0},{4,6},{6,4},{8,10},{10,8},{12,14},{14,12},{16,18},{18,... | collective-permute-start | bytes 1572872 | tf_op jit(solution)/shard_map/ppermute | solution.py:312
  187.1 4.6 %collective-permute-done.50 = bf16[64,1024]{1,0:T(8,128)(2,1)S(1)} collective-permute-done((bf16[64,1024]{1,0:T(8,128)(2,1)S(1)}, bf16[64,1024]{1,0:T(8,128)(2,1)S(1)}, u32[]{:S(2)}, u32[]{:S(2)}) %collective-permute-start.50) | collective-permute-done | bytes 131104 | tf_op jit(solution)/shard_map/ppermute | solution.py:324
  191.8 10.5 %collective-permute-done.44 = bf16[64,1152]{1,0:T(8,128)(2,1)S(1)} collective-permute-done((bf16[64,1152]{1,0:T(8,128)(2,1)S(1)}, bf16[64,1152]{1,0:T(8,128)(2,1)S(1)}, u32[]{:S(2)}, u32[]{:S(2)}) %collective-permute-start.44) | collective-permute-done | bytes 147488 | tf_op jit(solution)/shard_map/ppermute | solution.py:315
  207.3 9.7 %collective-permute-done.51 = bf16[64,2048]{1,0:T(8,128)(2,1)S(1)} collective-permute-done((bf16[64,2048]{1,0:T(8,128)(2,1)S(1)}, bf16[64,2048]{1,0:T(8,128)(2,1)S(1)}, u32[]{:S(2)}, u32[]{:S(2)}) %collective-permute-start.51) | collective-permute-done | bytes 262176 | tf_op jit(solution)/shard_map/ppermute | solution.py:315
  219.4 3.2 %collective-permute-done.31 = bf16[2,128,768]{2,1,0:T(8,128)(2,1)S(1)} collective-permute-done((bf16[2,128,768]{2,1,0:T(8,128)(2,1)S(1)}, bf16[2,128,768]{2,1,0:T(8,128)(2,1)S(1)}, u32[]{:S(2)}, u32[]{:S(2)}) %collective-permute-start.31) | collective-permute-done | bytes 393248 | tf_op jit(solution)/shard_map/ppermute | solution.py:315
  223.4 12.7 %collective-permute-done.32 = bf16[2,64,768]{2,1,0:T(8,128)(2,1)S(1)} collective-permute-done((bf16[2,64,768]{2,1,0:T(8,128)(2,1)S(1)}, bf16[2,64,768]{2,1,0:T(8,128)(2,1)S(1)}, u32[]{:S(2)}, u32[]{:S(2)}) %collective-permute-start.32) | collective-permute-done | bytes 196640 | tf_op jit(solution)/shard_map/ppermute | solution.py:315
  237.4 3.5 %collective-permute-done.33 = bf16[64,768]{1,0:T(8,128)(2,1)S(1)} collective-permute-done((bf16[64,768]{1,0:T(8,128)(2,1)S(1)}, bf16[64,768]{1,0:T(8,128)(2,1)S(1)}, u32[]{:S(2)}, u32[]{:S(2)}) %collective-permute-start.33) | collective-permute-done | bytes 98336 | tf_op jit(solution)/shard_map/ppermute | solution.py:324
  240.9 3.3 %collective-permute-start.46 = (bf16[256,1152]{1,0:T(8,128)(2,1)S(1)}, bf16[256,1152]{1,0:T(8,128)(2,1)S(1)}, u32[]{:S(2)}, u32[]{:S(2)}) collective-permute-start(bf16[256,1152]{1,0:T(8,128)(2,1)S(1)} %pad_maximum_fusion.12), channel_id=1, source_target_pairs={{0,2},{2,0},{4,6},{6,4},{8,10},{10,8},{12,14},{14,12},{16,18},{18,... | collective-permute-start | bytes 1769480 | tf_op jit(solution)/shard_map/ppermute | solution.py:312
  245.7 10.6 %collective-permute-done.34 = bf16[64,1536]{1,0:T(8,128)(2,1)S(1)} collective-permute-done((bf16[64,1536]{1,0:T(8,128)(2,1)S(1)}, bf16[64,1536]{1,0:T(8,128)(2,1)S(1)}, u32[]{:S(2)}, u32[]{:S(2)}) %collective-permute-start.34) | collective-permute-done | bytes 196640 | tf_op jit(solution)/shard_map/ppermute | solution.py:315
  256.8 11.6 %collective-permute-done.35 = bf16[128,1536]{1,0:T(8,128)(2,1)S(1)} collective-permute-done((bf16[128,1536]{1,0:T(8,128)(2,1)S(1)}, bf16[128,1536]{1,0:T(8,128)(2,1)S(1)}, u32[]{:S(2)}, u32[]{:S(2)}) %collective-permute-start.35) | collective-permute-done | bytes 393248 | tf_op jit(solution)/shard_map/ppermute | solution.py:315
  270.6 3.5 %collective-permute-done.60 = bf16[512,1024]{1,0:T(8,128)(2,1)S(1)} collective-permute-done((bf16[512,1024]{1,0:T(8,128)(2,1)S(1)}, bf16[512,1024]{1,0:T(8,128)(2,1)S(1)}, u32[]{:S(2)}, u32[]{:S(2)}) %collective-permute-start.60) | collective-permute-done | bytes 1048608 | tf_op jit(solution)/shard_map/ppermute | solution.py:315
  275.2 10.2 %collective-permute-done.53 = bf16[256,2048]{1,0:T(8,128)(2,1)S(1)} collective-permute-done((bf16[256,2048]{1,0:T(8,128)(2,1)S(1)}, bf16[256,2048]{1,0:T(8,128)(2,1)S(1)}, u32[]{:S(2)}, u32[]{:S(2)}) %collective-permute-start.53) | collective-permute-done | bytes 1048608 | tf_op jit(solution)/shard_map/ppermute | solution.py:315
  286.2 7.6 %collective-permute-done.36 = bf16[256,1536]{1,0:T(8,128)(2,1)S(1)} collective-permute-done((bf16[256,1536]{1,0:T(8,128)(2,1)S(1)}, bf16[256,1536]{1,0:T(8,128)(2,1)S(1)}, u32[]{:S(2)}, u32[]{:S(2)}) %collective-permute-start.36) | collective-permute-done | bytes 786464 | tf_op jit(solution)/shard_map/ppermute | solution.py:315
  300.2 4.0 %merge_columns.2 = f32[512,3072]{1,0:T(8,128)} custom-call(s32[1]{0:T(128)} %bitcast.8.at_ref, bf16[512,1536]{1,0:T(8,128)(2,1)S(1)} %pad_maximum_fusion.3.mine_ref, bf16[512,1536]{1,0:T(8,128)(2,1)S(1)} %collective-permute-done.37.other_ref), custom_call_target="tpu_custom_call" | custom-call | tf_op jit(solution)/shard_map/merge_columns/pallas_call | solution.py:281
  304.2 4.5 %merge_rows.3 = f32[2048,1024]{1,0:T(8,128)} custom-call(s32[1]{0:T(128)} %bitcast.8.at_ref, bf16[1024,1024]{1,0:T(8,128)(2,1)S(1)} %pad_maximum_fusion.2.mine_ref, bf16[1024,1024]{1,0:T(8,128)(2,1)S(1)} %collective-permute-done.61.other_ref), custom_call_target="tpu_custom_call" | custom-call | tf_op jit(solution)/shard_map/merge_rows/pallas_call | solution.py:219
  308.7 4.5 %merge_columns.3 = f32[512,4096]{1,0:T(8,128)} custom-call(s32[1]{0:T(128)} %bitcast.8.at_ref, bf16[512,2048]{1,0:T(8,128)(2,1)S(1)} %pad_maximum_fusion.1.mine_ref, bf16[512,2048]{1,0:T(8,128)(2,1)S(1)} %collective-permute-done.54.other_ref), custom_call_target="tpu_custom_call" | custom-call | tf_op jit(solution)/shard_map/merge_columns/pallas_call | solution.py:281
  (330 shorter events, 103.4 us)
Async XLA Ops:
  3.0 29.7 %collective-permute-start.6 = (bf16[512,768]{1,0:T(8,128)(2,1)}, bf16[512,768]{1,0:T(8,128)(2,1)S(1)}, u32[]{:S(2)}, u32[]{:S(2)}) collective-permute-start(bf16[512,768]{1,0:T(8,128)(2,1)} %take_columns.6), channel_id=1, source_target_pairs={{0,1},{1,0},{2,3},{3,2},{4,5},{5,4},{6,7},{7,6},{8,9},{9,8},{10,11... | collective-permute-start | bytes 2359304 | tf_op jit(solution)/shard_map/ppermute | solution.py:324
  6.0 23.5 %collective-permute-start.1 = (bf16[128,1024]{1,0:T(8,128)(2,1)S(1)}, bf16[128,1024]{1,0:T(8,128)(2,1)S(1)}, u32[]{:S(2)}, u32[]{:S(2)}) collective-permute-start(bf16[128,1024]{1,0:T(8,128)(2,1)S(1)} %copy-done.2), channel_id=1, source_target_pairs={{0,1},{1,0},{2,3},{3,2},{4,5},{5,4},{6,7},{7,6},{8,9},{9,8},{10,11... | collective-permute-start | bytes 786440 | tf_op jit(solution)/shard_map/ppermute | solution.py:324
  8.2 21.6 %collective-permute-start.4 = (bf16[7,512]{1,0:T(8,128)(2,1)S(1)}, bf16[7,512]{1,0:T(8,128)(2,1)S(1)}, u32[]{:S(2)}, u32[]{:S(2)}) collective-permute-start(bf16[7,512]{1,0:T(8,128)(2,1)S(1)} %reshape.186.refs_5_.refs_4_), channel_id=1, source_target_pairs={{0,1},{1,0},{2,3},{3,2},{4,5},{5,4},{6,7},{7,6},{8,9},{9,8},{10,11... | collective-permute-start | bytes 21512 | tf_op jit(solution)/shard_map/ppermute | solution.py:324
  10.2 22.6 %collective-permute-start.3 = (bf16[7,512]{1,0:T(8,128)(2,1)S(1)}, bf16[7,512]{1,0:T(8,128)(2,1)S(1)}, u32[]{:S(2)}, u32[]{:S(2)}) collective-permute-start(bf16[7,512]{1,0:T(8,128)(2,1)S(1)} %reshape.186.refs_5_.refs_4_), channel_id=1, source_target_pairs={{0,2},{2,0},{4,6},{6,4},{8,10},{10,8},{12,14},{14,12},{16,18},{18,... | collective-permute-start | bytes 21512 | tf_op jit(solution)/shard_map/ppermute | solution.py:312
  10.2 22.6 %collective-permute-start = (bf16[128,1024]{1,0:T(8,128)(2,1)S(1)}, bf16[128,1024]{1,0:T(8,128)(2,1)S(1)}, u32[]{:S(2)}, u32[]{:S(2)}) collective-permute-start(bf16[128,1024]{1,0:T(8,128)(2,1)S(1)} %copy-done.2), channel_id=1, source_target_pairs={{0,2},{2,0},{4,6},{6,4},{8,10},{10,8},{12,14},{14,12},{16,18},{18,... | collective-permute-start | bytes 786440 | tf_op jit(solution)/shard_map/ppermute | solution.py:312
  44.8 15.0 %collective-permute-start.13 = (bf16[256,1024]{1,0:T(8,128)(2,1)S(1)}, bf16[256,1024]{1,0:T(8,128)(2,1)}, u32[]{:S(2)}, u32[]{:S(2)}) collective-permute-start(bf16[256,1024]{1,0:T(8,128)(2,1)S(1)} %constant_dynamic-slice_fusion.13), channel_id=1, source_target_pairs={{0,1},{1,0},{2,3},{3,2},{4,5},{5,4},{6,7},{7,6},{8,9},{9,8},{10,11... | collective-permute-start | bytes 1572872 | tf_op jit(solution)/shard_map/ppermute | solution.py:324
  46.6 14.9 %collective-permute-start.7 = (f32[128,1024]{1,0:T(8,128)}, f32[128,1024]{1,0:T(8,128)S(1)}, u32[]{:S(2)}, u32[]{:S(2)}) collective-permute-start(f32[128,1024]{1,0:T(8,128)} %copy-done.9), channel_id=1, source_target_pairs={{0,2},{2,0},{4,6},{6,4},{8,10},{10,8},{12,14},{14,12},{16,18},{18,... | collective-permute-start | bytes 1572872 | tf_op jit(solution)/shard_map/ppermute | solution.py:312
  48.0 16.8 %collective-permute-start.9 = (bf16[128,1024]{1,0:T(8,128)(2,1)S(1)}, bf16[128,1024]{1,0:T(8,128)(2,1)S(1)}, u32[]{:S(2)}, u32[]{:S(2)}) collective-permute-start(bf16[128,1024]{1,0:T(8,128)(2,1)S(1)} %add_convert_fusion.10), channel_id=1, source_target_pairs={{0,1},{1,0},{2,3},{3,2},{4,5},{5,4},{6,7},{7,6},{8,9},{9,8},{10,11... | collective-permute-start | bytes 786440 | tf_op jit(solution)/shard_map/ppermute | solution.py:324
  110.1 16.8 %collective-permute-start.55 = (bf16[512,1024]{1,0:T(8,128)(2,1)}, bf16[512,1024]{1,0:T(8,128)(2,1)}, u32[]{:S(2)}, u32[]{:S(2)}) collective-permute-start(bf16[512,1024]{1,0:T(8,128)(2,1)} %constant_dynamic-slice_fusion.2), channel_id=1, source_target_pairs={{0,4},{2,10},{4,0},{6,14},{8,12},{10,2},{12,8},{14,6},{16,20},{18,... | collective-permute-start | bytes 3145736 | tf_op jit(solution)/shard_map/ppermute | solution.py:315
  117.1 23.5 %collective-permute-start.47 = (bf16[2,256,1024]{2,1,0:T(8,128)(2,1)}, bf16[2,256,1024]{2,1,0:T(8,128)(2,1)}, u32[]{:S(2)}, u32[]{:S(2)}) collective-permute-start(bf16[2,256,1024]{2,1,0:T(8,128)(2,1)} %constant_dynamic-slice_fusion.5), channel_id=1, source_target_pairs={{0,4},{2,10},{4,0},{6,14},{8,12},{10,2},{12,8},{14,6},{16,20},{18,... | collective-permute-start | bytes 3145736 | tf_op jit(solution)/shard_map/ppermute | solution.py:315
  126.9 17.5 %collective-permute-start.24 = (bf16[128,1024]{1,0:T(8,128)(2,1)S(1)}, bf16[128,1024]{1,0:T(8,128)(2,1)S(1)}, u32[]{:S(2)}, u32[]{:S(2)}) collective-permute-start(bf16[128,1024]{1,0:T(8,128)(2,1)S(1)} %convert_element_type.218.refs_0_), channel_id=1, source_target_pairs={{0,2},{2,0},{4,6},{6,4},{8,10},{10,8},{12,14},{14,12},{16,18},{18,... | collective-permute-start | bytes 786440 | tf_op jit(solution)/shard_map/ppermute | solution.py:312
  129.1 26.2 %collective-permute-start.56 = (bf16[256,1024]{1,0:T(8,128)(2,1)S(1)}, bf16[256,1024]{1,0:T(8,128)(2,1)S(1)}, u32[]{:S(2)}, u32[]{:S(2)}) collective-permute-start(bf16[256,1024]{1,0:T(8,128)(2,1)S(1)} %constant_dynamic-slice_fusion.1), channel_id=1, source_target_pairs={{0,8},{2,6},{4,12},{6,2},{8,0},{10,14},{12,4},{14,10},{16,24},{18,... | collective-permute-start | bytes 1572872 | tf_op jit(solution)/shard_map/ppermute | solution.py:315
  142.3 16.5 %collective-permute-start.48 = (bf16[2,128,1024]{2,1,0:T(8,128)(2,1)S(1)}, bf16[2,128,1024]{2,1,0:T(8,128)(2,1)S(1)}, u32[]{:S(2)}, u32[]{:S(2)}) collective-permute-start(bf16[2,128,1024]{2,1,0:T(8,128)(2,1)S(1)} %constant_dynamic-slice_fusion.4), channel_id=1, source_target_pairs={{0,8},{2,6},{4,12},{6,2},{8,0},{10,14},{12,4},{14,10},{16,24},{18,... | collective-permute-start | bytes 1572872 | tf_op jit(solution)/shard_map/ppermute | solution.py:315
  153.5 19.0 %collective-permute-start.28 = (f32[128,1024]{1,0:T(8,128)S(1)}, f32[128,1024]{1,0:T(8,128)S(1)}, u32[]{:S(2)}, u32[]{:S(2)}) collective-permute-start(f32[128,1024]{1,0:T(8,128)S(1)} %slice.230), channel_id=1, source_target_pairs={{0,2},{2,0},{4,6},{6,4},{8,10},{10,8},{12,14},{14,12},{16,18},{18,... | collective-permute-start | bytes 1572872 | tf_op jit(solution)/shard_map/ppermute | solution.py:312
  154.7 47.7 %collective-permute-start.30 = (bf16[2,256,768]{2,1,0:T(8,128)(2,1)S(1)}, bf16[2,256,768]{2,1,0:T(8,128)(2,1)S(1)}, u32[]{:S(2)}, u32[]{:S(2)}) collective-permute-start(bf16[2,256,768]{2,1,0:T(8,128)(2,1)S(1)} %constant_dynamic-slice_fusion.12), channel_id=1, source_target_pairs={{0,4},{2,6},{4,0},{6,2},{8,12},{10,14},{12,8},{14,10},{16,20},{18,... | collective-permute-start | bytes 2359304 | tf_op jit(solution)/shard_map/ppermute | solution.py:315
  155.6 19.7 %collective-permute-start.57 = (bf16[128,1024]{1,0:T(8,128)(2,1)S(1)}, bf16[128,1024]{1,0:T(8,128)(2,1)S(1)}, u32[]{:S(2)}, u32[]{:S(2)}) collective-permute-start(bf16[128,1024]{1,0:T(8,128)(2,1)S(1)} %constant_dynamic-slice_fusion), channel_id=1, source_target_pairs={{0,16},{2,18},{4,20},{6,22},{8,24},{10,26},{12,28},{14,30},{16,0},... | collective-permute-start | bytes 786440 | tf_op jit(solution)/shard_map/ppermute | solution.py:315
  167.1 18.5 %collective-permute-start.49 = (bf16[2,64,1024]{2,1,0:T(8,128)(2,1)S(1)}, bf16[2,64,1024]{2,1,0:T(8,128)(2,1)S(1)}, u32[]{:S(2)}, u32[]{:S(2)}) collective-permute-start(bf16[2,64,1024]{2,1,0:T(8,128)(2,1)S(1)} %constant_dynamic-slice_fusion.3), channel_id=1, source_target_pairs={{0,16},{2,18},{4,20},{6,22},{8,24},{10,26},{12,28},{14,30},{16,0},... | collective-permute-start | bytes 786440 | tf_op jit(solution)/shard_map/ppermute | solution.py:315
  171.2 15.4 %collective-permute-start.43 = (bf16[32,1152]{1,0:T(8,128)(2,1)S(1)}, bf16[32,1152]{1,0:T(8,128)(2,1)S(1)}, u32[]{:S(2)}, u32[]{:S(2)}) collective-permute-start(bf16[32,1152]{1,0:T(8,128)(2,1)S(1)} %add_convert_fusion.13), channel_id=1, source_target_pairs={{0,16},{2,18},{4,20},{6,22},{8,24},{10,26},{12,28},{14,30},{16,0},... | collective-permute-start | bytes 221192 | tf_op jit(solution)/shard_map/ppermute | solution.py:315
  172.6 121.5 %collective-permute-start.29 = (bf16[128,1024]{1,0:T(8,128)(2,1)S(1)}, bf16[128,1024]{1,0:T(8,128)(2,1)S(1)}, u32[]{:S(2)}, u32[]{:S(2)}) collective-permute-start(bf16[128,1024]{1,0:T(8,128)(2,1)S(1)} %get-tuple-element.68), channel_id=1, source_target_pairs={{0,1},{1,0},{2,3},{3,2},{4,5},{5,4},{6,7},{7,6},{8,9},{9,8},{10,11... | collective-permute-start | bytes 786440 | tf_op jit(solution)/shard_map/ppermute | solution.py:324
  175.3 119.5 %collective-permute-start.27 = (f32[128,1024]{1,0:T(8,128)S(1)}, f32[128,1024]{1,0:T(8,128)S(1)}, u32[]{:S(2)}, u32[]{:S(2)}) collective-permute-start(f32[128,1024]{1,0:T(8,128)S(1)} %get-tuple-element.69), channel_id=1, source_target_pairs={{0,2},{2,0},{4,6},{6,4},{8,10},{10,8},{12,14},{14,12},{16,18},{18,... | collective-permute-start | bytes 1572872 | tf_op jit(solution)/shard_map/ppermute | solution.py:312
  185.6 19.0 %collective-permute-start.58 = (bf16[128,1024]{1,0:T(8,128)(2,1)S(1)}, bf16[128,1024]{1,0:T(8,128)(2,1)S(1)}, u32[]{:S(2)}, u32[]{:S(2)}) collective-permute-start(bf16[128,1024]{1,0:T(8,128)(2,1)S(1)} %add_convert_fusion.7), channel_id=1, source_target_pairs={{0,16},{2,18},{4,20},{6,22},{8,24},{10,26},{12,28},{14,30},{16,0},... | collective-permute-start | bytes 786440 | tf_op jit(solution)/shard_map/ppermute | solution.py:315
  202.3 14.7 %collective-permute-start.51 = (bf16[64,2048]{1,0:T(8,128)(2,1)S(1)}, bf16[64,2048]{1,0:T(8,128)(2,1)S(1)}, u32[]{:S(2)}, u32[]{:S(2)}) collective-permute-start(bf16[64,2048]{1,0:T(8,128)(2,1)S(1)} %pad_maximum_fusion.17), channel_id=1, source_target_pairs={{0,16},{2,18},{4,20},{6,22},{8,24},{10,26},{12,28},{14,30},{16,0},... | collective-permute-start | bytes 786440 | tf_op jit(solution)/shard_map/ppermute | solution.py:315
  202.4 14.7 %collective-permute-start.45 = (bf16[128,1152]{1,0:T(8,128)(2,1)S(1)}, bf16[128,1152]{1,0:T(8,128)(2,1)S(1)}, u32[]{:S(2)}, u32[]{:S(2)}) collective-permute-start(bf16[128,1152]{1,0:T(8,128)(2,1)S(1)} %pad_maximum_fusion.16), channel_id=1, source_target_pairs={{0,4},{2,10},{4,0},{6,14},{8,12},{10,2},{12,8},{14,6},{16,20},{18,... | collective-permute-start | bytes 884744 | tf_op jit(solution)/shard_map/ppermute | solution.py:315
  204.7 17.9 %collective-permute-start.31 = (bf16[2,128,768]{2,1,0:T(8,128)(2,1)S(1)}, bf16[2,128,768]{2,1,0:T(8,128)(2,1)S(1)}, u32[]{:S(2)}, u32[]{:S(2)}) collective-permute-start(bf16[2,128,768]{2,1,0:T(8,128)(2,1)S(1)} %constant_dynamic-slice_fusion.11), channel_id=1, source_target_pairs={{0,8},{2,10},{4,12},{6,14},{8,0},{10,2},{12,4},{14,6},{16,24},{18,... | collective-permute-start | bytes 1179656 | tf_op jit(solution)/shard_map/ppermute | solution.py:315
  217.0 27.3 %collective-permute-start.59 = (bf16[256,1024]{1,0:T(8,128)(2,1)S(1)}, bf16[256,1024]{1,0:T(8,128)(2,1)S(1)}, u32[]{:S(2)}, u32[]{:S(2)}) collective-permute-start(bf16[256,1024]{1,0:T(8,128)(2,1)S(1)} %pad_maximum_fusion.14), channel_id=1, source_target_pairs={{0,8},{2,6},{4,12},{6,2},{8,0},{10,14},{12,4},{14,10},{16,24},{18,... | collective-permute-start | bytes 1572872 | tf_op jit(solution)/shard_map/ppermute | solution.py:315
  217.1 39.2 %collective-permute-start.52 = (bf16[128,2048]{1,0:T(8,128)(2,1)S(1)}, bf16[128,2048]{1,0:T(8,128)(2,1)S(1)}, u32[]{:S(2)}, u32[]{:S(2)}) collective-permute-start(bf16[128,2048]{1,0:T(8,128)(2,1)S(1)} %pad_maximum_fusion.13), channel_id=1, source_target_pairs={{0,8},{2,6},{4,12},{6,2},{8,0},{10,14},{12,4},{14,10},{16,24},{18,... | collective-permute-start | bytes 1572872 | tf_op jit(solution)/shard_map/ppermute | solution.py:315
  240.9 54.7 %collective-permute-start.46 = (bf16[256,1152]{1,0:T(8,128)(2,1)S(1)}, bf16[256,1152]{1,0:T(8,128)(2,1)S(1)}, u32[]{:S(2)}, u32[]{:S(2)}) collective-permute-start(bf16[256,1152]{1,0:T(8,128)(2,1)S(1)} %pad_maximum_fusion.12), channel_id=1, source_target_pairs={{0,2},{2,0},{4,6},{6,4},{8,10},{10,8},{12,14},{14,12},{16,18},{18,... | collective-permute-start | bytes 1769480 | tf_op jit(solution)/shard_map/ppermute | solution.py:312
  256.3 17.8 %collective-permute-start.60 = (bf16[512,1024]{1,0:T(8,128)(2,1)S(1)}, bf16[512,1024]{1,0:T(8,128)(2,1)S(1)}, u32[]{:S(2)}, u32[]{:S(2)}) collective-permute-start(bf16[512,1024]{1,0:T(8,128)(2,1)S(1)} %pad_maximum_fusion.10), channel_id=1, source_target_pairs={{0,4},{2,10},{4,0},{6,14},{8,12},{10,2},{12,8},{14,6},{16,20},{18,... | collective-permute-start | bytes 3145736 | tf_op jit(solution)/shard_map/ppermute | solution.py:315
  268.4 16.9 %collective-permute-start.53 = (bf16[256,2048]{1,0:T(8,128)(2,1)S(1)}, bf16[256,2048]{1,0:T(8,128)(2,1)S(1)}, u32[]{:S(2)}, u32[]{:S(2)}) collective-permute-start(bf16[256,2048]{1,0:T(8,128)(2,1)S(1)} %pad_maximum_fusion.9), channel_id=1, source_target_pairs={{0,4},{2,10},{4,0},{6,14},{8,12},{10,2},{12,8},{14,6},{16,20},{18,... | collective-permute-start | bytes 3145736 | tf_op jit(solution)/shard_map/ppermute | solution.py:315
  274.1 19.7 %collective-permute-start.36 = (bf16[256,1536]{1,0:T(8,128)(2,1)S(1)}, bf16[256,1536]{1,0:T(8,128)(2,1)S(1)}, u32[]{:S(2)}, u32[]{:S(2)}) collective-permute-start(bf16[256,1536]{1,0:T(8,128)(2,1)S(1)} %pad_maximum_fusion.11), channel_id=1, source_target_pairs={{0,4},{2,10},{4,0},{6,14},{8,12},{10,2},{12,8},{14,6},{16,20},{18,... | collective-permute-start | bytes 2359304 | tf_op jit(solution)/shard_map/ppermute | solution.py:315
  285.3 18.8 %collective-permute-start.61 = (bf16[1024,1024]{1,0:T(8,128)(2,1)S(1)}, bf16[1024,1024]{1,0:T(8,128)(2,1)S(1)}, u32[]{:S(2)}, u32[]{:S(2)}) collective-permute-start(bf16[1024,1024]{1,0:T(8,128)(2,1)S(1)} %pad_maximum_fusion.2.mine_ref), channel_id=1, source_target_pairs={{0,2},{2,0},{4,6},{6,4},{8,10},{10,8},{12,14},{14,12},{16,18},{18,... | collective-permute-start | bytes 6291464 | tf_op jit(solution)/shard_map/ppermute | solution.py:312
  293.8 14.9 %collective-permute-start.54 = (bf16[512,2048]{1,0:T(8,128)(2,1)S(1)}, bf16[512,2048]{1,0:T(8,128)(2,1)S(1)}, u32[]{:S(2)}, u32[]{:S(2)}) collective-permute-start(bf16[512,2048]{1,0:T(8,128)(2,1)S(1)} %pad_maximum_fusion.1.mine_ref), channel_id=1, source_target_pairs={{0,2},{2,0},{4,6},{6,4},{8,10},{10,8},{12,14},{14,12},{16,18},{18,... | collective-permute-start | bytes 6291464 | tf_op jit(solution)/shard_map/ppermute | solution.py:312
  (71 other events, 469.7 us)

commit v2 on v1

--- a/solution.py
+++ b/solution.py
@@ -99,7 +99,7 @@
                 outs.append(dot(probs.astype(BF16), values))
             context_ref[first : first + span, :] = jnp.concatenate(outs, axis=1).astype(BF16)
     copies[3].start()
-    result = dot(context_ref[...], out_ref[...])
+    result = dot(context_ref[...], out_ref[...]).astype(BF16)
     for i in range(blocks):
         partials[i][...] = result[i * rows : (i + 1) * rows]
     for copy in copies:
@@ -163,7 +163,7 @@
     return pltpu.CompilerParams(vmem_limit_bytes=min(used + spare * MEBI, 60 * MEBI))
 
 
-def take_columns(weight, index, block, repeats, grant=4):
+def take_columns(weight, index, block, repeats, grant=4, late=False):
     depth, width = weight.shape
     each = width // repeats
     if block % 128:
@@ -175,14 +175,15 @@
             axis=1,
         )
 
-    def kernel(at_ref, in_ref, out_ref, sems):
+    def kernel(at_ref, in_ref, out_ref, *scratch):
+        held, sems = (scratch[0] if late else out_ref), scratch[-1]
         copies = []
         for t in range(repeats):
             start = pl.multiple_of(t * each + at_ref[0] * block, 128)
             copies.append(
                 pltpu.make_async_copy(
                     in_ref.at[:, pl.ds(start, block)],
-                    out_ref.at[:, t * block : (t + 1) * block],
+                    held.at[:, t * block : (t + 1) * block],
                     sems.at[t],
                 )
             )
@@ -190,15 +191,43 @@
             copy.start()
         for copy in copies:
             copy.wait()
-
+        if late:
+            copy = pltpu.make_async_copy(held, out_ref, sems.at[repeats])
+            copy.start()
+            copy.wait()
+
+    shape = (depth, repeats * block)
+    scratch_shapes = [pltpu.VMEM(shape, weight.dtype)] if late else []
     return pl.pallas_call(
         kernel,
         in_specs=[SCALARS, pl.BlockSpec(memory_space=pltpu.HBM)],
-        out_specs=whole(1)[0],
-        out_shape=jax.ShapeDtypeStruct((depth, repeats * block), weight.dtype),
-        scratch_shapes=[pltpu.SemaphoreType.DMA((repeats,))],
+        out_specs=pl.BlockSpec(memory_space=pltpu.HBM) if late else whole(1)[0],
+        out_shape=pltpu.HBM(shape, weight.dtype) if late else jax.ShapeDtypeStruct(shape, weight.dtype),
+        scratch_shapes=scratch_shapes + [pltpu.SemaphoreType.DMA((repeats + 1,))],
         compiler_params=pltpu.CompilerParams(vmem_limit_bytes=grant * MEBI),
         name="take_columns",
+    )(index.reshape(1).astype(jnp.int32), pltpu.with_memory_space_constraint(weight, pltpu.HBM))
+
+
+def take_rows(weight, index, block):
+    width = weight.shape[1]
+    tall = min(block, 256)
+    steps = block // tall
+
+    def kernel(at_ref, in_ref, out_ref):
+        out_ref[...] = in_ref[...]
+
+    return pl.pallas_call(
+        kernel,
+        grid_spec=pltpu.PrefetchScalarGridSpec(
+            num_scalar_prefetch=1,
+            grid=(steps,),
+            in_specs=[pl.BlockSpec((tall, width), lambda i, at: (at[0] * steps + i, 0))],
+            out_specs=pl.BlockSpec((tall, width), lambda i, at: (i, 0)),
+        ),
+        out_shape=pltpu.HBM((block, width), weight.dtype),
+        compiler_params=pltpu.CompilerParams(vmem_limit_bytes=4 * MEBI),
+        name="take_rows",
     )(index.reshape(1).astype(jnp.int32), pltpu.with_memory_space_constraint(weight, pltpu.HBM))
 
 
@@ -368,16 +397,17 @@
             total = None
             for k in offsets:
                 other = sibling(blocks[2 * k + 1])
-                came = turn((blocks[2 * k] + other).astype(BF16), -k).astype(F32)
+                both = blocks[2 * k].astype(F32) + other.astype(F32)
+                came = turn(both.astype(BF16), -k).astype(F32)
                 total = came if total is None else total + came
-            near = blocks[0] + sibling(blocks[1])
+            near = blocks[0].astype(F32) + sibling(blocks[1]).astype(F32)
             return near if total is None else near + total
 
         def qkv_for(shard, grant=4):
             return take_columns(qkv_weight, shard * CORES + core_at, att_block, 3, grant)
 
         def up_for(shard):
-            return take_columns(up_weight, shard * CORES + core_at, ff_block, 1)
+            return take_columns(up_weight, shard * CORES + core_at, ff_block, 1, late=True)
 
         qkv_send = [qkv_for((shard_at + k) % num_shard, 60) for k in offsets]
         qkv_rel = [turn(item, k) for item, k in zip(qkv_send, offsets)]
@@ -414,7 +444,7 @@
         value_mine = lax.dynamic_slice(value_bias, (core_at * att_block,), (att_block,))
         qkv_bias = jnp.concatenate([query_mine, jnp.zeros_like(query_mine), value_mine]).astype(F32)
         out_mine = lax.dynamic_slice(out_weight, (core_at * att_block, 0), (att_block, width))
-        down_mine = lax.dynamic_slice(down_weight, (core_at * ff_block, 0), (ff_block, width))
+        down_mine = take_rows(down_weight, core_at, ff_block)
         up_bias_mine = lax.dynamic_slice(up_bias, (core_at * ff_block,), (ff_block,)).astype(F32)
 
         all_rows = parts * rows
@@ -428,7 +458,7 @@
             pltpu.HBM((width, 3 * att_block), BF16),
             pltpu.HBM((all_rows, 3 * att_block), BF16),
             pltpu.HBM((all_rows, att_block), BF16),
-        ] + [jax.ShapeDtypeStruct((rows, width), F32)] * parts
+        ] + [jax.ShapeDtypeStruct((rows, width), BF16)] * parts
         tok_all, qkv_mine, qkv_rows, context, *partials = pl.pallas_call(
             lambda *refs: attend_kernel(plan, *refs),
             in_specs=[SCALARS] + whole(2 * parts + num_shard + 2),
@@ -446,8 +476,10 @@
         up_mine = jnp.concatenate(in_order(up_rel, shard_at), axis=0)
         pre_act = dot(hid_all, up_mine) + up_bias_mine
         activ = erf_gelu(pre_act).astype(BF16)
-        slope = lax.optimization_barrier(gelu_slope(lax.optimization_barrier((pre_act, activ))[0]))
-        resid2 = hidden1 + scatter_rows(split(dot(activ, down_mine))) + down_bias_full
+        slope = lax.optimization_barrier(
+            gelu_slope(lax.optimization_barrier((pre_act, activ))[0]).astype(BF16)
+        )
+        resid2 = hidden1 + scatter_rows(split(dot(activ, down_mine).astype(BF16))) + down_bias_full
         layer_f32, normed2, inv_std2 = norm_rows(resid2, gain2, shift2)
         layer_out = layer_f32.astype(BF16)
 
@@ -458,11 +490,11 @@
         grad_down_bias = jnp.sum(grad_resid2, axis=0)
         mlp_all = stack(*gather_rows(grad_resid2.astype(BF16)))
         sum_down = dot_rows(activ, mlp_all).astype(BF16)
-        grad_pre = dot_cols(mlp_all, down_mine) * slope
+        grad_pre = dot_cols(mlp_all, down_mine) * slope.astype(F32)
         grad_pre_half = grad_pre.astype(BF16)
         grad_up_bias = jnp.sum(grad_pre, axis=0)
         sum_up = dot_rows(hid_all, grad_pre_half).astype(BF16)
-        grad_hidden1 = grad_resid2 + scatter_rows(split(dot_cols(grad_pre_half, up_mine)))
+        grad_hidden1 = grad_resid2 + scatter_rows(split(dot_cols(grad_pre_half, up_mine).astype(BF16)))
         grad_gain1 = jnp.sum(grad_hidden1 * normed1, axis=0)
         grad_shift1 = jnp.sum(grad_hidden1, axis=0)
         grad_resid1 = norm_back(grad_hidden1, normed1, inv_std1, gain1)
@@ -489,7 +521,7 @@
         sum_out = dot_rows(context, attn_all).astype(BF16)
         grad_query_bias, grad_value_bias = bias_sums[0], bias_sums[1]
         sum_qkv = dot_rows(tok_all, grad_qkv).astype(BF16)
-        input_sum = scatter_rows(split(dot_cols(grad_qkv, qkv_mine)))
+        input_sum = scatter_rows(split(dot_cols(grad_qkv, qkv_mine).astype(BF16)))
         input_grad = (grad_resid1 + input_sum).astype(BF16)
 
         def side_at(route, stage):

time: 314 us -> 301 us (0.959)
  waiting for transfers between devices: 163 us -> 125 us
  starting transfers between devices: 70.2 us -> 96.4 us
  Pallas kernels: 33 us -> 38.9 us
  local copies, waits for them, and re-layouts: 11.5 us -> 7.42 us
    ppermute x24, waiting for transfers between devices: 95.4 us -> 62.4 us  [step_flip(): lax.ppermute(value, 'rep', [(i, i ^ route[i % CORES][stage]) for i in ran...]
    ppermute x24, starting transfers between devices: 27.9 us -> 49.2 us  [step_flip(): lax.ppermute(value, 'rep', [(i, i ^ route[i % CORES][stage]) for i in ran...]
    ppermute x14, waiting for transfers between devices: 64.5 us -> 55.3 us  [turn(): return lax.ppermute(value, 'shard', pairs)]
    unnamed x94 -> x88, local copies, waits for them, and re-layouts: 7.75 us -> 1.79 us
    pallas_call x0 -> x1, Pallas kernels: none -> 3.79 us  [take_rows(): pl.pallas_call(kernel, grid_spec=pltpu.PrefetchScalarGridSpec(num_scalar_...]
    ppermute x24, waiting for transfers between devices: 3.36 us -> 6.98 us  [flip(): return lax.ppermute(value, 'rep', [(i, i ^ bit) for i in range(num_rep)])]
    ppermute x24, starting transfers between devices: 18.7 us -> 22 us  [flip(): return lax.ppermute(value, 'rep', [(i, i ^ bit) for i in range(num_rep)])]
  transfers between devices with their start and end apart: 62 -> 62, of which waited for: 26 -> 24; matrix products, arithmetic and copies ran while one was open for 9% -> 10% of each run, Pallas kernels for 6% -> 8%
where the time goes in v2:
time: 301 us; the launch traced here: 300 us
  waiting for transfers between devices  125 us (42%)
  starting transfers between devices  96.4 us (32%)
  Pallas kernels  38.9 us (13%)
  other arithmetic  16.2 us (5%)
  matrix products  13.4 us (4%)
  local copies, waits for them, and re-layouts  7.42 us (2%)
    ppermute x24, waiting for transfers between devices, step_flip(): lax.ppermute(value, 'rep', [(i, i ^ route[i % CORES][stage]) for i in ran...  62.4 us
    ppermute x14, waiting for transfers between devices, turn(): return lax.ppermute(value, 'shard', pairs)  55.3 us
    ppermute x24, starting transfers between devices, step_flip(): lax.ppermute(value, 'rep', [(i, i ^ route[i % CORES][stage]) for i in ran...  49.2 us
    ppermute x14, starting transfers between devices, turn(): return lax.ppermute(value, 'shard', pairs)  25.2 us
    ppermute x24, starting transfers between devices, flip(): return lax.ppermute(value, 'rep', [(i, i ^ bit) for i in range(num_rep)])  22 us
    pallas_call x2, Pallas kernels, merge_columns(): pl.pallas_call(kernel, grid_spec=pltpu.PrefetchScalarGridSpec(num_scalar_...  8.52 us
    pallas_call x4, Pallas kernels, take_columns(): pl.pallas_call(kernel, in_specs=[SCALARS, pl.BlockSpec(memory_space=pltpu...  7.76 us
    pallas_call x1, Pallas kernels, on_device(): pl.pallas_call(lambda *refs: attend_kernel(plan, *refs), in_specs=[SCALAR...  7.2 us
  transfers between devices with their start and end apart: 62, of which 24 were waited for; matrix products, arithmetic and copies ran while one was open for 10% of the time, Pallas kernels for 8%

profile of v2, /device:TPU:0, one launch (start us, length us, event | category | flops | bytes accessed | tf_op | source)
XLA Modules:
  0.0 299.7 jit_solution(12480564462797298072)
XLA Ops:
  10.7 18.8 %collective-permute-done.1.refs_3_ = bf16[128,1024]{1,0:T(8,128)(2,1)S(1)} collective-permute-done((bf16[128,1024]{1,0:T(8,128)(2,1)S(1)}, bf16[128,1024]{1,0:T(8,128)(2,1)S(1)}, u32[]{:S(2)}, u32[]{:S(2)}) %collective-permute-start.1) | collective-permute-done | bytes 262176 | tf_op jit(solution)/shard_map/ppermute | solution.py:353
  33.7 7.2 %attend.1 = (bf16[512,1024]{1,0:T(8,128)(2,1)}, bf16[1024,768]{1,0:T(8,128)(2,1)}, bf16[512,768]{1,0:T(8,128)(2,1)}, bf16[512,256]{1,0:T(8,128)(2,1)}, bf16[128,...) custom-call(s32[2]{0:T(128)S(1)} %and_select_fusion.refs_0_, ...), custom_call_target="tpu_custom_call" | custom-call | tf_op jit(solution)/shard_map/attend/pallas_call | solution.py:462
  46.1 6.0 %collective-permute-done.9 = bf16[128,1024]{1,0:T(8,128)(2,1)S(1)} collective-permute-done((bf16[128,1024]{1,0:T(8,128)(2,1)S(1)}, bf16[128,1024]{1,0:T(8,128)(2,1)S(1)}, u32[]{:S(2)}, u32[]{:S(2)}) %collective-permute-start.9) | collective-permute-done | bytes 262176 | tf_op jit(solution)/shard_map/ppermute | solution.py:353
  52.5 10.0 %collective-permute-done.13 = bf16[256,1024]{1,0:T(8,128)(2,1)S(1)} collective-permute-done((bf16[256,1024]{1,0:T(8,128)(2,1)S(1)}, bf16[256,1024]{1,0:T(8,128)(2,1)S(1)}, u32[]{:S(2)}, u32[]{:S(2)}) %collective-permute-start.13) | collective-permute-done | bytes 524320 | tf_op jit(solution)/shard_map/ppermute | solution.py:353
  68.2 3.8 %take_rows.1 = bf16[1024,1024]{1,0:T(8,128)(2,1)} custom-call(s32[1]{0:T(128)} %bitcast.5.at_ref, bf16[2048,1024]{1,0:T(8,128)(2,1)} %in_ref.9), custom_call_target="tpu_custom_call" | custom-call | tf_op jit(solution)/shard_map/take_rows/pallas_call | solution.py:220
  82.9 6.6 %collective-permute-done.17 = bf16[128,1024]{1,0:T(8,128)(2,1)S(1)} collective-permute-done((bf16[128,1024]{1,0:T(8,128)(2,1)S(1)}, bf16[128,1024]{1,0:T(8,128)(2,1)S(1)}, u32[]{:S(2)}, u32[]{:S(2)}) %collective-permute-start.17) | collective-permute-done | bytes 262176 | tf_op jit(solution)/shard_map/ppermute | solution.py:353
  93.2 5.8 %collective-permute-done.19 = bf16[128,1024]{1,0:T(8,128)(2,1)S(1)} collective-permute-done((bf16[128,1024]{1,0:T(8,128)(2,1)S(1)}, bf16[128,1024]{1,0:T(8,128)(2,1)S(1)}, u32[]{:S(2)}, u32[]{:S(2)}) %collective-permute-start.19) | collective-permute-done | bytes 262176 | tf_op jit(solution)/shard_map/ppermute | solution.py:353
  121.8 3.6 %collective-permute-done.25.refs_2_ = bf16[128,1024]{1,0:T(8,128)(2,1)S(1)} collective-permute-done((bf16[128,1024]{1,0:T(8,128)(2,1)S(1)}, bf16[128,1024]{1,0:T(8,128)(2,1)S(1)}, u32[]{:S(2)}, u32[]{:S(2)}) %collective-permute-start.25) | collective-permute-done | bytes 262176 | tf_op jit(solution)/shard_map/ppermute | solution.py:353
  128.0 5.7 %attend_back.1 = (bf16[512,1024]{1,0:T(8,128)(2,1)S(1)}, bf16[512,768]{1,0:T(8,128)(2,1)S(1)}, f32[2,256]{1,0:T(2,128)S(1)}) custom-call(bf16[128,1024]{1,0:T(8,128)(2,1)S(1)} %convert_element_type.297.refs_0_, bf16[128,1024]{1,0:T(8,128)(2,1)S(1)} %collective-permute-done.24.refs_1_, bf16[128,1024]{1,0:T(8,128)(2,1)S(1)} %collective-permute-done.25.refs_2_, ...), custom_call_target="tpu_custom_call" | custom-call | tf_op jit(solution)/shard_map/attend_back/pallas_call | solution.py:512
  141.0 7.6 %collective-permute-done.40 = bf16[128,1152]{1,0:T(8,128)(2,1)S(1)} collective-permute-done((bf16[128,1152]{1,0:T(8,128)(2,1)S(1)}, bf16[128,1152]{1,0:T(8,128)(2,1)S(1)}, u32[]{:S(2)}, u32[]{:S(2)}) %collective-permute-start.40) | collective-permute-done | bytes 294944 | tf_op jit(solution)/shard_map/ppermute | solution.py:344
  152.3 7.0 %collective-permute-done.41 = bf16[64,1152]{1,0:T(8,128)(2,1)S(1)} collective-permute-done((bf16[64,1152]{1,0:T(8,128)(2,1)S(1)}, bf16[64,1152]{1,0:T(8,128)(2,1)S(1)}, u32[]{:S(2)}, u32[]{:S(2)}) %collective-permute-start.41) | collective-permute-done | bytes 147488 | tf_op jit(solution)/shard_map/ppermute | solution.py:344
  163.7 4.7 %collective-permute-done.42 = bf16[32,1152]{1,0:T(8,128)(2,1)S(1)} collective-permute-done((bf16[32,1152]{1,0:T(8,128)(2,1)S(1)}, bf16[32,1152]{1,0:T(8,128)(2,1)S(1)}, u32[]{:S(2)}, u32[]{:S(2)}) %collective-permute-start.42) | collective-permute-done | bytes 73760 | tf_op jit(solution)/shard_map/ppermute | solution.py:344
  169.3 3.4 %collective-permute-start.43 = (bf16[32,1152]{1,0:T(8,128)(2,1)S(1)}, bf16[32,1152]{1,0:T(8,128)(2,1)S(1)}, u32[]{:S(2)}, u32[]{:S(2)}) collective-permute-start(bf16[32,1152]{1,0:T(8,128)(2,1)S(1)} %add_convert_fusion.17), channel_id=1, source_target_pairs={{0,16},{2,18},{4,20},{6,22},{8,24},{10,26},{12,28},{14,30},{16,0},... | collective-permute-start | bytes 221192 | tf_op jit(solution)/shard_map/ppermute | solution.py:344
  178.0 5.7 %collective-permute-start.44 = (bf16[64,1152]{1,0:T(8,128)(2,1)S(1)}, bf16[64,1152]{1,0:T(8,128)(2,1)S(1)}, u32[]{:S(2)}, u32[]{:S(2)}) collective-permute-start(bf16[64,1152]{1,0:T(8,128)(2,1)S(1)} %pad_maximum_fusion.23), channel_id=1, source_target_pairs={{0,8},{2,6},{4,12},{6,2},{8,0},{10,14},{12,4},{14,10},{16,24},{18,... | collective-permute-start | bytes 442376 | tf_op jit(solution)/shard_map/ppermute | solution.py:344
  184.6 3.4 %collective-permute-done.44 = bf16[64,1152]{1,0:T(8,128)(2,1)S(1)} collective-permute-done((bf16[64,1152]{1,0:T(8,128)(2,1)S(1)}, bf16[64,1152]{1,0:T(8,128)(2,1)S(1)}, u32[]{:S(2)}, u32[]{:S(2)}) %collective-permute-start.44) | collective-permute-done | bytes 147488 | tf_op jit(solution)/shard_map/ppermute | solution.py:344
  193.4 4.7 %collective-permute-done.57 = bf16[128,1024]{1,0:T(8,128)(2,1)S(1)} collective-permute-done((bf16[128,1024]{1,0:T(8,128)(2,1)S(1)}, bf16[128,1024]{1,0:T(8,128)(2,1)S(1)}, u32[]{:S(2)}, u32[]{:S(2)}) %collective-permute-start.57) | collective-permute-done | bytes 262176 | tf_op jit(solution)/shard_map/ppermute | solution.py:344
  202.1 7.8 %collective-permute-start.46 = (bf16[256,1152]{1,0:T(8,128)(2,1)S(1)}, bf16[256,1152]{1,0:T(8,128)(2,1)S(1)}, u32[]{:S(2)}, u32[]{:S(2)}) collective-permute-start(bf16[256,1152]{1,0:T(8,128)(2,1)S(1)} %pad_maximum_fusion.12), channel_id=1, source_target_pairs={{0,2},{2,0},{4,6},{6,4},{8,10},{10,8},{12,14},{14,12},{16,18},{18,... | collective-permute-start | bytes 1769480 | tf_op jit(solution)/shard_map/ppermute | solution.py:341
  212.1 7.2 %collective-permute-start.32 = (bf16[2,64,768]{2,1,0:T(8,128)(2,1)S(1)}, bf16[2,64,768]{2,1,0:T(8,128)(2,1)S(1)}, u32[]{:S(2)}, u32[]{:S(2)}) collective-permute-start(bf16[2,64,768]{2,1,0:T(8,128)(2,1)S(1)} %constant_dynamic-slice_fusion.10), channel_id=1, source_target_pairs={{0,16},{2,18},{4,20},{6,22},{8,24},{10,26},{12,28},{14,30},{16,0},... | collective-permute-start | bytes 589832 | tf_op jit(solution)/shard_map/ppermute | solution.py:344
  219.4 8.3 %collective-permute-done.32 = bf16[2,64,768]{2,1,0:T(8,128)(2,1)S(1)} collective-permute-done((bf16[2,64,768]{2,1,0:T(8,128)(2,1)S(1)}, bf16[2,64,768]{2,1,0:T(8,128)(2,1)S(1)}, u32[]{:S(2)}, u32[]{:S(2)}) %collective-permute-start.32) | collective-permute-done | bytes 196640 | tf_op jit(solution)/shard_map/ppermute | solution.py:344
  227.8 6.6 %collective-permute-start.33 = (bf16[64,768]{1,0:T(8,128)(2,1)S(1)}, bf16[64,768]{1,0:T(8,128)(2,1)S(1)}, u32[]{:S(2)}, u32[]{:S(2)}) collective-permute-start(bf16[64,768]{1,0:T(8,128)(2,1)S(1)} %dynamic-slice_bitcast_fusion.1), channel_id=1, source_target_pairs={{0,1},{1,0},{2,3},{3,2},{4,5},{5,4},{6,7},{7,6},{8,9},{9,8},{10,11... | collective-permute-start | bytes 294920 | tf_op jit(solution)/shard_map/ppermute | solution.py:353
  234.6 3.5 %collective-permute-done.33 = bf16[64,768]{1,0:T(8,128)(2,1)S(1)} collective-permute-done((bf16[64,768]{1,0:T(8,128)(2,1)S(1)}, bf16[64,768]{1,0:T(8,128)(2,1)S(1)}, u32[]{:S(2)}, u32[]{:S(2)}) %collective-permute-start.33) | collective-permute-done | bytes 98336 | tf_op jit(solution)/shard_map/ppermute | solution.py:353
  238.5 3.7 %collective-permute-start.60 = (bf16[512,1024]{1,0:T(8,128)(2,1)S(1)}, bf16[512,1024]{1,0:T(8,128)(2,1)S(1)}, u32[]{:S(2)}, u32[]{:S(2)}) collective-permute-start(bf16[512,1024]{1,0:T(8,128)(2,1)S(1)} %pad_maximum_fusion.10), channel_id=1, source_target_pairs={{0,4},{2,10},{4,0},{6,14},{8,12},{10,2},{12,8},{14,6},{16,20},{18,... | collective-permute-start | bytes 3145736 | tf_op jit(solution)/shard_map/ppermute | solution.py:344
  242.2 8.1 %collective-permute-done.34 = bf16[64,1536]{1,0:T(8,128)(2,1)S(1)} collective-permute-done((bf16[64,1536]{1,0:T(8,128)(2,1)S(1)}, bf16[64,1536]{1,0:T(8,128)(2,1)S(1)}, u32[]{:S(2)}, u32[]{:S(2)}) %collective-permute-start.34) | collective-permute-done | bytes 196640 | tf_op jit(solution)/shard_map/ppermute | solution.py:344
  250.8 3.9 %collective-permute-start.53 = (bf16[256,2048]{1,0:T(8,128)(2,1)S(1)}, bf16[256,2048]{1,0:T(8,128)(2,1)S(1)}, u32[]{:S(2)}, u32[]{:S(2)}) collective-permute-start(bf16[256,2048]{1,0:T(8,128)(2,1)S(1)} %pad_maximum_fusion.9), channel_id=1, source_target_pairs={{0,4},{2,10},{4,0},{6,14},{8,12},{10,2},{12,8},{14,6},{16,20},{18,... | collective-permute-start | bytes 3145736 | tf_op jit(solution)/shard_map/ppermute | solution.py:344
  254.7 7.7 %collective-permute-done.35 = bf16[128,1536]{1,0:T(8,128)(2,1)S(1)} collective-permute-done((bf16[128,1536]{1,0:T(8,128)(2,1)S(1)}, bf16[128,1536]{1,0:T(8,128)(2,1)S(1)}, u32[]{:S(2)}, u32[]{:S(2)}) %collective-permute-start.35) | collective-permute-done | bytes 393248 | tf_op jit(solution)/shard_map/ppermute | solution.py:344
  266.0 4.7 %collective-permute-done.53 = bf16[256,2048]{1,0:T(8,128)(2,1)S(1)} collective-permute-done((bf16[256,2048]{1,0:T(8,128)(2,1)S(1)}, bf16[256,2048]{1,0:T(8,128)(2,1)S(1)}, u32[]{:S(2)}, u32[]{:S(2)}) %collective-permute-start.53) | collective-permute-done | bytes 1048608 | tf_op jit(solution)/shard_map/ppermute | solution.py:344
  271.6 4.0 %collective-permute-start.54 = (bf16[512,2048]{1,0:T(8,128)(2,1)S(1)}, bf16[512,2048]{1,0:T(8,128)(2,1)S(1)}, u32[]{:S(2)}, u32[]{:S(2)}) collective-permute-start(bf16[512,2048]{1,0:T(8,128)(2,1)S(1)} %pad_maximum_fusion.1.mine_ref), channel_id=1, source_target_pairs={{0,2},{2,0},{4,6},{6,4},{8,10},{10,8},{12,14},{14,12},{16,18},{18,... | collective-permute-start | bytes 6291464 | tf_op jit(solution)/shard_map/ppermute | solution.py:341
  275.6 3.6 %collective-permute-done.36 = bf16[256,1536]{1,0:T(8,128)(2,1)S(1)} collective-permute-done((bf16[256,1536]{1,0:T(8,128)(2,1)S(1)}, bf16[256,1536]{1,0:T(8,128)(2,1)S(1)}, u32[]{:S(2)}, u32[]{:S(2)}) %collective-permute-start.36) | collective-permute-done | bytes 786464 | tf_op jit(solution)/shard_map/ppermute | solution.py:344
  279.6 3.8 %collective-permute-start.37 = (bf16[512,1536]{1,0:T(8,128)(2,1)S(1)}, bf16[512,1536]{1,0:T(8,128)(2,1)S(1)}, u32[]{:S(2)}, u32[]{:S(2)}) collective-permute-start(bf16[512,1536]{1,0:T(8,128)(2,1)S(1)} %pad_maximum_fusion.3.mine_ref), channel_id=1, source_target_pairs={{0,2},{2,0},{4,6},{6,4},{8,10},{10,8},{12,14},{14,12},{16,18},{18,... | collective-permute-start | bytes 4718600 | tf_op jit(solution)/shard_map/ppermute | solution.py:341
  286.7 4.0 %merge_columns.2 = f32[512,3072]{1,0:T(8,128)} custom-call(s32[1]{0:T(128)} %bitcast.5.at_ref, bf16[512,1536]{1,0:T(8,128)(2,1)S(1)} %pad_maximum_fusion.3.mine_ref, bf16[512,1536]{1,0:T(8,128)(2,1)S(1)} %collective-permute-done.37.other_ref), custom_call_target="tpu_custom_call" | custom-call | tf_op jit(solution)/shard_map/merge_columns/pallas_call | solution.py:310
  290.7 4.5 %merge_rows.3 = f32[2048,1024]{1,0:T(8,128)} custom-call(s32[1]{0:T(128)} %bitcast.5.at_ref, bf16[1024,1024]{1,0:T(8,128)(2,1)S(1)} %pad_maximum_fusion.2.mine_ref, bf16[1024,1024]{1,0:T(8,128)(2,1)S(1)} %collective-permute-done.61.other_ref), custom_call_target="tpu_custom_call" | custom-call | tf_op jit(solution)/shard_map/merge_rows/pallas_call | solution.py:248
  295.2 4.5 %merge_columns.3 = f32[512,4096]{1,0:T(8,128)} custom-call(s32[1]{0:T(128)} %bitcast.5.at_ref, bf16[512,2048]{1,0:T(8,128)(2,1)S(1)} %pad_maximum_fusion.1.mine_ref, bf16[512,2048]{1,0:T(8,128)(2,1)S(1)} %collective-permute-done.54.other_ref), custom_call_target="tpu_custom_call" | custom-call | tf_op jit(solution)/shard_map/merge_columns/pallas_call | solution.py:310
  (325 shorter events, 107.1 us)
Async XLA Ops:
  3.0 30.7 %collective-permute-start.6 = (bf16[512,768]{1,0:T(8,128)(2,1)}, bf16[512,768]{1,0:T(8,128)(2,1)S(1)}, u32[]{:S(2)}, u32[]{:S(2)}) collective-permute-start(bf16[512,768]{1,0:T(8,128)(2,1)} %take_columns.6), channel_id=1, source_target_pairs={{0,1},{1,0},{2,3},{3,2},{4,5},{5,4},{6,7},{7,6},{8,9},{9,8},{10,11... | collective-permute-start | bytes 2359304 | tf_op jit(solution)/shard_map/ppermute | solution.py:353
  6.0 23.5 %collective-permute-start.1 = (bf16[128,1024]{1,0:T(8,128)(2,1)S(1)}, bf16[128,1024]{1,0:T(8,128)(2,1)S(1)}, u32[]{:S(2)}, u32[]{:S(2)}) collective-permute-start(bf16[128,1024]{1,0:T(8,128)(2,1)S(1)} %copy-done.2), channel_id=1, source_target_pairs={{0,1},{1,0},{2,3},{3,2},{4,5},{5,4},{6,7},{7,6},{8,9},{9,8},{10,11... | collective-permute-start | bytes 786440 | tf_op jit(solution)/shard_map/ppermute | solution.py:353
  8.2 21.6 %collective-permute-start.4 = (bf16[7,512]{1,0:T(8,128)(2,1)S(1)}, bf16[7,512]{1,0:T(8,128)(2,1)S(1)}, u32[]{:S(2)}, u32[]{:S(2)}) collective-permute-start(bf16[7,512]{1,0:T(8,128)(2,1)S(1)} %reshape.187.refs_5_.refs_4_), channel_id=1, source_target_pairs={{0,1},{1,0},{2,3},{3,2},{4,5},{5,4},{6,7},{7,6},{8,9},{9,8},{10,11... | collective-permute-start | bytes 21512 | tf_op jit(solution)/shard_map/ppermute | solution.py:353
  10.2 23.5 %collective-permute-start.3 = (bf16[7,512]{1,0:T(8,128)(2,1)S(1)}, bf16[7,512]{1,0:T(8,128)(2,1)S(1)}, u32[]{:S(2)}, u32[]{:S(2)}) collective-permute-start(bf16[7,512]{1,0:T(8,128)(2,1)S(1)} %reshape.187.refs_5_.refs_4_), channel_id=1, source_target_pairs={{0,2},{2,0},{4,6},{6,4},{8,10},{10,8},{12,14},{14,12},{16,18},{18,... | collective-permute-start | bytes 21512 | tf_op jit(solution)/shard_map/ppermute | solution.py:341
  10.2 23.6 %collective-permute-start = (bf16[128,1024]{1,0:T(8,128)(2,1)S(1)}, bf16[128,1024]{1,0:T(8,128)(2,1)S(1)}, u32[]{:S(2)}, u32[]{:S(2)}) collective-permute-start(bf16[128,1024]{1,0:T(8,128)(2,1)S(1)} %copy-done.2), channel_id=1, source_target_pairs={{0,2},{2,0},{4,6},{6,4},{8,10},{10,8},{12,14},{14,12},{16,18},{18,... | collective-permute-start | bytes 786440 | tf_op jit(solution)/shard_map/ppermute | solution.py:341
  45.8 16.7 %collective-permute-start.13 = (bf16[256,1024]{1,0:T(8,128)(2,1)S(1)}, bf16[256,1024]{1,0:T(8,128)(2,1)S(1)}, u32[]{:S(2)}, u32[]{:S(2)}) collective-permute-start(bf16[256,1024]{1,0:T(8,128)(2,1)S(1)} %constant_dynamic-slice_fusion.13), channel_id=1, source_target_pairs={{0,1},{1,0},{2,3},{3,2},{4,5},{5,4},{6,7},{7,6},{8,9},{9,8},{10,11... | collective-permute-start | bytes 1572872 | tf_op jit(solution)/shard_map/ppermute | solution.py:353
  62.5 13.1 %collective-permute-start.14 = (bf16[256,1024]{1,0:T(8,128)(2,1)S(1)}, bf16[256,1024]{1,0:T(8,128)(2,1)S(1)}, u32[]{:S(2)}, u32[]{:S(2)}) collective-permute-start(bf16[256,1024]{1,0:T(8,128)(2,1)S(1)} %collective-permute-done.13), channel_id=1, source_target_pairs={{0,4},{2,6},{4,0},{6,2},{8,12},{10,14},{12,8},{14,10},{16,20},{18,... | collective-permute-start | bytes 1572872 | tf_op jit(solution)/shard_map/ppermute | solution.py:341
  111.7 26.1 %collective-permute-start.47 = (bf16[2,256,1024]{2,1,0:T(8,128)(2,1)}, bf16[2,256,1024]{2,1,0:T(8,128)(2,1)}, u32[]{:S(2)}, u32[]{:S(2)}) collective-permute-start(bf16[2,256,1024]{2,1,0:T(8,128)(2,1)} %constant_dynamic-slice_fusion.5), channel_id=1, source_target_pairs={{0,4},{2,10},{4,0},{6,14},{8,12},{10,2},{12,8},{14,6},{16,20},{18,... | collective-permute-start | bytes 3145736 | tf_op jit(solution)/shard_map/ppermute | solution.py:344
  126.4 23.9 %collective-permute-start.55 = (bf16[512,1024]{1,0:T(8,128)(2,1)}, bf16[512,1024]{1,0:T(8,128)(2,1)}, u32[]{:S(2)}, u32[]{:S(2)}) collective-permute-start(bf16[512,1024]{1,0:T(8,128)(2,1)} %constant_dynamic-slice_fusion.2), channel_id=1, source_target_pairs={{0,4},{2,10},{4,0},{6,14},{8,12},{10,2},{12,8},{14,6},{16,20},{18,... | collective-permute-start | bytes 3145736 | tf_op jit(solution)/shard_map/ppermute | solution.py:344
  134.2 14.3 %collective-permute-start.40 = (bf16[128,1152]{1,0:T(8,128)(2,1)S(1)}, bf16[128,1152]{1,0:T(8,128)(2,1)S(1)}, u32[]{:S(2)}, u32[]{:S(2)}) collective-permute-start(bf16[128,1152]{1,0:T(8,128)(2,1)S(1)} %fusion.16), channel_id=1, source_target_pairs={{0,4},{2,10},{4,0},{6,14},{8,12},{10,2},{12,8},{14,6},{16,20},{18,... | collective-permute-start | bytes 884744 | tf_op jit(solution)/shard_map/ppermute | solution.py:344
  135.9 42.2 %collective-permute-start.27 = (bf16[128,1024]{1,0:T(8,128)(2,1)S(1)}, bf16[128,1024]{1,0:T(8,128)(2,1)S(1)}, u32[]{:S(2)}, u32[]{:S(2)}) collective-permute-start(bf16[128,1024]{1,0:T(8,128)(2,1)S(1)} %get-tuple-element.76), channel_id=1, source_target_pairs={{0,2},{2,0},{4,6},{6,4},{8,10},{10,8},{12,14},{14,12},{16,18},{18,... | collective-permute-start | bytes 786440 | tf_op jit(solution)/shard_map/ppermute | solution.py:341
  135.9 25.0 %collective-permute-start.28 = (bf16[128,1024]{1,0:T(8,128)(2,1)S(1)}, bf16[128,1024]{1,0:T(8,128)(2,1)S(1)}, u32[]{:S(2)}, u32[]{:S(2)}) collective-permute-start(bf16[128,1024]{1,0:T(8,128)(2,1)S(1)} %get-tuple-element.77), channel_id=1, source_target_pairs={{0,2},{2,0},{4,6},{6,4},{8,10},{10,8},{12,14},{14,12},{16,18},{18,... | collective-permute-start | bytes 786440 | tf_op jit(solution)/shard_map/ppermute | solution.py:341
  137.8 51.6 %collective-permute-start.30 = (bf16[2,256,768]{2,1,0:T(8,128)(2,1)S(1)}, bf16[2,256,768]{2,1,0:T(8,128)(2,1)S(1)}, u32[]{:S(2)}, u32[]{:S(2)}) collective-permute-start(bf16[2,256,768]{2,1,0:T(8,128)(2,1)S(1)} %constant_dynamic-slice_fusion.12), channel_id=1, source_target_pairs={{0,4},{2,6},{4,0},{6,2},{8,12},{10,14},{12,8},{14,10},{16,20},{18,... | collective-permute-start | bytes 2359304 | tf_op jit(solution)/shard_map/ppermute | solution.py:344
  148.5 20.7 %collective-permute-start.48 = (bf16[2,128,1024]{2,1,0:T(8,128)(2,1)S(1)}, bf16[2,128,1024]{2,1,0:T(8,128)(2,1)S(1)}, u32[]{:S(2)}, u32[]{:S(2)}) collective-permute-start(bf16[2,128,1024]{2,1,0:T(8,128)(2,1)S(1)} %constant_dynamic-slice_fusion.4), channel_id=1, source_target_pairs={{0,8},{2,6},{4,12},{6,2},{8,0},{10,14},{12,4},{14,10},{16,24},{18,... | collective-permute-start | bytes 1572872 | tf_op jit(solution)/shard_map/ppermute | solution.py:344
  159.3 13.7 %collective-permute-start.56 = (bf16[256,1024]{1,0:T(8,128)(2,1)S(1)}, bf16[256,1024]{1,0:T(8,128)(2,1)S(1)}, u32[]{:S(2)}, u32[]{:S(2)}) collective-permute-start(bf16[256,1024]{1,0:T(8,128)(2,1)S(1)} %constant_dynamic-slice_fusion.1), channel_id=1, source_target_pairs={{0,8},{2,6},{4,12},{6,2},{8,0},{10,14},{12,4},{14,10},{16,24},{18,... | collective-permute-start | bytes 1572872 | tf_op jit(solution)/shard_map/ppermute | solution.py:344
  168.4 15.4 %collective-permute-start.29 = (bf16[128,1024]{1,0:T(8,128)(2,1)S(1)}, bf16[128,1024]{1,0:T(8,128)(2,1)S(1)}, u32[]{:S(2)}, u32[]{:S(2)}) collective-permute-start(bf16[128,1024]{1,0:T(8,128)(2,1)S(1)} %add_convert_fusion.10), channel_id=1, source_target_pairs={{0,1},{1,0},{2,3},{3,2},{4,5},{5,4},{6,7},{7,6},{8,9},{9,8},{10,11... | collective-permute-start | bytes 786440 | tf_op jit(solution)/shard_map/ppermute | solution.py:353
  173.0 19.2 %collective-permute-start.49 = (bf16[2,64,1024]{2,1,0:T(8,128)(2,1)S(1)}, bf16[2,64,1024]{2,1,0:T(8,128)(2,1)S(1)}, u32[]{:S(2)}, u32[]{:S(2)}) collective-permute-start(bf16[2,64,1024]{2,1,0:T(8,128)(2,1)S(1)} %constant_dynamic-slice_fusion.3), channel_id=1, source_target_pairs={{0,16},{2,18},{4,20},{6,22},{8,24},{10,26},{12,28},{14,30},{16,0},... | collective-permute-start | bytes 786440 | tf_op jit(solution)/shard_map/ppermute | solution.py:344
  176.0 22.2 %collective-permute-start.57 = (bf16[128,1024]{1,0:T(8,128)(2,1)S(1)}, bf16[128,1024]{1,0:T(8,128)(2,1)S(1)}, u32[]{:S(2)}, u32[]{:S(2)}) collective-permute-start(bf16[128,1024]{1,0:T(8,128)(2,1)S(1)} %constant_dynamic-slice_fusion), channel_id=1, source_target_pairs={{0,16},{2,18},{4,20},{6,22},{8,24},{10,26},{12,28},{14,30},{16,0},... | collective-permute-start | bytes 786440 | tf_op jit(solution)/shard_map/ppermute | solution.py:344
  188.1 13.2 %collective-permute-start.45 = (bf16[128,1152]{1,0:T(8,128)(2,1)S(1)}, bf16[128,1152]{1,0:T(8,128)(2,1)S(1)}, u32[]{:S(2)}, u32[]{:S(2)}) collective-permute-start(bf16[128,1152]{1,0:T(8,128)(2,1)S(1)} %pad_maximum_fusion.16), channel_id=1, source_target_pairs={{0,4},{2,10},{4,0},{6,14},{8,12},{10,2},{12,8},{14,6},{16,20},{18,... | collective-permute-start | bytes 884744 | tf_op jit(solution)/shard_map/ppermute | solution.py:344
  189.7 22.3 %collective-permute-start.31 = (bf16[2,128,768]{2,1,0:T(8,128)(2,1)S(1)}, bf16[2,128,768]{2,1,0:T(8,128)(2,1)S(1)}, u32[]{:S(2)}, u32[]{:S(2)}) collective-permute-start(bf16[2,128,768]{2,1,0:T(8,128)(2,1)S(1)} %constant_dynamic-slice_fusion.11), channel_id=1, source_target_pairs={{0,8},{2,10},{4,12},{6,14},{8,0},{10,2},{12,4},{14,6},{16,24},{18,... | collective-permute-start | bytes 1179656 | tf_op jit(solution)/shard_map/ppermute | solution.py:344
  198.4 21.0 %collective-permute-start.51 = (bf16[64,2048]{1,0:T(8,128)(2,1)S(1)}, bf16[64,2048]{1,0:T(8,128)(2,1)S(1)}, u32[]{:S(2)}, u32[]{:S(2)}) collective-permute-start(bf16[64,2048]{1,0:T(8,128)(2,1)S(1)} %pad_maximum_fusion.17), channel_id=1, source_target_pairs={{0,16},{2,18},{4,20},{6,22},{8,24},{10,26},{12,28},{14,30},{16,0},... | collective-permute-start | bytes 786440 | tf_op jit(solution)/shard_map/ppermute | solution.py:344
  202.1 81.3 %collective-permute-start.46 = (bf16[256,1152]{1,0:T(8,128)(2,1)S(1)}, bf16[256,1152]{1,0:T(8,128)(2,1)S(1)}, u32[]{:S(2)}, u32[]{:S(2)}) collective-permute-start(bf16[256,1152]{1,0:T(8,128)(2,1)S(1)} %pad_maximum_fusion.12), channel_id=1, source_target_pairs={{0,2},{2,0},{4,6},{6,4},{8,10},{10,8},{12,14},{14,12},{16,18},{18,... | collective-permute-start | bytes 1769480 | tf_op jit(solution)/shard_map/ppermute | solution.py:341
  210.1 28.1 %collective-permute-start.59 = (bf16[256,1024]{1,0:T(8,128)(2,1)S(1)}, bf16[256,1024]{1,0:T(8,128)(2,1)S(1)}, u32[]{:S(2)}, u32[]{:S(2)}) collective-permute-start(bf16[256,1024]{1,0:T(8,128)(2,1)S(1)} %pad_maximum_fusion.14), channel_id=1, source_target_pairs={{0,8},{2,6},{4,12},{6,2},{8,0},{10,14},{12,4},{14,10},{16,24},{18,... | collective-permute-start | bytes 1572872 | tf_op jit(solution)/shard_map/ppermute | solution.py:344
  212.1 15.6 %collective-permute-start.32 = (bf16[2,64,768]{2,1,0:T(8,128)(2,1)S(1)}, bf16[2,64,768]{2,1,0:T(8,128)(2,1)S(1)}, u32[]{:S(2)}, u32[]{:S(2)}) collective-permute-start(bf16[2,64,768]{2,1,0:T(8,128)(2,1)S(1)} %constant_dynamic-slice_fusion.10), channel_id=1, source_target_pairs={{0,16},{2,18},{4,20},{6,22},{8,24},{10,26},{12,28},{14,30},{16,0},... | collective-permute-start | bytes 589832 | tf_op jit(solution)/shard_map/ppermute | solution.py:344
  234.5 16.0 %collective-permute-start.52 = (bf16[128,2048]{1,0:T(8,128)(2,1)S(1)}, bf16[128,2048]{1,0:T(8,128)(2,1)S(1)}, u32[]{:S(2)}, u32[]{:S(2)}) collective-permute-start(bf16[128,2048]{1,0:T(8,128)(2,1)S(1)} %pad_maximum_fusion.13), channel_id=1, source_target_pairs={{0,8},{2,6},{4,12},{6,2},{8,0},{10,14},{12,4},{14,10},{16,24},{18,... | collective-permute-start | bytes 1572872 | tf_op jit(solution)/shard_map/ppermute | solution.py:344
  238.1 12.2 %collective-permute-start.34 = (bf16[64,1536]{1,0:T(8,128)(2,1)S(1)}, bf16[64,1536]{1,0:T(8,128)(2,1)S(1)}, u32[]{:S(2)}, u32[]{:S(2)}) collective-permute-start(bf16[64,1536]{1,0:T(8,128)(2,1)S(1)} %pad_maximum_fusion.18), channel_id=1, source_target_pairs={{0,16},{2,18},{4,20},{6,22},{8,24},{10,26},{12,28},{14,30},{16,0},... | collective-permute-start | bytes 589832 | tf_op jit(solution)/shard_map/ppermute | solution.py:344
  238.5 26.7 %collective-permute-start.60 = (bf16[512,1024]{1,0:T(8,128)(2,1)S(1)}, bf16[512,1024]{1,0:T(8,128)(2,1)S(1)}, u32[]{:S(2)}, u32[]{:S(2)}) collective-permute-start(bf16[512,1024]{1,0:T(8,128)(2,1)S(1)} %pad_maximum_fusion.10), channel_id=1, source_target_pairs={{0,4},{2,10},{4,0},{6,14},{8,12},{10,2},{12,8},{14,6},{16,20},{18,... | collective-permute-start | bytes 3145736 | tf_op jit(solution)/shard_map/ppermute | solution.py:344
  250.4 12.1 %collective-permute-start.35 = (bf16[128,1536]{1,0:T(8,128)(2,1)S(1)}, bf16[128,1536]{1,0:T(8,128)(2,1)S(1)}, u32[]{:S(2)}, u32[]{:S(2)}) collective-permute-start(bf16[128,1536]{1,0:T(8,128)(2,1)S(1)} %pad_maximum_fusion.15), channel_id=1, source_target_pairs={{0,8},{2,6},{4,12},{6,2},{8,0},{10,14},{12,4},{14,10},{16,24},{18,... | collective-permute-start | bytes 1179656 | tf_op jit(solution)/shard_map/ppermute | solution.py:344
  250.8 19.9 %collective-permute-start.53 = (bf16[256,2048]{1,0:T(8,128)(2,1)S(1)}, bf16[256,2048]{1,0:T(8,128)(2,1)S(1)}, u32[]{:S(2)}, u32[]{:S(2)}) collective-permute-start(bf16[256,2048]{1,0:T(8,128)(2,1)S(1)} %pad_maximum_fusion.9), channel_id=1, source_target_pairs={{0,4},{2,10},{4,0},{6,14},{8,12},{10,2},{12,8},{14,6},{16,20},{18,... | collective-permute-start | bytes 3145736 | tf_op jit(solution)/shard_map/ppermute | solution.py:344
  262.6 16.6 %collective-permute-start.36 = (bf16[256,1536]{1,0:T(8,128)(2,1)S(1)}, bf16[256,1536]{1,0:T(8,128)(2,1)S(1)}, u32[]{:S(2)}, u32[]{:S(2)}) collective-permute-start(bf16[256,1536]{1,0:T(8,128)(2,1)S(1)} %pad_maximum_fusion.11), channel_id=1, source_target_pairs={{0,4},{2,10},{4,0},{6,14},{8,12},{10,2},{12,8},{14,6},{16,20},{18,... | collective-permute-start | bytes 2359304 | tf_op jit(solution)/shard_map/ppermute | solution.py:344
  265.9 24.8 %collective-permute-start.61 = (bf16[1024,1024]{1,0:T(8,128)(2,1)S(1)}, bf16[1024,1024]{1,0:T(8,128)(2,1)S(1)}, u32[]{:S(2)}, u32[]{:S(2)}) collective-permute-start(bf16[1024,1024]{1,0:T(8,128)(2,1)S(1)} %pad_maximum_fusion.2.mine_ref), channel_id=1, source_target_pairs={{0,2},{2,0},{4,6},{6,4},{8,10},{10,8},{12,14},{14,12},{16,18},{18,... | collective-permute-start | bytes 6291464 | tf_op jit(solution)/shard_map/ppermute | solution.py:341
  271.6 23.6 %collective-permute-start.54 = (bf16[512,2048]{1,0:T(8,128)(2,1)S(1)}, bf16[512,2048]{1,0:T(8,128)(2,1)S(1)}, u32[]{:S(2)}, u32[]{:S(2)}) collective-permute-start(bf16[512,2048]{1,0:T(8,128)(2,1)S(1)} %pad_maximum_fusion.1.mine_ref), channel_id=1, source_target_pairs={{0,2},{2,0},{4,6},{6,4},{8,10},{10,8},{12,14},{14,12},{16,18},{18,... | collective-permute-start | bytes 6291464 | tf_op jit(solution)/shard_map/ppermute | solution.py:341
  (68 other events, 467.3 us)

commit v3 on v2

--- a/solution.py
+++ b/solution.py
@@ -421,14 +421,16 @@
         qkv_rel = [qkv_for(shard_at)] + qkv_rel
         up_send = [up_for((shard_at + k) % num_shard) for k in offsets]
         up_own = up_for(shard_at)
+        up_side = (rep_at // bits[0]) % 2
+        low = up_side == 0
+        up_send = [
+            lax.dynamic_slice_in_dim(item, up_side * (depth // 2), depth // 2, 0) for item in up_send
+        ]
         up_send, qkv_rel = lax.optimization_barrier((up_send, qkv_rel))
-        up_side = (rep_at // bits[0]) % 2
         up_rel = [up_own]
-        for item, k in zip(up_send, offsets):
-            half = lax.dynamic_slice_in_dim(item, up_side * (depth // 2), depth // 2, 0)
+        for half, k in zip(up_send, offsets):
             half = turn(half, k)
             other = flip(half, bits[0])
-            low = up_side == 0
             up_rel.append(
                 jnp.concatenate([jnp.where(low, half, other), jnp.where(low, other, half)], axis=0)
             )

time: 301 us -> 300 us (level)
  no operation moved by 1% of the time
where the time goes in v3:
time: 300 us; the launch traced here: 299 us
  waiting for transfers between devices  123 us (41%)
  starting transfers between devices  96.4 us (32%)
  Pallas kernels  38.8 us (13%)
  other arithmetic  16.2 us (5%)
  matrix products  13.4 us (4%)
  local copies, waits for them, and re-layouts  8.22 us (3%)
    ppermute x24, waiting for transfers between devices, step_flip(): lax.ppermute(value, 'rep', [(i, i ^ route[i % CORES][stage]) for i in ran...  62.3 us
    ppermute x14, waiting for transfers between devices, turn(): return lax.ppermute(value, 'shard', pairs)  54.1 us
    ppermute x24, starting transfers between devices, step_flip(): lax.ppermute(value, 'rep', [(i, i ^ route[i % CORES][stage]) for i in ran...  49.4 us
    ppermute x14, starting transfers between devices, turn(): return lax.ppermute(value, 'shard', pairs)  25.1 us
    ppermute x24, starting transfers between devices, flip(): return lax.ppermute(value, 'rep', [(i, i ^ bit) for i in range(num_rep)])  21.9 us
    pallas_call x2, Pallas kernels, merge_columns(): pl.pallas_call(kernel, grid_spec=pltpu.PrefetchScalarGridSpec(num_scalar_...  8.52 us
    pallas_call x4, Pallas kernels, take_columns(): pl.pallas_call(kernel, in_specs=[SCALARS, pl.BlockSpec(memory_space=pltpu...  7.68 us
    pallas_call x1, Pallas kernels, on_device(): pl.pallas_call(lambda *refs: attend_kernel(plan, *refs), in_specs=[SCALAR...  7.19 us
  transfers between devices with their start and end apart: 62, of which 24 were waited for; matrix products, arithmetic and copies ran while one was open for 10% of the time, Pallas kernels for 8%

profile of v3, /device:TPU:0, one launch (start us, length us, event | category | flops | bytes accessed | tf_op | source)
XLA Modules:
  0.0 299.2 jit_solution(3084131562485425241)
XLA Ops:
  12.9 16.5 %collective-permute-done.1.refs_3_ = bf16[128,1024]{1,0:T(8,128)(2,1)S(1)} collective-permute-done((bf16[128,1024]{1,0:T(8,128)(2,1)S(1)}, bf16[128,1024]{1,0:T(8,128)(2,1)S(1)}, u32[]{:S(2)}, u32[]{:S(2)}) %collective-permute-start.1) | collective-permute-done | bytes 262176 | tf_op jit(solution)/shard_map/ppermute | solution.py:353
  33.3 7.2 %attend.1 = (bf16[512,1024]{1,0:T(8,128)(2,1)}, bf16[1024,768]{1,0:T(8,128)(2,1)}, bf16[512,768]{1,0:T(8,128)(2,1)}, bf16[512,256]{1,0:T(8,128)(2,1)}, bf16[128,...) custom-call(s32[2]{0:T(128)S(1)} %and_select_fusion.refs_0_, ...), custom_call_target="tpu_custom_call" | custom-call | tf_op jit(solution)/shard_map/attend/pallas_call | solution.py:464
  44.5 7.0 %collective-permute-done.9 = bf16[128,1024]{1,0:T(8,128)(2,1)S(1)} collective-permute-done((bf16[128,1024]{1,0:T(8,128)(2,1)S(1)}, bf16[128,1024]{1,0:T(8,128)(2,1)S(1)}, u32[]{:S(2)}, u32[]{:S(2)}) %collective-permute-start.9) | collective-permute-done | bytes 262176 | tf_op jit(solution)/shard_map/ppermute | solution.py:353
  52.0 10.0 %collective-permute-done.13 = bf16[256,1024]{1,0:T(8,128)(2,1)S(1)} collective-permute-done((bf16[256,1024]{1,0:T(8,128)(2,1)}, bf16[256,1024]{1,0:T(8,128)(2,1)S(1)}, u32[]{:S(2)}, u32[]{:S(2)}) %collective-permute-start.13) | collective-permute-done | bytes 524320 | tf_op jit(solution)/shard_map/ppermute | solution.py:353
  67.7 3.8 %take_rows.1 = bf16[1024,1024]{1,0:T(8,128)(2,1)} custom-call(s32[1]{0:T(128)} %bitcast.5.at_ref, bf16[2048,1024]{1,0:T(8,128)(2,1)} %in_ref.9), custom_call_target="tpu_custom_call" | custom-call | tf_op jit(solution)/shard_map/take_rows/pallas_call | solution.py:220
  82.4 6.6 %collective-permute-done.17 = bf16[128,1024]{1,0:T(8,128)(2,1)S(1)} collective-permute-done((bf16[128,1024]{1,0:T(8,128)(2,1)S(1)}, bf16[128,1024]{1,0:T(8,128)(2,1)S(1)}, u32[]{:S(2)}, u32[]{:S(2)}) %collective-permute-start.17) | collective-permute-done | bytes 262176 | tf_op jit(solution)/shard_map/ppermute | solution.py:353
  92.7 5.8 %collective-permute-done.19 = bf16[128,1024]{1,0:T(8,128)(2,1)S(1)} collective-permute-done((bf16[128,1024]{1,0:T(8,128)(2,1)S(1)}, bf16[128,1024]{1,0:T(8,128)(2,1)S(1)}, u32[]{:S(2)}, u32[]{:S(2)}) %collective-permute-start.19) | collective-permute-done | bytes 262176 | tf_op jit(solution)/shard_map/ppermute | solution.py:353
  121.3 3.6 %collective-permute-done.25.refs_2_ = bf16[128,1024]{1,0:T(8,128)(2,1)S(1)} collective-permute-done((bf16[128,1024]{1,0:T(8,128)(2,1)S(1)}, bf16[128,1024]{1,0:T(8,128)(2,1)S(1)}, u32[]{:S(2)}, u32[]{:S(2)}) %collective-permute-start.25) | collective-permute-done | bytes 262176 | tf_op jit(solution)/shard_map/ppermute | solution.py:353
  127.5 5.7 %attend_back.1 = (bf16[512,1024]{1,0:T(8,128)(2,1)S(1)}, bf16[512,768]{1,0:T(8,128)(2,1)S(1)}, f32[2,256]{1,0:T(2,128)S(1)}) custom-call(bf16[128,1024]{1,0:T(8,128)(2,1)S(1)} %convert_element_type.297.refs_0_, bf16[128,1024]{1,0:T(8,128)(2,1)S(1)} %collective-permute-done.24.refs_1_, bf16[128,1024]{1,0:T(8,128)(2,1)S(1)} %collective-permute-done.25.refs_2_, ...), custom_call_target="tpu_custom_call" | custom-call | tf_op jit(solution)/shard_map/attend_back/pallas_call | solution.py:514
  140.5 7.6 %collective-permute-done.40 = bf16[128,1152]{1,0:T(8,128)(2,1)S(1)} collective-permute-done((bf16[128,1152]{1,0:T(8,128)(2,1)S(1)}, bf16[128,1152]{1,0:T(8,128)(2,1)S(1)}, u32[]{:S(2)}, u32[]{:S(2)}) %collective-permute-start.40) | collective-permute-done | bytes 294944 | tf_op jit(solution)/shard_map/ppermute | solution.py:344
  151.8 7.0 %collective-permute-done.41 = bf16[64,1152]{1,0:T(8,128)(2,1)S(1)} collective-permute-done((bf16[64,1152]{1,0:T(8,128)(2,1)S(1)}, bf16[64,1152]{1,0:T(8,128)(2,1)S(1)}, u32[]{:S(2)}, u32[]{:S(2)}) %collective-permute-start.41) | collective-permute-done | bytes 147488 | tf_op jit(solution)/shard_map/ppermute | solution.py:344
  163.2 4.7 %collective-permute-done.42 = bf16[32,1152]{1,0:T(8,128)(2,1)S(1)} collective-permute-done((bf16[32,1152]{1,0:T(8,128)(2,1)S(1)}, bf16[32,1152]{1,0:T(8,128)(2,1)S(1)}, u32[]{:S(2)}, u32[]{:S(2)}) %collective-permute-start.42) | collective-permute-done | bytes 73760 | tf_op jit(solution)/shard_map/ppermute | solution.py:344
  168.8 3.4 %collective-permute-start.43 = (bf16[32,1152]{1,0:T(8,128)(2,1)S(1)}, bf16[32,1152]{1,0:T(8,128)(2,1)S(1)}, u32[]{:S(2)}, u32[]{:S(2)}) collective-permute-start(bf16[32,1152]{1,0:T(8,128)(2,1)S(1)} %add_convert_fusion.17), channel_id=1, source_target_pairs={{0,16},{2,18},{4,20},{6,22},{8,24},{10,26},{12,28},{14,30},{16,0},... | collective-permute-start | bytes 221192 | tf_op jit(solution)/shard_map/ppermute | solution.py:344
  177.6 5.7 %collective-permute-start.44 = (bf16[64,1152]{1,0:T(8,128)(2,1)S(1)}, bf16[64,1152]{1,0:T(8,128)(2,1)S(1)}, u32[]{:S(2)}, u32[]{:S(2)}) collective-permute-start(bf16[64,1152]{1,0:T(8,128)(2,1)S(1)} %pad_maximum_fusion.23), channel_id=1, source_target_pairs={{0,8},{2,6},{4,12},{6,2},{8,0},{10,14},{12,4},{14,10},{16,24},{18,... | collective-permute-start | bytes 442376 | tf_op jit(solution)/shard_map/ppermute | solution.py:344
  184.1 3.4 %collective-permute-done.44 = bf16[64,1152]{1,0:T(8,128)(2,1)S(1)} collective-permute-done((bf16[64,1152]{1,0:T(8,128)(2,1)S(1)}, bf16[64,1152]{1,0:T(8,128)(2,1)S(1)}, u32[]{:S(2)}, u32[]{:S(2)}) %collective-permute-start.44) | collective-permute-done | bytes 147488 | tf_op jit(solution)/shard_map/ppermute | solution.py:344
  192.9 4.8 %collective-permute-done.57 = bf16[128,1024]{1,0:T(8,128)(2,1)S(1)} collective-permute-done((bf16[128,1024]{1,0:T(8,128)(2,1)S(1)}, bf16[128,1024]{1,0:T(8,128)(2,1)S(1)}, u32[]{:S(2)}, u32[]{:S(2)}) %collective-permute-start.57) | collective-permute-done | bytes 262176 | tf_op jit(solution)/shard_map/ppermute | solution.py:344
  201.7 7.8 %collective-permute-start.46 = (bf16[256,1152]{1,0:T(8,128)(2,1)S(1)}, bf16[256,1152]{1,0:T(8,128)(2,1)S(1)}, u32[]{:S(2)}, u32[]{:S(2)}) collective-permute-start(bf16[256,1152]{1,0:T(8,128)(2,1)S(1)} %pad_maximum_fusion.12), channel_id=1, source_target_pairs={{0,2},{2,0},{4,6},{6,4},{8,10},{10,8},{12,14},{14,12},{16,18},{18,... | collective-permute-start | bytes 1769480 | tf_op jit(solution)/shard_map/ppermute | solution.py:341
  211.6 7.3 %collective-permute-start.32 = (bf16[2,64,768]{2,1,0:T(8,128)(2,1)S(1)}, bf16[2,64,768]{2,1,0:T(8,128)(2,1)S(1)}, u32[]{:S(2)}, u32[]{:S(2)}) collective-permute-start(bf16[2,64,768]{2,1,0:T(8,128)(2,1)S(1)} %constant_dynamic-slice_fusion.10), channel_id=1, source_target_pairs={{0,16},{2,18},{4,20},{6,22},{8,24},{10,26},{12,28},{14,30},{16,0},... | collective-permute-start | bytes 589832 | tf_op jit(solution)/shard_map/ppermute | solution.py:344
  219.0 8.2 %collective-permute-done.32 = bf16[2,64,768]{2,1,0:T(8,128)(2,1)S(1)} collective-permute-done((bf16[2,64,768]{2,1,0:T(8,128)(2,1)S(1)}, bf16[2,64,768]{2,1,0:T(8,128)(2,1)S(1)}, u32[]{:S(2)}, u32[]{:S(2)}) %collective-permute-start.32) | collective-permute-done | bytes 196640 | tf_op jit(solution)/shard_map/ppermute | solution.py:344
  227.3 6.6 %collective-permute-start.33 = (bf16[64,768]{1,0:T(8,128)(2,1)S(1)}, bf16[64,768]{1,0:T(8,128)(2,1)S(1)}, u32[]{:S(2)}, u32[]{:S(2)}) collective-permute-start(bf16[64,768]{1,0:T(8,128)(2,1)S(1)} %dynamic-slice_bitcast_fusion.1), channel_id=1, source_target_pairs={{0,1},{1,0},{2,3},{3,2},{4,5},{5,4},{6,7},{7,6},{8,9},{9,8},{10,11... | collective-permute-start | bytes 294920 | tf_op jit(solution)/shard_map/ppermute | solution.py:353
  234.0 3.5 %collective-permute-done.33 = bf16[64,768]{1,0:T(8,128)(2,1)S(1)} collective-permute-done((bf16[64,768]{1,0:T(8,128)(2,1)S(1)}, bf16[64,768]{1,0:T(8,128)(2,1)S(1)}, u32[]{:S(2)}, u32[]{:S(2)}) %collective-permute-start.33) | collective-permute-done | bytes 98336 | tf_op jit(solution)/shard_map/ppermute | solution.py:353
  238.0 3.7 %collective-permute-start.60 = (bf16[512,1024]{1,0:T(8,128)(2,1)S(1)}, bf16[512,1024]{1,0:T(8,128)(2,1)S(1)}, u32[]{:S(2)}, u32[]{:S(2)}) collective-permute-start(bf16[512,1024]{1,0:T(8,128)(2,1)S(1)} %pad_maximum_fusion.10), channel_id=1, source_target_pairs={{0,4},{2,10},{4,0},{6,14},{8,12},{10,2},{12,8},{14,6},{16,20},{18,... | collective-permute-start | bytes 3145736 | tf_op jit(solution)/shard_map/ppermute | solution.py:344
  241.7 8.0 %collective-permute-done.34 = bf16[64,1536]{1,0:T(8,128)(2,1)S(1)} collective-permute-done((bf16[64,1536]{1,0:T(8,128)(2,1)S(1)}, bf16[64,1536]{1,0:T(8,128)(2,1)S(1)}, u32[]{:S(2)}, u32[]{:S(2)}) %collective-permute-start.34) | collective-permute-done | bytes 196640 | tf_op jit(solution)/shard_map/ppermute | solution.py:344
  250.3 4.0 %collective-permute-start.53 = (bf16[256,2048]{1,0:T(8,128)(2,1)S(1)}, bf16[256,2048]{1,0:T(8,128)(2,1)S(1)}, u32[]{:S(2)}, u32[]{:S(2)}) collective-permute-start(bf16[256,2048]{1,0:T(8,128)(2,1)S(1)} %pad_maximum_fusion.9), channel_id=1, source_target_pairs={{0,4},{2,10},{4,0},{6,14},{8,12},{10,2},{12,8},{14,6},{16,20},{18,... | collective-permute-start | bytes 3145736 | tf_op jit(solution)/shard_map/ppermute | solution.py:344
  254.2 7.7 %collective-permute-done.35 = bf16[128,1536]{1,0:T(8,128)(2,1)S(1)} collective-permute-done((bf16[128,1536]{1,0:T(8,128)(2,1)S(1)}, bf16[128,1536]{1,0:T(8,128)(2,1)S(1)}, u32[]{:S(2)}, u32[]{:S(2)}) %collective-permute-start.35) | collective-permute-done | bytes 393248 | tf_op jit(solution)/shard_map/ppermute | solution.py:344
  265.5 4.7 %collective-permute-done.53 = bf16[256,2048]{1,0:T(8,128)(2,1)S(1)} collective-permute-done((bf16[256,2048]{1,0:T(8,128)(2,1)S(1)}, bf16[256,2048]{1,0:T(8,128)(2,1)S(1)}, u32[]{:S(2)}, u32[]{:S(2)}) %collective-permute-start.53) | collective-permute-done | bytes 1048608 | tf_op jit(solution)/shard_map/ppermute | solution.py:344
  271.1 4.0 %collective-permute-start.54 = (bf16[512,2048]{1,0:T(8,128)(2,1)S(1)}, bf16[512,2048]{1,0:T(8,128)(2,1)S(1)}, u32[]{:S(2)}, u32[]{:S(2)}) collective-permute-start(bf16[512,2048]{1,0:T(8,128)(2,1)S(1)} %pad_maximum_fusion.1.mine_ref), channel_id=1, source_target_pairs={{0,2},{2,0},{4,6},{6,4},{8,10},{10,8},{12,14},{14,12},{16,18},{18,... | collective-permute-start | bytes 6291464 | tf_op jit(solution)/shard_map/ppermute | solution.py:341
  275.1 3.6 %collective-permute-done.36 = bf16[256,1536]{1,0:T(8,128)(2,1)S(1)} collective-permute-done((bf16[256,1536]{1,0:T(8,128)(2,1)S(1)}, bf16[256,1536]{1,0:T(8,128)(2,1)S(1)}, u32[]{:S(2)}, u32[]{:S(2)}) %collective-permute-start.36) | collective-permute-done | bytes 786464 | tf_op jit(solution)/shard_map/ppermute | solution.py:344
  279.1 3.7 %collective-permute-start.37 = (bf16[512,1536]{1,0:T(8,128)(2,1)S(1)}, bf16[512,1536]{1,0:T(8,128)(2,1)S(1)}, u32[]{:S(2)}, u32[]{:S(2)}) collective-permute-start(bf16[512,1536]{1,0:T(8,128)(2,1)S(1)} %pad_maximum_fusion.3.mine_ref), channel_id=1, source_target_pairs={{0,2},{2,0},{4,6},{6,4},{8,10},{10,8},{12,14},{14,12},{16,18},{18,... | collective-permute-start | bytes 4718600 | tf_op jit(solution)/shard_map/ppermute | solution.py:341
  286.2 4.0 %merge_columns.2 = f32[512,3072]{1,0:T(8,128)} custom-call(s32[1]{0:T(128)} %bitcast.5.at_ref, bf16[512,1536]{1,0:T(8,128)(2,1)S(1)} %pad_maximum_fusion.3.mine_ref, bf16[512,1536]{1,0:T(8,128)(2,1)S(1)} %collective-permute-done.37.other_ref), custom_call_target="tpu_custom_call" | custom-call | tf_op jit(solution)/shard_map/merge_columns/pallas_call | solution.py:310
  290.2 4.5 %merge_rows.3 = f32[2048,1024]{1,0:T(8,128)} custom-call(s32[1]{0:T(128)} %bitcast.5.at_ref, bf16[1024,1024]{1,0:T(8,128)(2,1)S(1)} %pad_maximum_fusion.2.mine_ref, bf16[1024,1024]{1,0:T(8,128)(2,1)S(1)} %collective-permute-done.61.other_ref), custom_call_target="tpu_custom_call" | custom-call | tf_op jit(solution)/shard_map/merge_rows/pallas_call | solution.py:248
  294.7 4.5 %merge_columns.3 = f32[512,4096]{1,0:T(8,128)} custom-call(s32[1]{0:T(128)} %bitcast.5.at_ref, bf16[512,2048]{1,0:T(8,128)(2,1)S(1)} %pad_maximum_fusion.1.mine_ref, bf16[512,2048]{1,0:T(8,128)(2,1)S(1)} %collective-permute-done.54.other_ref), custom_call_target="tpu_custom_call" | custom-call | tf_op jit(solution)/shard_map/merge_columns/pallas_call | solution.py:310
  (325 shorter events, 107.9 us)
Async XLA Ops:
  2.9 30.3 %collective-permute-start.6 = (bf16[512,768]{1,0:T(8,128)(2,1)}, bf16[512,768]{1,0:T(8,128)(2,1)S(1)}, u32[]{:S(2)}, u32[]{:S(2)}) collective-permute-start(bf16[512,768]{1,0:T(8,128)(2,1)} %take_columns.6), channel_id=1, source_target_pairs={{0,1},{1,0},{2,3},{3,2},{4,5},{5,4},{6,7},{7,6},{8,9},{9,8},{10,11... | collective-permute-start | bytes 2359304 | tf_op jit(solution)/shard_map/ppermute | solution.py:353
  5.9 23.5 %collective-permute-start.1 = (bf16[128,1024]{1,0:T(8,128)(2,1)S(1)}, bf16[128,1024]{1,0:T(8,128)(2,1)S(1)}, u32[]{:S(2)}, u32[]{:S(2)}) collective-permute-start(bf16[128,1024]{1,0:T(8,128)(2,1)S(1)} %copy-done.2), channel_id=1, source_target_pairs={{0,1},{1,0},{2,3},{3,2},{4,5},{5,4},{6,7},{7,6},{8,9},{9,8},{10,11... | collective-permute-start | bytes 786440 | tf_op jit(solution)/shard_map/ppermute | solution.py:353
  8.1 23.4 %collective-permute-start.4 = (bf16[7,512]{1,0:T(8,128)(2,1)S(1)}, bf16[7,512]{1,0:T(8,128)(2,1)S(1)}, u32[]{:S(2)}, u32[]{:S(2)}) collective-permute-start(bf16[7,512]{1,0:T(8,128)(2,1)S(1)} %reshape.187.refs_5_.refs_4_), channel_id=1, source_target_pairs={{0,1},{1,0},{2,3},{3,2},{4,5},{5,4},{6,7},{7,6},{8,9},{9,8},{10,11... | collective-permute-start | bytes 21512 | tf_op jit(solution)/shard_map/ppermute | solution.py:353
  10.1 23.1 %collective-permute-start.3 = (bf16[7,512]{1,0:T(8,128)(2,1)S(1)}, bf16[7,512]{1,0:T(8,128)(2,1)S(1)}, u32[]{:S(2)}, u32[]{:S(2)}) collective-permute-start(bf16[7,512]{1,0:T(8,128)(2,1)S(1)} %reshape.187.refs_5_.refs_4_), channel_id=1, source_target_pairs={{0,2},{2,0},{4,6},{6,4},{8,10},{10,8},{12,14},{14,12},{16,18},{18,... | collective-permute-start | bytes 21512 | tf_op jit(solution)/shard_map/ppermute | solution.py:341
  10.1 23.2 %collective-permute-start = (bf16[128,1024]{1,0:T(8,128)(2,1)S(1)}, bf16[128,1024]{1,0:T(8,128)(2,1)S(1)}, u32[]{:S(2)}, u32[]{:S(2)}) collective-permute-start(bf16[128,1024]{1,0:T(8,128)(2,1)S(1)} %copy-done.2), channel_id=1, source_target_pairs={{0,2},{2,0},{4,6},{6,4},{8,10},{10,8},{12,14},{14,12},{16,18},{18,... | collective-permute-start | bytes 786440 | tf_op jit(solution)/shard_map/ppermute | solution.py:341
  44.2 17.8 %collective-permute-start.13 = (bf16[256,1024]{1,0:T(8,128)(2,1)}, bf16[256,1024]{1,0:T(8,128)(2,1)S(1)}, u32[]{:S(2)}, u32[]{:S(2)}) collective-permute-start(bf16[256,1024]{1,0:T(8,128)(2,1)} %constant_dynamic-slice_fusion.14), channel_id=1, source_target_pairs={{0,1},{1,0},{2,3},{3,2},{4,5},{5,4},{6,7},{7,6},{8,9},{9,8},{10,11... | collective-permute-start | bytes 1572872 | tf_op jit(solution)/shard_map/ppermute | solution.py:353
  62.0 13.1 %collective-permute-start.14 = (bf16[256,1024]{1,0:T(8,128)(2,1)S(1)}, bf16[256,1024]{1,0:T(8,128)(2,1)S(1)}, u32[]{:S(2)}, u32[]{:S(2)}) collective-permute-start(bf16[256,1024]{1,0:T(8,128)(2,1)S(1)} %collective-permute-done.13), channel_id=1, source_target_pairs={{0,4},{2,6},{4,0},{6,2},{8,12},{10,14},{12,8},{14,10},{16,20},{18,... | collective-permute-start | bytes 1572872 | tf_op jit(solution)/shard_map/ppermute | solution.py:341
  111.2 26.1 %collective-permute-start.47 = (bf16[2,256,1024]{2,1,0:T(8,128)(2,1)}, bf16[2,256,1024]{2,1,0:T(8,128)(2,1)}, u32[]{:S(2)}, u32[]{:S(2)}) collective-permute-start(bf16[2,256,1024]{2,1,0:T(8,128)(2,1)} %constant_dynamic-slice_fusion.5), channel_id=1, source_target_pairs={{0,4},{2,10},{4,0},{6,14},{8,12},{10,2},{12,8},{14,6},{16,20},{18,... | collective-permute-start | bytes 3145736 | tf_op jit(solution)/shard_map/ppermute | solution.py:344
  125.9 23.9 %collective-permute-start.55 = (bf16[512,1024]{1,0:T(8,128)(2,1)}, bf16[512,1024]{1,0:T(8,128)(2,1)}, u32[]{:S(2)}, u32[]{:S(2)}) collective-permute-start(bf16[512,1024]{1,0:T(8,128)(2,1)} %constant_dynamic-slice_fusion.2), channel_id=1, source_target_pairs={{0,4},{2,10},{4,0},{6,14},{8,12},{10,2},{12,8},{14,6},{16,20},{18,... | collective-permute-start | bytes 3145736 | tf_op jit(solution)/shard_map/ppermute | solution.py:344
  133.7 14.3 %collective-permute-start.40 = (bf16[128,1152]{1,0:T(8,128)(2,1)S(1)}, bf16[128,1152]{1,0:T(8,128)(2,1)S(1)}, u32[]{:S(2)}, u32[]{:S(2)}) collective-permute-start(bf16[128,1152]{1,0:T(8,128)(2,1)S(1)} %fusion.16), channel_id=1, source_target_pairs={{0,4},{2,10},{4,0},{6,14},{8,12},{10,2},{12,8},{14,6},{16,20},{18,... | collective-permute-start | bytes 884744 | tf_op jit(solution)/shard_map/ppermute | solution.py:344
  135.4 42.2 %collective-permute-start.27 = (bf16[128,1024]{1,0:T(8,128)(2,1)S(1)}, bf16[128,1024]{1,0:T(8,128)(2,1)S(1)}, u32[]{:S(2)}, u32[]{:S(2)}) collective-permute-start(bf16[128,1024]{1,0:T(8,128)(2,1)S(1)} %get-tuple-element.76), channel_id=1, source_target_pairs={{0,2},{2,0},{4,6},{6,4},{8,10},{10,8},{12,14},{14,12},{16,18},{18,... | collective-permute-start | bytes 786440 | tf_op jit(solution)/shard_map/ppermute | solution.py:341
  135.4 25.0 %collective-permute-start.28 = (bf16[128,1024]{1,0:T(8,128)(2,1)S(1)}, bf16[128,1024]{1,0:T(8,128)(2,1)S(1)}, u32[]{:S(2)}, u32[]{:S(2)}) collective-permute-start(bf16[128,1024]{1,0:T(8,128)(2,1)S(1)} %get-tuple-element.77), channel_id=1, source_target_pairs={{0,2},{2,0},{4,6},{6,4},{8,10},{10,8},{12,14},{14,12},{16,18},{18,... | collective-permute-start | bytes 786440 | tf_op jit(solution)/shard_map/ppermute | solution.py:341
  137.3 51.6 %collective-permute-start.30 = (bf16[2,256,768]{2,1,0:T(8,128)(2,1)S(1)}, bf16[2,256,768]{2,1,0:T(8,128)(2,1)S(1)}, u32[]{:S(2)}, u32[]{:S(2)}) collective-permute-start(bf16[2,256,768]{2,1,0:T(8,128)(2,1)S(1)} %constant_dynamic-slice_fusion.12), channel_id=1, source_target_pairs={{0,4},{2,6},{4,0},{6,2},{8,12},{10,14},{12,8},{14,10},{16,20},{18,... | collective-permute-start | bytes 2359304 | tf_op jit(solution)/shard_map/ppermute | solution.py:344
  148.0 20.7 %collective-permute-start.48 = (bf16[2,128,1024]{2,1,0:T(8,128)(2,1)S(1)}, bf16[2,128,1024]{2,1,0:T(8,128)(2,1)S(1)}, u32[]{:S(2)}, u32[]{:S(2)}) collective-permute-start(bf16[2,128,1024]{2,1,0:T(8,128)(2,1)S(1)} %constant_dynamic-slice_fusion.4), channel_id=1, source_target_pairs={{0,8},{2,6},{4,12},{6,2},{8,0},{10,14},{12,4},{14,10},{16,24},{18,... | collective-permute-start | bytes 1572872 | tf_op jit(solution)/shard_map/ppermute | solution.py:344
  158.8 13.7 %collective-permute-start.56 = (bf16[256,1024]{1,0:T(8,128)(2,1)S(1)}, bf16[256,1024]{1,0:T(8,128)(2,1)S(1)}, u32[]{:S(2)}, u32[]{:S(2)}) collective-permute-start(bf16[256,1024]{1,0:T(8,128)(2,1)S(1)} %constant_dynamic-slice_fusion.1), channel_id=1, source_target_pairs={{0,8},{2,6},{4,12},{6,2},{8,0},{10,14},{12,4},{14,10},{16,24},{18,... | collective-permute-start | bytes 1572872 | tf_op jit(solution)/shard_map/ppermute | solution.py:344
  167.9 15.4 %collective-permute-start.29 = (bf16[128,1024]{1,0:T(8,128)(2,1)S(1)}, bf16[128,1024]{1,0:T(8,128)(2,1)S(1)}, u32[]{:S(2)}, u32[]{:S(2)}) collective-permute-start(bf16[128,1024]{1,0:T(8,128)(2,1)S(1)} %add_convert_fusion.10), channel_id=1, source_target_pairs={{0,1},{1,0},{2,3},{3,2},{4,5},{5,4},{6,7},{7,6},{8,9},{9,8},{10,11... | collective-permute-start | bytes 786440 | tf_op jit(solution)/shard_map/ppermute | solution.py:353
  172.5 19.2 %collective-permute-start.49 = (bf16[2,64,1024]{2,1,0:T(8,128)(2,1)S(1)}, bf16[2,64,1024]{2,1,0:T(8,128)(2,1)S(1)}, u32[]{:S(2)}, u32[]{:S(2)}) collective-permute-start(bf16[2,64,1024]{2,1,0:T(8,128)(2,1)S(1)} %constant_dynamic-slice_fusion.3), channel_id=1, source_target_pairs={{0,16},{2,18},{4,20},{6,22},{8,24},{10,26},{12,28},{14,30},{16,0},... | collective-permute-start | bytes 786440 | tf_op jit(solution)/shard_map/ppermute | solution.py:344
  175.5 22.2 %collective-permute-start.57 = (bf16[128,1024]{1,0:T(8,128)(2,1)S(1)}, bf16[128,1024]{1,0:T(8,128)(2,1)S(1)}, u32[]{:S(2)}, u32[]{:S(2)}) collective-permute-start(bf16[128,1024]{1,0:T(8,128)(2,1)S(1)} %constant_dynamic-slice_fusion), channel_id=1, source_target_pairs={{0,16},{2,18},{4,20},{6,22},{8,24},{10,26},{12,28},{14,30},{16,0},... | collective-permute-start | bytes 786440 | tf_op jit(solution)/shard_map/ppermute | solution.py:344
  187.6 13.3 %collective-permute-start.45 = (bf16[128,1152]{1,0:T(8,128)(2,1)S(1)}, bf16[128,1152]{1,0:T(8,128)(2,1)S(1)}, u32[]{:S(2)}, u32[]{:S(2)}) collective-permute-start(bf16[128,1152]{1,0:T(8,128)(2,1)S(1)} %pad_maximum_fusion.16), channel_id=1, source_target_pairs={{0,4},{2,10},{4,0},{6,14},{8,12},{10,2},{12,8},{14,6},{16,20},{18,... | collective-permute-start | bytes 884744 | tf_op jit(solution)/shard_map/ppermute | solution.py:344
  189.2 22.3 %collective-permute-start.31 = (bf16[2,128,768]{2,1,0:T(8,128)(2,1)S(1)}, bf16[2,128,768]{2,1,0:T(8,128)(2,1)S(1)}, u32[]{:S(2)}, u32[]{:S(2)}) collective-permute-start(bf16[2,128,768]{2,1,0:T(8,128)(2,1)S(1)} %constant_dynamic-slice_fusion.11), channel_id=1, source_target_pairs={{0,8},{2,10},{4,12},{6,14},{8,0},{10,2},{12,4},{14,6},{16,24},{18,... | collective-permute-start | bytes 1179656 | tf_op jit(solution)/shard_map/ppermute | solution.py:344
  197.9 21.0 %collective-permute-start.51 = (bf16[64,2048]{1,0:T(8,128)(2,1)S(1)}, bf16[64,2048]{1,0:T(8,128)(2,1)S(1)}, u32[]{:S(2)}, u32[]{:S(2)}) collective-permute-start(bf16[64,2048]{1,0:T(8,128)(2,1)S(1)} %pad_maximum_fusion.17), channel_id=1, source_target_pairs={{0,16},{2,18},{4,20},{6,22},{8,24},{10,26},{12,28},{14,30},{16,0},... | collective-permute-start | bytes 786440 | tf_op jit(solution)/shard_map/ppermute | solution.py:344
  201.7 81.2 %collective-permute-start.46 = (bf16[256,1152]{1,0:T(8,128)(2,1)S(1)}, bf16[256,1152]{1,0:T(8,128)(2,1)S(1)}, u32[]{:S(2)}, u32[]{:S(2)}) collective-permute-start(bf16[256,1152]{1,0:T(8,128)(2,1)S(1)} %pad_maximum_fusion.12), channel_id=1, source_target_pairs={{0,2},{2,0},{4,6},{6,4},{8,10},{10,8},{12,14},{14,12},{16,18},{18,... | collective-permute-start | bytes 1769480 | tf_op jit(solution)/shard_map/ppermute | solution.py:341
  209.5 28.1 %collective-permute-start.59 = (bf16[256,1024]{1,0:T(8,128)(2,1)S(1)}, bf16[256,1024]{1,0:T(8,128)(2,1)S(1)}, u32[]{:S(2)}, u32[]{:S(2)}) collective-permute-start(bf16[256,1024]{1,0:T(8,128)(2,1)S(1)} %pad_maximum_fusion.14), channel_id=1, source_target_pairs={{0,8},{2,6},{4,12},{6,2},{8,0},{10,14},{12,4},{14,10},{16,24},{18,... | collective-permute-start | bytes 1572872 | tf_op jit(solution)/shard_map/ppermute | solution.py:344
  211.6 15.6 %collective-permute-start.32 = (bf16[2,64,768]{2,1,0:T(8,128)(2,1)S(1)}, bf16[2,64,768]{2,1,0:T(8,128)(2,1)S(1)}, u32[]{:S(2)}, u32[]{:S(2)}) collective-permute-start(bf16[2,64,768]{2,1,0:T(8,128)(2,1)S(1)} %constant_dynamic-slice_fusion.10), channel_id=1, source_target_pairs={{0,16},{2,18},{4,20},{6,22},{8,24},{10,26},{12,28},{14,30},{16,0},... | collective-permute-start | bytes 589832 | tf_op jit(solution)/shard_map/ppermute | solution.py:344
  234.0 16.0 %collective-permute-start.52 = (bf16[128,2048]{1,0:T(8,128)(2,1)S(1)}, bf16[128,2048]{1,0:T(8,128)(2,1)S(1)}, u32[]{:S(2)}, u32[]{:S(2)}) collective-permute-start(bf16[128,2048]{1,0:T(8,128)(2,1)S(1)} %pad_maximum_fusion.13), channel_id=1, source_target_pairs={{0,8},{2,6},{4,12},{6,2},{8,0},{10,14},{12,4},{14,10},{16,24},{18,... | collective-permute-start | bytes 1572872 | tf_op jit(solution)/shard_map/ppermute | solution.py:344
  237.6 12.2 %collective-permute-start.34 = (bf16[64,1536]{1,0:T(8,128)(2,1)S(1)}, bf16[64,1536]{1,0:T(8,128)(2,1)S(1)}, u32[]{:S(2)}, u32[]{:S(2)}) collective-permute-start(bf16[64,1536]{1,0:T(8,128)(2,1)S(1)} %pad_maximum_fusion.18), channel_id=1, source_target_pairs={{0,16},{2,18},{4,20},{6,22},{8,24},{10,26},{12,28},{14,30},{16,0},... | collective-permute-start | bytes 589832 | tf_op jit(solution)/shard_map/ppermute | solution.py:344
  238.0 26.7 %collective-permute-start.60 = (bf16[512,1024]{1,0:T(8,128)(2,1)S(1)}, bf16[512,1024]{1,0:T(8,128)(2,1)S(1)}, u32[]{:S(2)}, u32[]{:S(2)}) collective-permute-start(bf16[512,1024]{1,0:T(8,128)(2,1)S(1)} %pad_maximum_fusion.10), channel_id=1, source_target_pairs={{0,4},{2,10},{4,0},{6,14},{8,12},{10,2},{12,8},{14,6},{16,20},{18,... | collective-permute-start | bytes 3145736 | tf_op jit(solution)/shard_map/ppermute | solution.py:344
  249.9 12.1 %collective-permute-start.35 = (bf16[128,1536]{1,0:T(8,128)(2,1)S(1)}, bf16[128,1536]{1,0:T(8,128)(2,1)S(1)}, u32[]{:S(2)}, u32[]{:S(2)}) collective-permute-start(bf16[128,1536]{1,0:T(8,128)(2,1)S(1)} %pad_maximum_fusion.15), channel_id=1, source_target_pairs={{0,8},{2,6},{4,12},{6,2},{8,0},{10,14},{12,4},{14,10},{16,24},{18,... | collective-permute-start | bytes 1179656 | tf_op jit(solution)/shard_map/ppermute | solution.py:344
  250.3 20.0 %collective-permute-start.53 = (bf16[256,2048]{1,0:T(8,128)(2,1)S(1)}, bf16[256,2048]{1,0:T(8,128)(2,1)S(1)}, u32[]{:S(2)}, u32[]{:S(2)}) collective-permute-start(bf16[256,2048]{1,0:T(8,128)(2,1)S(1)} %pad_maximum_fusion.9), channel_id=1, source_target_pairs={{0,4},{2,10},{4,0},{6,14},{8,12},{10,2},{12,8},{14,6},{16,20},{18,... | collective-permute-start | bytes 3145736 | tf_op jit(solution)/shard_map/ppermute | solution.py:344
  262.1 16.6 %collective-permute-start.36 = (bf16[256,1536]{1,0:T(8,128)(2,1)S(1)}, bf16[256,1536]{1,0:T(8,128)(2,1)S(1)}, u32[]{:S(2)}, u32[]{:S(2)}) collective-permute-start(bf16[256,1536]{1,0:T(8,128)(2,1)S(1)} %pad_maximum_fusion.11), channel_id=1, source_target_pairs={{0,4},{2,10},{4,0},{6,14},{8,12},{10,2},{12,8},{14,6},{16,20},{18,... | collective-permute-start | bytes 2359304 | tf_op jit(solution)/shard_map/ppermute | solution.py:344
  265.4 24.7 %collective-permute-start.61 = (bf16[1024,1024]{1,0:T(8,128)(2,1)S(1)}, bf16[1024,1024]{1,0:T(8,128)(2,1)S(1)}, u32[]{:S(2)}, u32[]{:S(2)}) collective-permute-start(bf16[1024,1024]{1,0:T(8,128)(2,1)S(1)} %pad_maximum_fusion.2.mine_ref), channel_id=1, source_target_pairs={{0,2},{2,0},{4,6},{6,4},{8,10},{10,8},{12,14},{14,12},{16,18},{18,... | collective-permute-start | bytes 6291464 | tf_op jit(solution)/shard_map/ppermute | solution.py:341
  271.1 23.6 %collective-permute-start.54 = (bf16[512,2048]{1,0:T(8,128)(2,1)S(1)}, bf16[512,2048]{1,0:T(8,128)(2,1)S(1)}, u32[]{:S(2)}, u32[]{:S(2)}) collective-permute-start(bf16[512,2048]{1,0:T(8,128)(2,1)S(1)} %pad_maximum_fusion.1.mine_ref), channel_id=1, source_target_pairs={{0,2},{2,0},{4,6},{6,4},{8,10},{10,8},{12,14},{14,12},{16,18},{18,... | collective-permute-start | bytes 6291464 | tf_op jit(solution)/shard_map/ppermute | solution.py:341
  (68 other events, 425.6 us)
